TPU v7x, 32 devices: a whole 2x2x4 slice. The times are simulated.
32 devices in a mesh: rows: 16 (over z, x, core), inner: 2 (over y).
Axes of the slice: x: 2, y: 2, z: 4, core: 2. Of those that a mesh axis runs over, the one named last changes fastest.
Arguments:
- p_blocks: bfloat16 [48, 16, 128, 128], P('rows', 'inner'), may hold values from -0.5 to 0.5
- col_lists: int32 [48, 16], replicated, may hold values from 0 to 47, as said below
- fill_lists: int32 [48, 16], replicated, may hold values from 0 to 47, as said below
Outputs:
- purified: float32 [48, 16, 128, 128], P('rows', 'inner')
Inputs may be any that keep to these rules, and one draw needn't show every extreme that they name: Entry col_lists[i, s] names a block row whose owner (entry // 3) lies within 2 owners of row i's owner (i // 3), counting around the end. Over the 3 block rows of one owner, the slots of one inner group name block rows of any one owner at most 5 times, and some owner exactly 5 times. Entries may repeat within a row. `fill_lists`: the 16 entries of a row are distinct and name block rows whose owners lie within 4 owners of the row's owner, counting around the end.
All inputs are finite; a program needn't handle non-finite values.
Results may differ from a plain program's by a relative error of at most 0.02.
Values may be sent and summed in bfloat16 or wider, within the bound.
No kernel may reach another device: no remote copies, remote signals or barrier semaphores. Data moves between devices by JAX's collectives and lax.ppermute only.
A program may use at most 128 MiB of HBM per device.

v0:
```python
import jax
import jax.numpy as jnp
from jax import lax
from jax.sharding import PartitionSpec as P

REACH = 2


def passed_along(block, axis, distance):
    devices = range(lax.axis_size(axis))
    route = [((i - distance) % len(devices), i) for i in devices]
    return lax.ppermute(block, axis, route)


def per_device(p_blocks, col_lists, fill_lists):
    row_count = p_blocks.shape[0]
    slot_count = p_blocks.shape[1]
    owner_count = lax.axis_size("rows")
    my_row = lax.axis_index("rows")
    my_group = lax.axis_index("inner")
    owner_span = 2 * REACH + 1
    request_count = row_count * slot_count
    capacity = (request_count + 2 * REACH) // owner_span
    slot_ids = jnp.arange(capacity, dtype=jnp.int32)
    request_ids = jnp.arange(request_count, dtype=jnp.int32)
    my_fill = lax.dynamic_slice_in_dim(fill_lists, my_row * row_count, row_count, 0)
    fill_count = my_fill.shape[1]

    def requests(device_row):
        targets = lax.dynamic_slice(
            col_lists, (device_row * row_count, my_group * slot_count), (row_count, slot_count)
        ).reshape(-1)
        distance = (targets // row_count - device_row + REACH) % owner_count
        within = targets % row_count
        matched = distance[:, None] == distance[None, :]
        earlier = request_ids[None, :] < request_ids[:, None]
        position = jnp.sum((matched & earlier).astype(jnp.int32), axis=1)
        return (targets, distance, within, position)

    def select_slots(values, distance, position, offset):
        matches = (distance[None, :] == offset + REACH) & (position[None, :] == slot_ids[:, None])
        return (jnp.sum(jnp.where(matches, values[None, :], 0), axis=1), jnp.any(matches, axis=1))

    targets, distance, within, position = requests(my_row)

    def multiply(sources, source_index, present, entries, list_table):
        entry_rows = entries // slot_count
        left_blocks = p_blocks[entry_rows, entries % slot_count]
        right_blocks = sources[source_index]
        remote = list_table[targets[entries]]
        fill_rows = my_fill[entry_rows]
        matches = remote[:, :, None] == fill_rows[:, None, :]
        landed = jnp.any(matches, axis=2) & present[:, None]
        column = jnp.where(landed, jnp.argmax(matches.astype(jnp.int32), axis=2), fill_count)
        products = jnp.einsum(
            "cxy,cuyz->cuxz", left_blocks, right_blocks, preferred_element_type=jnp.float32
        )
        row_index = jnp.broadcast_to(entry_rows[:, None], column.shape)
        return (row_index, column, products)

    def product_rows(complete, list_table):
        row_pieces = []
        column_pieces = []
        value_pieces = []
        for offset in range(-REACH, REACH + 1):
            entries, present = select_slots(request_ids, distance, position, offset)
            if offset == 0:
                sources = complete
                source_index = within[entries]
            else:
                partner = (my_row - offset) % owner_count
                other_targets, other_distance, other_within, other_position = requests(partner)
                chosen, unused = select_slots(other_within, other_distance, other_position, offset)
                outgoing = complete[chosen]
                sources = passed_along(outgoing, "rows", -offset)
                source_index = slot_ids
            row_index, column, products = multiply(
                sources, source_index, present, entries, list_table
            )
            row_pieces.append(row_index)
            column_pieces.append(column)
            value_pieces.append(products)
        all_rows = jnp.concatenate(row_pieces, axis=0)
        all_columns = jnp.concatenate(column_pieces, axis=0)
        all_values = jnp.concatenate(value_pieces, axis=0)
        partial_value = jnp.zeros(
            (row_count, fill_count, p_blocks.shape[2], p_blocks.shape[3]), jnp.float32
        )
        return partial_value.at[all_rows, all_columns].add(all_values, mode="drop")

    complete_p = lax.all_gather(p_blocks, "inner", axis=1, tiled=True)
    square_terms = product_rows(complete_p, col_lists)
    square_share = lax.psum_scatter(
        square_terms.astype(jnp.bfloat16), "inner", scatter_dimension=1, tiled=True
    ).astype(jnp.float32)
    square_low = lax.all_gather(square_share.astype(jnp.bfloat16), "inner", axis=1, tiled=True)
    cube_terms = product_rows(square_low, fill_lists)
    cubed = lax.psum_scatter(
        cube_terms.astype(jnp.bfloat16), "inner", scatter_dimension=1, tiled=True
    ).astype(jnp.float32)
    return 3.0 * square_share - 2.0 * cubed


def solution(mesh):
    in_specs = (P("rows", "inner", None, None), P(), P())
    out_specs = P("rows", "inner", None, None)
    return jax.shard_map(
        per_device, mesh=mesh, in_specs=in_specs, out_specs=out_specs, check_vma=False
    )
```

profile of v0, /device:TPU:0, one launch (start us, length us, event | category | flops | bytes accessed | tf_op | source)
XLA Modules:
  0.0 705.2 jit_solution(5771524124150951329)
XLA Ops:
  32.1 6.7 all-gather.3.cloned.1.call-done
  38.9 4.1 gather_fusion.15
  49.5 4.4 collective-permute-start.2
  70.2 116.0 %collective-permute-done = bf16[5,16,128,128]{3,2,1,0:T(8,128)(2,1)} collective-permute-done((bf16[5,16,128,128]{3,2,1,0:T(8,128)(2,1)}, bf16[5,16,128,128]{3,2,1,0:T(8,128)(2,1)}, u32[]{:S(2)}, u32[]{:S(2)}) %collective-permute-start) | collective-permute-done | bytes 2621472 | tf_op jit(solution)/shard_map/ppermute | solution.py:12
  189.1 4.2 gather_fusion.19
  193.3 4.2 gather_fusion.25
  200.9 3.4 bitcast_dynamic-update-slice_fusion.8
  204.3 3.4 bitcast_dynamic-update-slice_fusion.7
  210.9 6.0 collective-permute-done.3
  223.1 26.5 %copy.136 = f32[400,128,128]{2,1,0:T(8,128)} copy(f32[400,128,128]{1,2,0:T(8,128)} %bitcast.60) | data formatting | bytes 52428800 | tf_op jit(solution)/shard_map/concatenate | solution.py:85
  250.0 54.6 %scatter_fusion = f32[3,16,128,128]{3,2,1,0:T(8,128)S(1)} fusion(f32[3,16,128,128]{3,2,1,0:T(8,128)S(1)} %broadcast.2231.clone, s32[400]{0:T(512)S(1)} %reshape.2118, f32[400,128,128]{2,1,0:T(8,128)} %copy.136), kind=kCustom, calls=%fused_computation.44 | custom fusion | flops 6553600 | bytes 78646400 | tf_op jit(solution)/shard_map/scatter-add | solution.py:89
  307.3 45.3 %reduce-scatter.9.cloned.1.call-done = bf16[8,49152]{1,0:T(8,128)(2,1)} async-done(((bf16[16,49152]{1,0:T(8,128)(2,1)}), bf16[8,49152]{1,0:T(8,128)(2,1)}) %reduce-scatter.9.cloned.1.call-update) | async-done | bytes 786448
  355.1 27.1 %all-gather.5.cloned.1.call-done = bf16[3,16,128,128]{3,2,1,0:T(8,128)(2,1)} async-done(((bf16[3,8,128,128]{3,2,1,0:T(8,128)(2,1)}), bf16[3,16,128,128]{3,2,1,0:T(8,128)(2,1)}) %all-gather.5.cloned.1.call-update) | async-done | bytes 1572880 | tf_op jit(solution)/shard_map/all_gather | solution.py:96
  382.2 4.1 gather_fusion.35
  392.8 4.4 collective-permute-start.6
  402.9 126.7 %collective-permute-done.4 = bf16[5,16,128,128]{3,2,1,0:T(8,128)(2,1)} collective-permute-done((bf16[5,16,128,128]{3,2,1,0:T(8,128)(2,1)}, bf16[5,16,128,128]{3,2,1,0:T(8,128)(2,1)}, u32[]{:S(2)}, u32[]{:S(2)}) %collective-permute-start.4) | collective-permute-done | bytes 2621472 | tf_op jit(solution)/shard_map/ppermute | solution.py:12
  532.4 4.2 gather_fusion.38
  536.6 4.3 gather_fusion.41
  544.3 3.4 bitcast_dynamic-update-slice_fusion.3
  547.6 3.4 bitcast_dynamic-update-slice_fusion.2
  554.3 5.9 collective-permute-done.7
  566.4 26.5 %copy.147 = f32[400,128,128]{2,1,0:T(8,128)} copy(f32[400,128,128]{1,2,0:T(8,128)} %bitcast.76) | data formatting | bytes 52428800 | tf_op jit(solution)/shard_map/concatenate | solution.py:85
  593.3 54.6 %scatter_fusion.1 = f32[3,16,128,128]{3,2,1,0:T(8,128)S(1)} fusion(f32[3,16,128,128]{3,2,1,0:T(8,128)S(1)} %broadcast.2231, s32[400]{0:T(512)S(1)} %reshape.2124, f32[400,128,128]{2,1,0:T(8,128)} %copy.147), kind=kCustom, calls=%fused_computation.45 | custom fusion | flops 6553600 | bytes 78646400 | tf_op jit(solution)/shard_map/scatter-add | solution.py:89
  650.7 45.3 %reduce-scatter.11.cloned.1.call-done = bf16[8,49152]{1,0:T(8,128)(2,1)} async-done(((bf16[16,49152]{1,0:T(8,128)(2,1)}), bf16[8,49152]{1,0:T(8,128)(2,1)}) %reduce-scatter.11.cloned.1.call-update) | async-done | bytes 786448
  (225 shorter events, 102.4 us)
Async XLA Ops:
  6.5 32.3 %all-gather.3.cloned.1.call-start = ((), (), s32[]{:S(2)}) async-start(), calls=%async_computation.2 | async-start | bytes 2359296 | tf_op jit(solution)/shard_map/all_gather | solution.py:91
  7.3 345.3 %reduce-scatter.9.cloned.1.call-start = ((), (), s32[]{:S(2)}) async-start(), calls=%async_computation.4 | async-start | bytes 2359296
  38.9 5.6 copy-start
  43.0 143.3 %collective-permute-start = (bf16[5,16,128,128]{3,2,1,0:T(8,128)(2,1)}, bf16[5,16,128,128]{3,2,1,0:T(8,128)(2,1)}, u32[]{:S(2)}, u32[]{:S(2)}) collective-permute-start(bf16[5,16,128,128]{3,2,1,0:T(8,128)(2,1)} %gather_fusion.15), channel_id=1, source_target_pairs={{28,0},{30,2},{0,4},{2,6},{4,8},{6,10},{8,12},{10,14},{12,16},{14,... | collective-permute-start | bytes 7864328 | tf_op jit(solution)/shard_map/ppermute | solution.py:12
  46.9 142.1 %collective-permute-start.1 = (bf16[5,16,128,128]{3,2,1,0:T(8,128)(2,1)}, bf16[5,16,128,128]{3,2,1,0:T(8,128)(2,1)}, u32[]{:S(2)}, u32[]{:S(2)}) collective-permute-start(bf16[5,16,128,128]{3,2,1,0:T(8,128)(2,1)} %gather_fusion.18), channel_id=1, source_target_pairs={{30,0},{0,2},{2,4},{4,6},{6,8},{8,10},{10,12},{12,14},{14,16},{16,... | collective-permute-start | bytes 7864328 | tf_op jit(solution)/shard_map/ppermute | solution.py:12
  49.5 143.9 %collective-permute-start.2 = (bf16[5,16,128,128]{3,2,1,0:T(8,128)(2,1)}, bf16[5,16,128,128]{3,2,1,0:T(8,128)(2,1)}, u32[]{:S(2)}, u32[]{:S(2)}) collective-permute-start(bf16[5,16,128,128]{3,2,1,0:T(8,128)(2,1)} %gather_fusion.24), channel_id=1, source_target_pairs={{2,0},{4,2},{6,4},{8,6},{10,8},{12,10},{14,12},{16,14},{18,16},{20... | collective-permute-start | bytes 7864328 | tf_op jit(solution)/shard_map/ppermute | solution.py:12
  62.1 154.8 %collective-permute-start.3 = (bf16[5,16,128,128]{3,2,1,0:T(8,128)(2,1)}, bf16[5,16,128,128]{3,2,1,0:T(8,128)(2,1)}, u32[]{:S(2)}, u32[]{:S(2)}) collective-permute-start(bf16[5,16,128,128]{3,2,1,0:T(8,128)(2,1)} %gather_fusion.27), channel_id=1, source_target_pairs={{4,0},{6,2},{8,4},{10,6},{12,8},{14,10},{16,12},{18,14},{20,16},{2... | collective-permute-start | bytes 7864328 | tf_op jit(solution)/shard_map/ppermute | solution.py:12
  63.3 134.3 %copy-start.12 = (bf16[5,128,128]{2,1,0:T(8,128)(2,1)}, bf16[5,128,128]{2,1,0:T(8,128)(2,1)S(1)}, u32[]{:S(2)}) copy-start(bf16[5,128,128]{2,1,0:T(8,128)(2,1)S(1)} %gather_fusion.17) | copy-start | bytes 491524
  65.2 139.1 %copy-start.14 = (bf16[5,128,128]{2,1,0:T(8,128)(2,1)}, bf16[5,128,128]{2,1,0:T(8,128)(2,1)S(1)}, u32[]{:S(2)}) copy-start(bf16[5,128,128]{2,1,0:T(8,128)(2,1)S(1)} %gather_fusion.23) | copy-start | bytes 491524
  65.8 141.9 %copy-start.10 = (bf16[5,128,128]{2,1,0:T(8,128)(2,1)}, bf16[5,128,128]{2,1,0:T(8,128)(2,1)S(1)}, u32[]{:S(2)}) copy-start(bf16[5,128,128]{2,1,0:T(8,128)(2,1)S(1)} %gather_fusion.26) | copy-start | bytes 491524
  200.9 3.4 copy-start.3
  204.3 3.4 copy-start.7
  307.2 74.9 %all-gather.5.cloned.1.call-start = ((), (), s32[]{:S(2)}) async-start(), calls=%async_computation.3 | async-start | bytes 2359296 | tf_op jit(solution)/shard_map/all_gather | solution.py:96
  354.8 341.2 %reduce-scatter.11.cloned.1.call-start = ((), (), s32[]{:S(2)}) async-start(), calls=%async_computation.5 | async-start | bytes 2359296
  382.2 5.6 copy-start.1
  386.3 143.3 %collective-permute-start.4 = (bf16[5,16,128,128]{3,2,1,0:T(8,128)(2,1)}, bf16[5,16,128,128]{3,2,1,0:T(8,128)(2,1)}, u32[]{:S(2)}, u32[]{:S(2)}) collective-permute-start(bf16[5,16,128,128]{3,2,1,0:T(8,128)(2,1)} %gather_fusion.35), channel_id=1, source_target_pairs={{28,0},{30,2},{0,4},{2,6},{4,8},{6,10},{8,12},{10,14},{12,16},{14,... | collective-permute-start | bytes 7864328 | tf_op jit(solution)/shard_map/ppermute | solution.py:12
  390.2 142.1 %collective-permute-start.5 = (bf16[5,16,128,128]{3,2,1,0:T(8,128)(2,1)}, bf16[5,16,128,128]{3,2,1,0:T(8,128)(2,1)}, u32[]{:S(2)}, u32[]{:S(2)}) collective-permute-start(bf16[5,16,128,128]{3,2,1,0:T(8,128)(2,1)} %gather_fusion.37), channel_id=1, source_target_pairs={{30,0},{0,2},{2,4},{4,6},{6,8},{8,10},{10,12},{12,14},{14,16},{16,... | collective-permute-start | bytes 7864328 | tf_op jit(solution)/shard_map/ppermute | solution.py:12
  392.8 143.9 %collective-permute-start.6 = (bf16[5,16,128,128]{3,2,1,0:T(8,128)(2,1)}, bf16[5,16,128,128]{3,2,1,0:T(8,128)(2,1)}, u32[]{:S(2)}, u32[]{:S(2)}) collective-permute-start(bf16[5,16,128,128]{3,2,1,0:T(8,128)(2,1)} %gather_fusion.40), channel_id=1, source_target_pairs={{2,0},{4,2},{6,4},{8,6},{10,8},{12,10},{14,12},{16,14},{18,16},{20... | collective-permute-start | bytes 7864328 | tf_op jit(solution)/shard_map/ppermute | solution.py:12
  399.7 160.5 %collective-permute-start.7 = (bf16[5,16,128,128]{3,2,1,0:T(8,128)(2,1)}, bf16[5,16,128,128]{3,2,1,0:T(8,128)(2,1)}, u32[]{:S(2)}, u32[]{:S(2)}) collective-permute-start(bf16[5,16,128,128]{3,2,1,0:T(8,128)(2,1)} %gather_fusion.42), channel_id=1, source_target_pairs={{4,0},{6,2},{8,4},{10,6},{12,8},{14,10},{16,12},{18,14},{20,16},{2... | collective-permute-start | bytes 7864328 | tf_op jit(solution)/shard_map/ppermute | solution.py:12
  536.6 4.3 copy-start.13
  544.3 3.4 copy-start.2
  544.3 3.4 copy-start.15
  547.6 3.4 copy-start.4
  547.6 3.4 copy-start.11
  (4 other events, 12.0 us)
Sparse Core Ops, SparseCore 0:
  8.9 29.9 all-gather.2
  307.3 45.1 reduce-scatter.8
  354.9 27.1 all-gather.4
  650.7 45.3 reduce-scatter.10
where the time goes:
time: 708 us; the launch traced here: 705 us
  waiting for transfers between devices  380 us (54%)
  local copies, waits for them, and re-layouts  139 us (20%)
  other arithmetic  126 us (18%)
  matrix products  33.4 us (5%)
  between operations  13.7 us (2%)
  starting transfers between devices  13.3 us (2%)
    ppermute x8, waiting for transfers between devices, passed_along(): return lax.ppermute(block, axis, route)  255 us
    scatter-add x2, other arithmetic, product_rows(): return partial_value.at[all_rows, all_columns].add(all_values, mode='drop')  109 us
    unnamed x6, waiting for transfers between devices  91.4 us
    concatenate x2, local copies, waits for them, and re-layouts, product_rows(): all_values = jnp.concatenate(value_pieces, axis=0)  53.1 us
    dot_general x10, matrix products, multiply(): jnp.einsum('cxy,cuyz->cuxz', left_blocks, right_blocks, preferred_element...  33.4 us
    gather x10, local copies, waits for them, and re-layouts, multiply(): right_blocks = sources[source_index]  33.2 us
    all_gather x1, waiting for transfers between devices, per_device(): lax.all_gather(square_share.astype(jnp.bfloat16), 'inner', axis=1, tiled=...  27.1 us
    gather x8, local copies, waits for them, and re-layouts, product_rows(): outgoing = complete[chosen]  23.3 us
  transfers between devices with their start and end apart: 12, of which 8 were waited for; matrix products, arithmetic and copies ran while one was open for 15% of the time, Pallas kernels for 0%

commit v1 on v0

v1 whole, which is shorter than its diff:
```python
import functools

import jax
import jax.numpy as jnp
from jax import lax
from jax.experimental import pallas as pl
from jax.experimental.pallas import tpu as pltpu
from jax.sharding import PartitionSpec as P

REACH = 2
BAND = 2 * REACH + 1
WIDE = 4 * REACH + 1
VMEM = pl.BlockSpec(memory_space=pltpu.VMEM)
SMEM = pl.BlockSpec(memory_space=pltpu.SMEM)
PARAMS = pltpu.CompilerParams(vmem_limit_bytes=56 * 1024 * 1024)


def call(kernel, ins, outs, scratch=()):
    specs = [SMEM if x.dtype == jnp.int32 else VMEM for x in ins]
    many = isinstance(outs, (list, tuple))
    return pl.pallas_call(
        kernel,
        out_shape=tuple(outs) if many else outs,
        in_specs=specs,
        out_specs=tuple(VMEM for _ in outs) if many else VMEM,
        scratch_shapes=list(scratch),
        compiler_params=PARAMS,
    )(*ins)


def offsets(j):
    first = j < 2
    return {
        "own": 0,
        "x": jnp.where(first, 2, -2),
        "core": jnp.where(j % 2 == 0, 1, -1),
        "core_x": jnp.where(first, 1, -1),
        "z": jnp.where(first, -2, 2),
        "core_z": jnp.where(first, -1, 1),
    }


def per_device(p_blocks, col_lists, fill_lists):
    rb, slots, bs, _ = p_blocks.shape
    nb, k_row = col_lists.shape
    fill = fill_lists.shape[1]
    n_rows = lax.axis_size("rows")
    n = lax.axis_size("inner")
    part = bs // n
    width = rb * bs
    bf16, f32 = jnp.bfloat16, jnp.float32
    shape = jax.ShapeDtypeStruct
    half = fill // 2

    def shift(m):
        return [(i, (i + m) % n) for i in range(n)]

    def along(r):
        group, j = divmod(r, 4)
        return (group + (1 if j < 2 else -1)) % (n_rows // 4) * 4 + j

    flip_x = [(r, r ^ 2) for r in range(n_rows)]
    flip_core = [(r, r ^ 1) for r in range(n_rows)]
    move_z = [(r, along(r)) for r in range(n_rows)]
    core_x = [(r, r ^ 1) for r in range(n_rows) if r % 4 in (0, 3)]
    core_z = [(r, r ^ 1) for r in range(n_rows) if r % 4 in (1, 2)]

    def send(x, axis, pairs):
        return lax.ppermute(x, axis, pairs)

    def slice_at(index):
        return pl.ds(pl.multiple_of(index * part, part), part)

    def wrapped(x):
        return jnp.where(x < 0, x + nb, jnp.where(x >= nb, x - nb, x))

    def pack(p_ref, own_ref, rest_ref, turned):
        q = lax.axis_index("inner")
        for i in range(rb):
            for s in range(slots):
                turned[i, s] = p_ref[i, s].T
                own_ref[i, s] = turned[i, s, slice_at(q), :]
                for m in range(1, n):
                    rest_ref[m - 1, i, s] = turned[i, s, slice_at(lax.rem(q + m, n)), :]

    own, rest = call(
        pack,
        [p_blocks],
        [shape((rb, slots, part, bs), bf16), shape((n - 1, rb, slots, part, bs), bf16)],
        [pltpu.VMEM((rb, slots, bs, bs), bf16)],
    )

    def received(parts):
        return parts[0][None] if n == 2 else jnp.stack(parts)

    def nth(x, m):
        return x.reshape(x.shape[1:]) if n == 2 else x[m]

    got = received([send(nth(rest, m - 1), "inner", shift(m)) for m in range(1, n)])
    x_own = send(own, "rows", flip_x)
    x_got = send(got, "rows", flip_x)
    z_own = send(x_own, "rows", move_z)
    z_got = send(x_got, "rows", move_z)
    if n == 2:
        left = send(own, "inner", shift(1))
    else:
        left = lax.all_gather(p_blocks, "inner", axis=0)
    c_own, c_got = send(own, "rows", flip_core), send(got, "rows", flip_core)
    cx_own, cx_got = send(x_own, "rows", core_x), send(x_got, "rows", core_x)
    cz_own, cz_got = send(z_own, "rows", core_z), send(z_got, "rows", core_z)

    def band(col_ref, own_ref, rest_ref, got_ref, left_ref, out_ref):
        o = lax.axis_index("rows")
        q = lax.axis_index("inner")
        out_ref[...] = jnp.zeros(out_ref.shape, bf16)

        def place(row, i, slot, block):
            c = wrapped(col_ref[row, slot] - rb * (o - REACH))
            return pl.multiple_of(c * bs, bs), pl.ds(i * bs, bs), block

        def add(base, lanes, at, value):
            where = pl.ds(pl.multiple_of(base + at * part, part), part)
            out_ref[where, lanes] = (out_ref[where, lanes].astype(f32) + value.astype(f32)).astype(bf16)

        for i in range(rb):
            row = o * rb + i
            for s in range(slots):
                c = wrapped(col_ref[row, q * slots + s] - rb * (o - REACH)) * bs
                lanes = pl.ds(i * bs, bs)
                add(c, lanes, q, own_ref[i, s])
                for m in range(1, n):
                    add(c, lanes, lax.rem(q + m, n), rest_ref[m - 1, i, s])
                for m in range(1, n):
                    g = lax.rem(q - m + n, n)
                    c = wrapped(col_ref[row, g * slots + s] - rb * (o - REACH)) * bs
                    if n == 2:
                        add(c, lanes, q, got_ref[0, i, s])
                        add(c, lanes, g, left_ref[i, s])
                    else:
                        where = pl.ds(pl.multiple_of(c, bs), bs)
                        block = left_ref[g, i, s].T.astype(f32)
                        out_ref[where, lanes] = (out_ref[where, lanes].astype(f32) + block).astype(bf16)

    left_band = call(
        band, [col_lists, own, rest, got, left], shape((BAND * width, width), bf16)
    )

    span = BAND * rb * part
    wide = WIDE * rb * part
    owner_rows = rb * part

    def square_term(col_ref, d, own_ref, got_ref, left_ref, dense, acc_ref, first=False):
        o = lax.axis_index("rows")
        q = lax.axis_index("inner")
        source = lax.rem(o + d + n_rows, n_rows)
        dense[...] = jnp.zeros(dense.shape, bf16)

        def add(k, slot, value):
            c = wrapped(col_ref[source * rb + k, slot] - rb * (source - REACH))
            where, lanes = slice_at(c), pl.ds(k * bs, bs)
            dense[where, lanes] = (dense[where, lanes].astype(f32) + value.astype(f32)).astype(bf16)

        for s in range(slots):
            for k in range(rb):
                add(k, q * slots + s, own_ref[k, s])
                for m in range(1, n):
                    g = lax.rem(q - m + n, n)
                    add(k, g * slots + s, got_ref[m - 1, k, s])
        weights = left_ref[pl.ds(pl.multiple_of((d + REACH) * width, width), width), :]
        term = jnp.dot(dense[...], weights, preferred_element_type=f32)
        where = pl.ds(pl.multiple_of((d + REACH) * owner_rows, owner_rows), span)
        if first:
            acc_ref[...] = jnp.zeros(acc_ref.shape, f32)
            acc_ref[where, :] = term
        else:
            acc_ref[where, :] += term

    def square_near(col, w, wg, c, cg, x, xg, cx, cxg, left_ref, acc_ref, dense):
        j = lax.rem(lax.axis_index("rows"), 4)
        d = offsets(j)
        square_term(col, 0, w, wg, left_ref, dense, acc_ref, first=True)
        square_term(col, d["core"], c, cg, left_ref, dense, acc_ref)
        square_term(col, d["x"], x, xg, left_ref, dense, acc_ref)

        @pl.when((j == 1) | (j == 2))
        def _():
            square_term(col, d["core_x"], cx, cxg, left_ref, dense, acc_ref)

    acc = call(
        square_near,
        [col_lists, own, got, c_own, c_got, x_own, x_got, cx_own, cx_got, left_band],
        shape((wide, width), f32),
        [pltpu.VMEM((span, width), bf16)],
    )

    def kept(fill_ref, i, v):
        o = lax.axis_index("rows")
        return slice_at(wrapped(fill_ref[o * rb + i, v] - rb * (o - 2 * REACH)))

    def square_far(col, fill_ref, acc_in, z, zg, cz, czg, left_ref, sq_ref, low0, low1, acc_ref, dense):
        j = lax.rem(lax.axis_index("rows"), 4)
        d = offsets(j)
        acc_ref[...] = acc_in[...]
        square_term(col, d["z"], z, zg, left_ref, dense, acc_ref)

        @pl.when((j == 0) | (j == 3))
        def _():
            square_term(col, d["core_z"], cz, czg, left_ref, dense, acc_ref)

        for i in range(rb):
            for v in range(fill):
                value = acc_ref[kept(fill_ref, i, v), pl.ds(i * bs, bs)]
                sq_ref[i, v] = value
                (low0 if v < half else low1)[i, v % half] = value.astype(bf16)

    low_shape = shape((rb, half, part, bs), bf16)
    square, low0, low1 = call(
        square_far,
        [col_lists, fill_lists, acc, z_own, z_got, cz_own, cz_got, left_band],
        [shape((rb, fill, part, bs), f32), low_shape, low_shape],
        [pltpu.VMEM((wide, width), f32), pltpu.VMEM((span, width), bf16)],
    )

    x0, x1 = send(low0, "rows", flip_x), send(low1, "rows", flip_x)
    z0, z1 = send(x0, "rows", move_z), send(x1, "rows", move_z)
    c0, c1 = send(low0, "rows", flip_core), send(low1, "rows", flip_core)
    cx0, cx1 = send(x0, "rows", core_x), send(x1, "rows", core_x)
    cz0, cz1 = send(z0, "rows", core_z), send(z1, "rows", core_z)

    def cube_term(fill_ref, d, reach, ref0, ref1, left_ref, dense, acc_ref, first=False):
        o = lax.axis_index("rows")
        source = lax.rem(o + d + n_rows, n_rows)
        blocks = (WIDE - reach) * rb
        start = jnp.maximum(d, 0) * rb
        rows = blocks * part
        dense[:rows, :] = jnp.zeros((rows, width), bf16)
        for v in range(fill):
            for k in range(rb):
                c = wrapped(fill_ref[source * rb + k, v] - rb * (o - 2 * REACH)) - start

                @pl.when((c >= 0) & (c < blocks))
                def _():
                    dense[slice_at(c), pl.ds(k * bs, bs)] = (ref0 if v < half else ref1)[k, v % half]

        weights = left_ref[pl.ds(pl.multiple_of((d + REACH) * width, width), width), :]
        term = jnp.dot(dense[:rows, :], weights, preferred_element_type=f32)
        if first:
            acc_ref[...] = term
        else:
            acc_ref[pl.ds(pl.multiple_of(start * part, rb * part), rows), :] += term

    def cube_near(fill_ref, w0, w1, c0, c1, x0, x1, cx0, cx1, left_ref, acc_ref, dense):
        j = lax.rem(lax.axis_index("rows"), 4)
        d = offsets(j)
        cube_term(fill_ref, 0, 0, w0, w1, left_ref, dense, acc_ref, first=True)
        cube_term(fill_ref, d["core"], 1, c0, c1, left_ref, dense, acc_ref)
        cube_term(fill_ref, d["x"], 2, x0, x1, left_ref, dense, acc_ref)

        @pl.when((j == 1) | (j == 2))
        def _():
            cube_term(fill_ref, d["core_x"], 1, cx0, cx1, left_ref, dense, acc_ref)

    acc = call(
        cube_near,
        [fill_lists, low0, low1, c0, c1, x0, x1, cx0, cx1, left_band],
        shape((wide, width), f32),
        [pltpu.VMEM((wide, width), bf16)],
    )

    def cube_far(fill_ref, acc_in, z0, z1, cz0, cz1, left_ref, sq_ref, keep_ref, give_ref, acc_ref, dense):
        q = lax.axis_index("inner")
        j = lax.rem(lax.axis_index("rows"), 4)
        d = offsets(j)
        acc_ref[...] = acc_in[...]
        cube_term(fill_ref, d["z"], 2, z0, z1, left_ref, dense, acc_ref)

        @pl.when((j == 0) | (j == 3))
        def _():
            cube_term(fill_ref, d["core_z"], 1, cz0, cz1, left_ref, dense, acc_ref)

        def result(i, v):
            return 3.0 * sq_ref[i, v] - 2.0 * acc_ref[kept(fill_ref, i, v), pl.ds(i * bs, bs)]

        for i in range(rb):
            for s in range(slots):
                keep_ref[i, s] = result(i, q * slots + s)
                for m in range(1, n):
                    give_ref[m - 1, i, s] = result(i, lax.rem(q + m, n) * slots + s).astype(bf16)

    keep, give = call(
        cube_far,
        [fill_lists, acc, z0, z1, cz0, cz1, left_band, square],
        [shape((rb, slots, part, bs), f32), shape((n - 1, rb, slots, part, bs), bf16)],
        [pltpu.VMEM((wide, width), f32), pltpu.VMEM((wide, width), bf16)],
    )
    taken = received([send(nth(give, m - 1), "inner", shift(m)) for m in range(1, n)])

    def join(keep_ref, taken_ref, out_ref, turned):
        q = lax.axis_index("inner")
        for i in range(rb):
            for s in range(slots):
                turned[i, s, slice_at(q), :] = keep_ref[i, s]
                for m in range(1, n):
                    turned[i, s, slice_at(lax.rem(q - m + n, n)), :] = taken_ref[m - 1, i, s].astype(f32)
                out_ref[i, s] = turned[i, s].T

    return call(
        join,
        [keep, taken],
        shape((rb, slots, bs, bs), f32),
        [pltpu.VMEM((rb, slots, bs, bs), f32)],
    )


def solution(mesh):
    in_specs = (P("rows", "inner", None, None), P(), P())
    out_specs = P("rows", "inner", None, None)
    return jax.shard_map(
        per_device, mesh=mesh, in_specs=in_specs, out_specs=out_specs, check_vma=False
    )
```

time: 708 us -> 132 us (0.19)
  waiting for transfers between devices: 380 us -> 57 us
  local copies, waits for them, and re-layouts: 139 us -> 6.92 us
  other arithmetic: 126 us -> 0 us
  Pallas kernels: 0 us -> 38.6 us
  matrix products: 33.4 us -> 0 us
  starting transfers between devices: 13.3 us -> 28.4 us
  between operations: 13.7 us -> 0.29 us
    ppermute x8 -> x23, waiting for transfers between devices: 255 us -> 57 us  [send(): return lax.ppermute(x, axis, pairs)]
    scatter-add x2 -> x0, other arithmetic: 109 us -> none  [product_rows(): return partial_value.at[all_rows, all_columns].add(all_values, mode='drop')]
    unnamed x6 -> x0, waiting for transfers between devices: 91.4 us -> none
    gather x44 -> x0, local copies, waits for them, and re-layouts: 71.7 us -> none  [the longest x10 33.2 us: multiply(): right_blocks = sources[source_index]]
    concatenate x7 -> x0, local copies, waits for them, and re-layouts: 54 us -> none  [the longest x2 53.1 us: product_rows(): all_values = jnp.concatenate(value_pieces, axis=0)]
    pallas_call x0 -> x7, Pallas kernels: none -> 38.6 us  [call(): pl.pallas_call(kernel, out_shape=tuple(outs) if many else outs, in_specs=...]
    all_gather x2 -> x0, waiting for transfers between devices: 33.8 us -> none  [the longest x1 27.1 us: per_device(): lax.all_gather(square_share.astype(jnp.bfloat16), 'inner', axis=1, tiled=...]
    dot_general x10 -> x0, matrix products: 33.4 us -> none  [multiply(): jnp.einsum('cxy,cuyz->cuxz', left_blocks, right_blocks, preferred_element...]
  transfers between devices with their start and end apart: 12 -> 23, of which waited for: 8 -> 9; matrix products, arithmetic and copies ran while one was open for 15% -> 2% of each run, Pallas kernels for 0% -> 14%
where the time goes in v1:
time: 132 us; the launch traced here: 131 us
  waiting for transfers between devices  57 us (43%)
  Pallas kernels  38.6 us (29%)
  starting transfers between devices  28.4 us (22%)
  local copies, waits for them, and re-layouts  6.92 us (5%)
    ppermute x23, waiting for transfers between devices, send(): return lax.ppermute(x, axis, pairs)  57 us
    pallas_call x7, Pallas kernels, call(): pl.pallas_call(kernel, out_shape=tuple(outs) if many else outs, in_specs=...  38.6 us
    ppermute x23, starting transfers between devices, send(): return lax.ppermute(x, axis, pairs)  28.4 us
    unnamed x42, local copies, waits for them, and re-layouts  6.92 us
  transfers between devices with their start and end apart: 23, of which 9 were waited for; matrix products, arithmetic and copies ran while one was open for 2% of the time, Pallas kernels for 14%

profile of v1, /device:TPU:0, one launch (start us, length us, event | category | flops | bytes accessed | tf_op | source)
XLA Modules:
  0.0 131.2 jit_solution(9715554224825563436)
XLA Ops:
  0.0 2.5 %shard_map.37 = (bf16[3,8,64,128]{3,2,1,0:T(8,128)(2,1)}, bf16[1,3,8,64,128]{4,3,2,1,0:T(8,128)(2,1)}) custom-call(bf16[3,8,128,128]{3,2,1,0:T(8,128)(2,1)} %p_ref.1), custom_call_target="tpu_custom_call" | custom-call | tf_op jit(solution)/shard_map/pallas_call | solution.py:21
  2.5 3.0 %collective-permute-start = (bf16[3,8,64,128]{3,2,1,0:T(8,128)(2,1)}, bf16[3,8,64,128]{3,2,1,0:T(8,128)(2,1)S(1)}, u32[]{:S(2)}, u32[]{:S(2)}) collective-permute-start(bf16[3,8,64,128]{3,2,1,0:T(8,128)(2,1)} %bitcast.8), channel_id=1, source_target_pairs={{0,1},{1,0},{2,3},{3,2},{4,5},{5,4},{6,7},{7,6},{8,9},{9,8},{10,11... | collective-permute-start | bytes 1179656 | tf_op jit(solution)/shard_map/ppermute | solution.py:69
  5.4 1.5 %collective-permute-start.3 = (bf16[3,8,64,128]{3,2,1,0:T(8,128)(2,1)}, bf16[3,8,64,128]{3,2,1,0:T(8,128)(2,1)S(1)}, u32[]{:S(2)}, u32[]{:S(2)}) collective-permute-start(bf16[3,8,64,128]{3,2,1,0:T(8,128)(2,1)} %get-tuple-element.12.own_ref.w), channel_id=1, source_target_pairs={{0,4},{2,6},{4,0},{6,2},{8,12},{10,14},{12,8},{14,10},{16,20},{18,... | collective-permute-start | bytes 1179656 | tf_op jit(solution)/shard_map/ppermute | solution.py:69
  6.9 7.8 %collective-permute-done = bf16[3,8,64,128]{3,2,1,0:T(8,128)(2,1)S(1)} collective-permute-done((bf16[3,8,64,128]{3,2,1,0:T(8,128)(2,1)}, bf16[3,8,64,128]{3,2,1,0:T(8,128)(2,1)S(1)}, u32[]{:S(2)}, u32[]{:S(2)}) %collective-permute-start) | collective-permute-done | bytes 393248 | tf_op jit(solution)/shard_map/ppermute | solution.py:69
  14.8 1.7 %collective-permute-start.4 = (bf16[1,3,8,64,128]{4,3,2,1,0:T(8,128)(2,1)S(1)}, bf16[1,3,8,64,128]{4,3,2,1,0:T(8,128)(2,1)S(1)}, u32[]{:S(2)}, u32[]{:S(2)}) collective-permute-start(bf16[1,3,8,64,128]{4,3,2,1,0:T(8,128)(2,1)S(1)} %bitcast.4), channel_id=1, source_target_pairs={{0,4},{2,6},{4,0},{6,2},{8,12},{10,14},{12,8},{14,10},{16,20},{18,... | collective-permute-start | bytes 1179656 | tf_op jit(solution)/shard_map/ppermute | solution.py:69
  16.5 1.5 %collective-permute-start.7 = (bf16[3,8,64,128]{3,2,1,0:T(8,128)(2,1)}, bf16[3,8,64,128]{3,2,1,0:T(8,128)(2,1)S(1)}, u32[]{:S(2)}, u32[]{:S(2)}) collective-permute-start(bf16[3,8,64,128]{3,2,1,0:T(8,128)(2,1)} %get-tuple-element.12.own_ref.w), channel_id=1, source_target_pairs={{0,1},{1,0},{2,3},{3,2},{4,5},{5,4},{6,7},{7,6},{8,9},{9,8},{10,11... | collective-permute-start | bytes 1179656 | tf_op jit(solution)/shard_map/ppermute | solution.py:69
  18.0 1.6 %collective-permute-start.8 = (bf16[3,8,64,128]{3,2,1,0:T(8,128)(2,1)S(1)}, bf16[3,8,64,128]{3,2,1,0:T(8,128)(2,1)S(1)}, u32[]{:S(2)}, u32[]{:S(2)}) collective-permute-start(bf16[3,8,64,128]{3,2,1,0:T(8,128)(2,1)S(1)} %collective-permute-done.3.x), channel_id=1, source_target_pairs={{0,8},{2,10},{4,28},{6,30},{8,16},{10,18},{12,4},{14,6},{16,24},{1... | collective-permute-start | bytes 1179656 | tf_op jit(solution)/shard_map/ppermute | solution.py:69
  19.6 5.4 %collective-permute-done.4.xg = bf16[1,3,8,64,128]{4,3,2,1,0:T(8,128)(2,1)S(1)} collective-permute-done((bf16[1,3,8,64,128]{4,3,2,1,0:T(8,128)(2,1)S(1)}, bf16[1,3,8,64,128]{4,3,2,1,0:T(8,128)(2,1)S(1)}, u32[]{:S(2)}, u32[]{:S(2)}) %collective-permute-start.4) | collective-permute-done | bytes 393248 | tf_op jit(solution)/shard_map/ppermute | solution.py:69
  25.1 1.5 %collective-permute-start.9 = (bf16[1,3,8,64,128]{4,3,2,1,0:T(8,128)(2,1)S(1)}, bf16[1,3,8,64,128]{4,3,2,1,0:T(8,128)(2,1)S(1)}, u32[]{:S(2)}, u32[]{:S(2)}) collective-permute-start(bf16[1,3,8,64,128]{4,3,2,1,0:T(8,128)(2,1)S(1)} %collective-permute-done.4.xg), channel_id=1, source_target_pairs={{0,8},{2,10},{4,28},{6,30},{8,16},{10,18},{12,4},{14,6},{16,24},{1... | collective-permute-start | bytes 1179656 | tf_op jit(solution)/shard_map/ppermute | solution.py:69
  26.5 2.4 %collective-permute-start.5 = (bf16[3,8,64,128]{3,2,1,0:T(8,128)(2,1)S(1)}, bf16[3,8,64,128]{3,2,1,0:T(8,128)(2,1)S(1)}, u32[]{:S(2)}, u32[]{:S(2)}) collective-permute-start(bf16[3,8,64,128]{3,2,1,0:T(8,128)(2,1)S(1)} %collective-permute-done.3.x), channel_id=1, source_target_pairs={{0,2},{6,4},{8,10},{14,12},{16,18},{22,20},{24,26},{30,28},{1,3},{... | collective-permute-start | bytes 1179656 | tf_op jit(solution)/shard_map/ppermute | solution.py:69
  29.0 2.1 %collective-permute-start.6 = (bf16[1,3,8,64,128]{4,3,2,1,0:T(8,128)(2,1)S(1)}, bf16[1,3,8,64,128]{4,3,2,1,0:T(8,128)(2,1)}, u32[]{:S(2)}, u32[]{:S(2)}) collective-permute-start(bf16[1,3,8,64,128]{4,3,2,1,0:T(8,128)(2,1)S(1)} %collective-permute-done.4.xg), channel_id=1, source_target_pairs={{0,2},{6,4},{8,10},{14,12},{16,18},{22,20},{24,26},{30,28},{1,3},{... | collective-permute-start | bytes 1179656 | tf_op jit(solution)/shard_map/ppermute | solution.py:69
  33.1 6.8 %collective-permute-done.9.zg = bf16[1,3,8,64,128]{4,3,2,1,0:T(8,128)(2,1)S(1)} collective-permute-done((bf16[1,3,8,64,128]{4,3,2,1,0:T(8,128)(2,1)S(1)}, bf16[1,3,8,64,128]{4,3,2,1,0:T(8,128)(2,1)S(1)}, u32[]{:S(2)}, u32[]{:S(2)}) %collective-permute-start.9) | collective-permute-done | bytes 393248 | tf_op jit(solution)/shard_map/ppermute | solution.py:69
  42.5 1.4 %copy.9.fill_ref = s32[48,16]{1,0:T(8,128)} copy(s32[48,16]{0,1:T(8,128)} %param.5) | data formatting | bytes 6144 | tf_op args[2]
  43.9 3.4 %shard_map.38.left_ref = bf16[1920,384]{1,0:T(8,128)(2,1)} custom-call(s32[48,16]{1,0:T(8,128)} %copy.6.col_ref.col, bf16[3,8,64,128]{3,2,1,0:T(8,128)(2,1)} %get-tuple-element.12.own_ref.w, bf16[1,3,8,64,128]{4,3,2,1,0:T(8,128)(2,1)} %get-tuple-element.13.rest_ref, bf16[1,3,8,64,128]{4,3,2,1,0:T(8,128)(2,1)} %bitcast.6, bf16[3,8,64,128]{3,2,1,0:T(8,128)(2,1)} %copy-done.11), custom_call_target="tpu_custom_call" | custom-call | tf_op jit(solution)/shard_map/pallas_call | solution.py:21
  48.2 6.3 %shard_map.39.acc_in = f32[1728,384]{1,0:T(8,128)} custom-call(s32[48,16]{1,0:T(8,128)} %copy.6.col_ref.col, bf16[3,8,64,128]{3,2,1,0:T(8,128)(2,1)} %get-tuple-element.12.own_ref.w, bf16[1,3,8,64,128]{4,3,2,1,0:T(8,128)(2,1)} %bitcast.7, bf16[3,8,64,128]{3,2,1,0:T(8,128)(2,1)} %copy-done.6, bf16[1,3,8,64,128]{4,3,2,1,0:T(8,128)(2,1)} %copy-done.12, ...), custom_call_target="tpu_custom_call" | custom-call | tf_op jit(solution)/shard_map/pallas_call | solution.py:21
  54.5 6.6 %shard_map.40 = (f32[3,16,64,128]{3,2,1,0:T(8,128)}, bf16[3,8,64,128]{3,2,1,0:T(8,128)(2,1)}, bf16[3,8,64,128]{3,2,1,0:T(8,128)(2,1)}) custom-call(s32[48,16]{1,0:T(8,128)} %copy.6.col_ref.col, s32[48,16]{1,0:T(8,128)} %copy.9.fill_ref, f32[1728,384]{1,0:T(8,128)} %shard_map.39.acc_in, bf16[3,8,64,128]{3,2,1,0:T(8,128)(2,1)} %copy-done.3, ...), custom_call_target="tpu_custom_call" | custom-call | tf_op jit(solution)/shard_map/pallas_call | solution.py:21
  64.4 8.0 %collective-permute-done.14.x0 = bf16[3,8,64,128]{3,2,1,0:T(8,128)(2,1)S(1)} collective-permute-done((bf16[3,8,64,128]{3,2,1,0:T(8,128)(2,1)}, bf16[3,8,64,128]{3,2,1,0:T(8,128)(2,1)S(1)}, u32[]{:S(2)}, u32[]{:S(2)}) %collective-permute-start.14) | collective-permute-done | bytes 393248 | tf_op jit(solution)/shard_map/ppermute | solution.py:69
  72.4 8.4 %collective-permute-done.15.x1 = bf16[3,8,64,128]{3,2,1,0:T(8,128)(2,1)S(1)} collective-permute-done((bf16[3,8,64,128]{3,2,1,0:T(8,128)(2,1)}, bf16[3,8,64,128]{3,2,1,0:T(8,128)(2,1)S(1)}, u32[]{:S(2)}, u32[]{:S(2)}) %collective-permute-start.15) | collective-permute-done | bytes 393248 | tf_op jit(solution)/shard_map/ppermute | solution.py:69
  81.8 1.9 %collective-permute-start.16 = (bf16[3,8,64,128]{3,2,1,0:T(8,128)(2,1)S(1)}, bf16[3,8,64,128]{3,2,1,0:T(8,128)(2,1)S(1)}, u32[]{:S(2)}, u32[]{:S(2)}) collective-permute-start(bf16[3,8,64,128]{3,2,1,0:T(8,128)(2,1)S(1)} %collective-permute-done.14.x0), channel_id=1, source_target_pairs={{0,2},{6,4},{8,10},{14,12},{16,18},{22,20},{24,26},{30,28},{1,3},{... | collective-permute-start | bytes 1179656 | tf_op jit(solution)/shard_map/ppermute | solution.py:69
  86.7 8.0 %collective-permute-done.19.z1 = bf16[3,8,64,128]{3,2,1,0:T(8,128)(2,1)S(1)} collective-permute-done((bf16[3,8,64,128]{3,2,1,0:T(8,128)(2,1)S(1)}, bf16[3,8,64,128]{3,2,1,0:T(8,128)(2,1)S(1)}, u32[]{:S(2)}, u32[]{:S(2)}) %collective-permute-start.19) | collective-permute-done | bytes 393248 | tf_op jit(solution)/shard_map/ppermute | solution.py:69
  97.7 9.0 %shard_map.41.acc_in = f32[1728,384]{1,0:T(8,128)} custom-call(s32[48,16]{1,0:T(8,128)} %copy.9.fill_ref, bf16[3,8,64,128]{3,2,1,0:T(8,128)(2,1)} %get-tuple-element.14.w0, bf16[3,8,64,128]{3,2,1,0:T(8,128)(2,1)} %get-tuple-element.15.w1, bf16[3,8,64,128]{3,2,1,0:T(8,128)(2,1)} %copy-done.10, bf16[3,8,64,128]{3,2,1,0:T(8,128)(2,1)} %copy-done.14, ...), custom_call_target="tpu_custom_call" | custom-call | tf_op jit(solution)/shard_map/pallas_call | solution.py:21
  107.6 7.7 %shard_map.42 = (f32[3,8,64,128]{3,2,1,0:T(8,128)}, bf16[1,3,8,64,128]{4,3,2,1,0:T(8,128)(2,1)}) custom-call(s32[48,16]{1,0:T(8,128)} %copy.9.fill_ref, f32[1728,384]{1,0:T(8,128)} %shard_map.41.acc_in, bf16[3,8,64,128]{3,2,1,0:T(8,128)(2,1)} %copy-done.4, bf16[3,8,64,128]{3,2,1,0:T(8,128)(2,1)} %copy-done.8, bf16[3,8,64,128]{3,2,1,0:T(8,128)(2,1)} %copy-done.15, ...), custom_call_target="tpu_custom_call" | custom-call | tf_op jit(solution)/shard_map/pallas_call | solution.py:21
  115.7 11.6 %collective-permute-done.22 = bf16[3,8,64,128]{3,2,1,0:T(8,128)(2,1)S(1)} collective-permute-done((bf16[3,8,64,128]{3,2,1,0:T(8,128)(2,1)}, bf16[3,8,64,128]{3,2,1,0:T(8,128)(2,1)S(1)}, u32[]{:S(2)}, u32[]{:S(2)}) %collective-permute-start.22) | collective-permute-done | bytes 393248 | tf_op jit(solution)/shard_map/ppermute | solution.py:69
  128.1 3.2 %shard_map.43 = f32[3,8,128,128]{3,2,1,0:T(8,128)} custom-call(f32[3,8,64,128]{3,2,1,0:T(8,128)} %get-tuple-element.17.keep_ref, bf16[1,3,8,64,128]{4,3,2,1,0:T(8,128)(2,1)} %bitcast.9), custom_call_target="tpu_custom_call" | custom-call | tf_op jit(solution)/shard_map/pallas_call | solution.py:21
  (71 shorter events, 17.7 us)
Async XLA Ops:
  2.5 12.3 %collective-permute-start = (bf16[3,8,64,128]{3,2,1,0:T(8,128)(2,1)}, bf16[3,8,64,128]{3,2,1,0:T(8,128)(2,1)S(1)}, u32[]{:S(2)}, u32[]{:S(2)}) collective-permute-start(bf16[3,8,64,128]{3,2,1,0:T(8,128)(2,1)} %bitcast.8), channel_id=1, source_target_pairs={{0,1},{1,0},{2,3},{3,2},{4,5},{5,4},{6,7},{7,6},{8,9},{9,8},{10,11... | collective-permute-start | bytes 1179656 | tf_op jit(solution)/shard_map/ppermute | solution.py:69
  5.4 12.6 %collective-permute-start.3 = (bf16[3,8,64,128]{3,2,1,0:T(8,128)(2,1)}, bf16[3,8,64,128]{3,2,1,0:T(8,128)(2,1)S(1)}, u32[]{:S(2)}, u32[]{:S(2)}) collective-permute-start(bf16[3,8,64,128]{3,2,1,0:T(8,128)(2,1)} %get-tuple-element.12.own_ref.w), channel_id=1, source_target_pairs={{0,4},{2,6},{4,0},{6,2},{8,12},{10,14},{12,8},{14,10},{16,20},{18,... | collective-permute-start | bytes 1179656 | tf_op jit(solution)/shard_map/ppermute | solution.py:69
  14.8 10.3 %collective-permute-start.4 = (bf16[1,3,8,64,128]{4,3,2,1,0:T(8,128)(2,1)S(1)}, bf16[1,3,8,64,128]{4,3,2,1,0:T(8,128)(2,1)S(1)}, u32[]{:S(2)}, u32[]{:S(2)}) collective-permute-start(bf16[1,3,8,64,128]{4,3,2,1,0:T(8,128)(2,1)S(1)} %bitcast.4), channel_id=1, source_target_pairs={{0,4},{2,6},{4,0},{6,2},{8,12},{10,14},{12,8},{14,10},{16,20},{18,... | collective-permute-start | bytes 1179656 | tf_op jit(solution)/shard_map/ppermute | solution.py:69
  16.5 10.1 %collective-permute-start.7 = (bf16[3,8,64,128]{3,2,1,0:T(8,128)(2,1)}, bf16[3,8,64,128]{3,2,1,0:T(8,128)(2,1)S(1)}, u32[]{:S(2)}, u32[]{:S(2)}) collective-permute-start(bf16[3,8,64,128]{3,2,1,0:T(8,128)(2,1)} %get-tuple-element.12.own_ref.w), channel_id=1, source_target_pairs={{0,1},{1,0},{2,3},{3,2},{4,5},{5,4},{6,7},{7,6},{8,9},{9,8},{10,11... | collective-permute-start | bytes 1179656 | tf_op jit(solution)/shard_map/ppermute | solution.py:69
  18.0 11.0 %collective-permute-start.1 = (bf16[3,8,64,128]{3,2,1,0:T(8,128)(2,1)}, bf16[3,8,64,128]{3,2,1,0:T(8,128)(2,1)S(1)}, u32[]{:S(2)}, u32[]{:S(2)}) collective-permute-start(bf16[3,8,64,128]{3,2,1,0:T(8,128)(2,1)} %get-tuple-element.12.own_ref.w), channel_id=1, source_target_pairs={{0,2},{2,0},{4,6},{6,4},{8,10},{10,8},{12,14},{14,12},{16,18},{18,... | collective-permute-start | bytes 1179656 | tf_op jit(solution)/shard_map/ppermute | solution.py:69
  18.0 29.3 %copy-start.1 = (bf16[3,8,64,128]{3,2,1,0:T(8,128)(2,1)}, bf16[3,8,64,128]{3,2,1,0:T(8,128)(2,1)S(1)}, u32[]{:S(2)}) copy-start(bf16[3,8,64,128]{3,2,1,0:T(8,128)(2,1)S(1)} %collective-permute-done.3.x) | copy-start | bytes 1179652
  18.0 13.8 %collective-permute-start.8 = (bf16[3,8,64,128]{3,2,1,0:T(8,128)(2,1)S(1)}, bf16[3,8,64,128]{3,2,1,0:T(8,128)(2,1)S(1)}, u32[]{:S(2)}, u32[]{:S(2)}) collective-permute-start(bf16[3,8,64,128]{3,2,1,0:T(8,128)(2,1)S(1)} %collective-permute-done.3.x), channel_id=1, source_target_pairs={{0,8},{2,10},{4,28},{6,30},{8,16},{10,18},{12,4},{14,6},{16,24},{1... | collective-permute-start | bytes 1179656 | tf_op jit(solution)/shard_map/ppermute | solution.py:69
  25.1 14.8 %collective-permute-start.9 = (bf16[1,3,8,64,128]{4,3,2,1,0:T(8,128)(2,1)S(1)}, bf16[1,3,8,64,128]{4,3,2,1,0:T(8,128)(2,1)S(1)}, u32[]{:S(2)}, u32[]{:S(2)}) collective-permute-start(bf16[1,3,8,64,128]{4,3,2,1,0:T(8,128)(2,1)S(1)} %collective-permute-done.4.xg), channel_id=1, source_target_pairs={{0,8},{2,10},{4,28},{6,30},{8,16},{10,18},{12,4},{14,6},{16,24},{1... | collective-permute-start | bytes 1179656 | tf_op jit(solution)/shard_map/ppermute | solution.py:69
  26.5 20.8 %collective-permute-start.2 = (bf16[1,3,8,64,128]{4,3,2,1,0:T(8,128)(2,1)S(1)}, bf16[1,3,8,64,128]{4,3,2,1,0:T(8,128)(2,1)S(1)}, u32[]{:S(2)}, u32[]{:S(2)}) collective-permute-start(bf16[1,3,8,64,128]{4,3,2,1,0:T(8,128)(2,1)S(1)} %bitcast.5), channel_id=1, source_target_pairs={{0,2},{2,0},{4,6},{6,4},{8,10},{10,8},{12,14},{14,12},{16,18},{18,... | collective-permute-start | bytes 1179656 | tf_op jit(solution)/shard_map/ppermute | solution.py:69
  26.5 20.7 %collective-permute-start.5 = (bf16[3,8,64,128]{3,2,1,0:T(8,128)(2,1)S(1)}, bf16[3,8,64,128]{3,2,1,0:T(8,128)(2,1)S(1)}, u32[]{:S(2)}, u32[]{:S(2)}) collective-permute-start(bf16[3,8,64,128]{3,2,1,0:T(8,128)(2,1)S(1)} %collective-permute-done.3.x), channel_id=1, source_target_pairs={{0,2},{6,4},{8,10},{14,12},{16,18},{22,20},{24,26},{30,28},{1,3},{... | collective-permute-start | bytes 1179656 | tf_op jit(solution)/shard_map/ppermute | solution.py:69
  29.0 18.3 %collective-permute-start.6 = (bf16[1,3,8,64,128]{4,3,2,1,0:T(8,128)(2,1)S(1)}, bf16[1,3,8,64,128]{4,3,2,1,0:T(8,128)(2,1)}, u32[]{:S(2)}, u32[]{:S(2)}) collective-permute-start(bf16[1,3,8,64,128]{4,3,2,1,0:T(8,128)(2,1)S(1)} %collective-permute-done.4.xg), channel_id=1, source_target_pairs={{0,2},{6,4},{8,10},{14,12},{16,18},{22,20},{24,26},{30,28},{1,3},{... | collective-permute-start | bytes 1179656 | tf_op jit(solution)/shard_map/ppermute | solution.py:69
  31.8 22.7 %collective-permute-start.10 = (bf16[3,8,64,128]{3,2,1,0:T(8,128)(2,1)S(1)}, bf16[3,8,64,128]{3,2,1,0:T(8,128)(2,1)}, u32[]{:S(2)}, u32[]{:S(2)}) collective-permute-start(bf16[3,8,64,128]{3,2,1,0:T(8,128)(2,1)S(1)} %collective-permute-done.8.z), channel_id=1, source_target_pairs={{2,0},{4,6},{10,8},{12,14},{18,16},{20,22},{26,24},{28,30},{3,1},{... | collective-permute-start | bytes 1179656 | tf_op jit(solution)/shard_map/ppermute | solution.py:69
  39.8 14.7 %collective-permute-start.11 = (bf16[1,3,8,64,128]{4,3,2,1,0:T(8,128)(2,1)S(1)}, bf16[1,3,8,64,128]{4,3,2,1,0:T(8,128)(2,1)}, u32[]{:S(2)}, u32[]{:S(2)}) collective-permute-start(bf16[1,3,8,64,128]{4,3,2,1,0:T(8,128)(2,1)S(1)} %collective-permute-done.9.zg), channel_id=1, source_target_pairs={{2,0},{4,6},{10,8},{12,14},{18,16},{20,22},{26,24},{28,30},{3,1},{... | collective-permute-start | bytes 1179656 | tf_op jit(solution)/shard_map/ppermute | solution.py:69
  61.1 11.3 %collective-permute-start.14 = (bf16[3,8,64,128]{3,2,1,0:T(8,128)(2,1)}, bf16[3,8,64,128]{3,2,1,0:T(8,128)(2,1)S(1)}, u32[]{:S(2)}, u32[]{:S(2)}) collective-permute-start(bf16[3,8,64,128]{3,2,1,0:T(8,128)(2,1)} %get-tuple-element.14.w0), channel_id=1, source_target_pairs={{0,4},{2,6},{4,0},{6,2},{8,12},{10,14},{12,8},{14,10},{16,20},{18,... | collective-permute-start | bytes 1179656 | tf_op jit(solution)/shard_map/ppermute | solution.py:69
  61.9 18.9 %collective-permute-start.15 = (bf16[3,8,64,128]{3,2,1,0:T(8,128)(2,1)}, bf16[3,8,64,128]{3,2,1,0:T(8,128)(2,1)S(1)}, u32[]{:S(2)}, u32[]{:S(2)}) collective-permute-start(bf16[3,8,64,128]{3,2,1,0:T(8,128)(2,1)} %get-tuple-element.15.w1), channel_id=1, source_target_pairs={{0,4},{2,6},{4,0},{6,2},{8,12},{10,14},{12,8},{14,10},{16,20},{18,... | collective-permute-start | bytes 1179656 | tf_op jit(solution)/shard_map/ppermute | solution.py:69
  63.1 20.7 %collective-permute-start.12 = (bf16[3,8,64,128]{3,2,1,0:T(8,128)(2,1)}, bf16[3,8,64,128]{3,2,1,0:T(8,128)(2,1)S(1)}, u32[]{:S(2)}, u32[]{:S(2)}) collective-permute-start(bf16[3,8,64,128]{3,2,1,0:T(8,128)(2,1)} %get-tuple-element.14.w0), channel_id=1, source_target_pairs={{0,2},{2,0},{4,6},{6,4},{8,10},{10,8},{12,14},{14,12},{16,18},{18,... | collective-permute-start | bytes 1179656 | tf_op jit(solution)/shard_map/ppermute | solution.py:69
  72.4 13.0 %collective-permute-start.18 = (bf16[3,8,64,128]{3,2,1,0:T(8,128)(2,1)S(1)}, bf16[3,8,64,128]{3,2,1,0:T(8,128)(2,1)S(1)}, u32[]{:S(2)}, u32[]{:S(2)}) collective-permute-start(bf16[3,8,64,128]{3,2,1,0:T(8,128)(2,1)S(1)} %collective-permute-done.14.x0), channel_id=1, source_target_pairs={{0,8},{2,10},{4,28},{6,30},{8,16},{10,18},{12,4},{14,6},{16,24},{1... | collective-permute-start | bytes 1179656 | tf_op jit(solution)/shard_map/ppermute | solution.py:69
  80.8 13.9 %collective-permute-start.19 = (bf16[3,8,64,128]{3,2,1,0:T(8,128)(2,1)S(1)}, bf16[3,8,64,128]{3,2,1,0:T(8,128)(2,1)S(1)}, u32[]{:S(2)}, u32[]{:S(2)}) collective-permute-start(bf16[3,8,64,128]{3,2,1,0:T(8,128)(2,1)S(1)} %collective-permute-done.15.x1), channel_id=1, source_target_pairs={{0,8},{2,10},{4,28},{6,30},{8,16},{10,18},{12,4},{14,6},{16,24},{1... | collective-permute-start | bytes 1179656 | tf_op jit(solution)/shard_map/ppermute | solution.py:69
  80.8 15.1 %collective-permute-start.13 = (bf16[3,8,64,128]{3,2,1,0:T(8,128)(2,1)}, bf16[3,8,64,128]{3,2,1,0:T(8,128)(2,1)S(1)}, u32[]{:S(2)}, u32[]{:S(2)}) collective-permute-start(bf16[3,8,64,128]{3,2,1,0:T(8,128)(2,1)} %get-tuple-element.15.w1), channel_id=1, source_target_pairs={{0,2},{2,0},{4,6},{6,4},{8,10},{10,8},{12,14},{14,12},{16,18},{18,... | collective-permute-start | bytes 1179656 | tf_op jit(solution)/shard_map/ppermute | solution.py:69
  81.8 14.2 %collective-permute-start.16 = (bf16[3,8,64,128]{3,2,1,0:T(8,128)(2,1)S(1)}, bf16[3,8,64,128]{3,2,1,0:T(8,128)(2,1)S(1)}, u32[]{:S(2)}, u32[]{:S(2)}) collective-permute-start(bf16[3,8,64,128]{3,2,1,0:T(8,128)(2,1)S(1)} %collective-permute-done.14.x0), channel_id=1, source_target_pairs={{0,2},{6,4},{8,10},{14,12},{16,18},{22,20},{24,26},{30,28},{1,3},{... | collective-permute-start | bytes 1179656 | tf_op jit(solution)/shard_map/ppermute | solution.py:69
  83.8 12.2 %collective-permute-start.17 = (bf16[3,8,64,128]{3,2,1,0:T(8,128)(2,1)S(1)}, bf16[3,8,64,128]{3,2,1,0:T(8,128)(2,1)S(1)}, u32[]{:S(2)}, u32[]{:S(2)}) collective-permute-start(bf16[3,8,64,128]{3,2,1,0:T(8,128)(2,1)S(1)} %collective-permute-done.15.x1), channel_id=1, source_target_pairs={{0,2},{6,4},{8,10},{14,12},{16,18},{22,20},{24,26},{30,28},{1,3},{... | collective-permute-start | bytes 1179656 | tf_op jit(solution)/shard_map/ppermute | solution.py:69
  85.4 21.3 %collective-permute-start.20 = (bf16[3,8,64,128]{3,2,1,0:T(8,128)(2,1)S(1)}, bf16[3,8,64,128]{3,2,1,0:T(8,128)(2,1)S(1)}, u32[]{:S(2)}, u32[]{:S(2)}) collective-permute-start(bf16[3,8,64,128]{3,2,1,0:T(8,128)(2,1)S(1)} %collective-permute-done.18.z0), channel_id=1, source_target_pairs={{2,0},{4,6},{10,8},{12,14},{18,16},{20,22},{26,24},{28,30},{3,1},{... | collective-permute-start | bytes 1179656 | tf_op jit(solution)/shard_map/ppermute | solution.py:69
  94.7 12.0 %collective-permute-start.21 = (bf16[3,8,64,128]{3,2,1,0:T(8,128)(2,1)S(1)}, bf16[3,8,64,128]{3,2,1,0:T(8,128)(2,1)S(1)}, u32[]{:S(2)}, u32[]{:S(2)}) collective-permute-start(bf16[3,8,64,128]{3,2,1,0:T(8,128)(2,1)S(1)} %collective-permute-done.19.z1), channel_id=1, source_target_pairs={{2,0},{4,6},{10,8},{12,14},{18,16},{20,22},{26,24},{28,30},{3,1},{... | collective-permute-start | bytes 1179656 | tf_op jit(solution)/shard_map/ppermute | solution.py:69
  115.3 12.0 %collective-permute-start.22 = (bf16[3,8,64,128]{3,2,1,0:T(8,128)(2,1)}, bf16[3,8,64,128]{3,2,1,0:T(8,128)(2,1)S(1)}, u32[]{:S(2)}, u32[]{:S(2)}) collective-permute-start(bf16[3,8,64,128]{3,2,1,0:T(8,128)(2,1)} %bitcast.10), channel_id=1, source_target_pairs={{0,1},{1,0},{2,3},{3,2},{4,5},{5,4},{6,7},{7,6},{8,9},{9,8},{10,11... | collective-permute-start | bytes 1179656 | tf_op jit(solution)/shard_map/ppermute | solution.py:69
  (19 other events, 215.3 us)

commit v2 on v1

v2 whole, which is shorter than its diff:
```python
import jax
import jax.numpy as jnp
from jax import lax
from jax.experimental import pallas as pl
from jax.experimental.pallas import tpu as pltpu
from jax.sharding import PartitionSpec as P

REACH = 2
BAND = 2 * REACH + 1
WIDE = 4 * REACH + 1
VMEM = pl.BlockSpec(memory_space=pltpu.VMEM)
SMEM = pl.BlockSpec(memory_space=pltpu.SMEM)
PARAMS = pltpu.CompilerParams(vmem_limit_bytes=16 * 1024 * 1024)


def call(kernel, ins, outs, scratch=(), aliases=None, resident=True):
    specs = [SMEM if x.dtype == jnp.int32 else VMEM for x in ins]
    if resident:
        outs = [pltpu.VMEM(x.shape, x.dtype) for x in outs]
    ins = [
        x if x.dtype == jnp.int32 else pltpu.with_memory_space_constraint(x, pltpu.VMEM)
        for x in ins
    ]
    return pl.pallas_call(
        kernel,
        out_shape=tuple(outs),
        in_specs=specs,
        out_specs=tuple(VMEM for _ in outs),
        scratch_shapes=list(scratch),
        input_output_aliases=aliases or {},
        compiler_params=PARAMS,
    )(*ins)


def after(x, *others):
    return lax.optimization_barrier((x, *others))[0]


def offsets(j):
    first = j < 2
    return {
        "own": 0,
        "x": jnp.where(first, 2, -2),
        "core": jnp.where(j % 2 == 0, 1, -1),
        "core_x": jnp.where(first, 1, -1),
        "z": jnp.where(first, -2, 2),
        "core_z": jnp.where(first, -1, 1),
    }


def per_device(p_blocks, col_lists, fill_lists):
    rb, slots, bs, _ = p_blocks.shape
    nb, k_row = col_lists.shape
    fill = fill_lists.shape[1]
    n_rows = lax.axis_size("rows")
    n = lax.axis_size("inner")
    part = bs // n
    width = rb * bs
    bf16, f32 = jnp.bfloat16, jnp.float32
    shape = jax.ShapeDtypeStruct
    half = fill // 2

    def shift(m):
        return [(i, (i + m) % n) for i in range(n)]

    def along(r):
        group, j = divmod(r, 4)
        return (group + (1 if j < 2 else -1)) % (n_rows // 4) * 4 + j

    flip_x = [(r, r ^ 2) for r in range(n_rows)]
    flip_core = [(r, r ^ 1) for r in range(n_rows)]
    move_z = [(r, along(r)) for r in range(n_rows)]
    core_x = [(r, r ^ 1) for r in range(n_rows) if r % 4 in (0, 3)]
    core_z = [(r, r ^ 1) for r in range(n_rows) if r % 4 in (1, 2)]

    def send(x, axis, pairs):
        return lax.ppermute(x, axis, pairs)

    def slice_at(index):
        return pl.ds(pl.multiple_of(index * part, part), part)

    def wrapped(x):
        return jnp.where(x < 0, x + nb, jnp.where(x >= nb, x - nb, x))

    def pack(p_ref, own_ref, rest_ref, turned):
        q = lax.axis_index("inner")
        for i in range(rb):
            for s in range(slots):
                turned[i, s] = p_ref[i, s].T
                own_ref[i, s] = turned[i, s, slice_at(q), :]
                for m in range(1, n):
                    rest_ref[m - 1, i, s] = turned[i, s, slice_at(lax.rem(q + m, n)), :]

    own, rest = call(
        pack,
        [p_blocks],
        [shape((rb, slots, part, bs), bf16), shape((n - 1, rb, slots, part, bs), bf16)],
        [pltpu.VMEM((rb, slots, bs, bs), bf16)],
    )
    lists = jnp.concatenate([col_lists, fill_lists], axis=0)

    def received(parts):
        return parts[0][None] if n == 2 else jnp.stack(parts)

    def nth(x, m):
        return x.reshape(x.shape[1:]) if n == 2 else x[m]

    def add(ref, where, lanes, value):
        ref[where, lanes] = (ref[where, lanes].astype(f32) + value.astype(f32)).astype(bf16)

    def band_own(lists_ref, own_ref, rest_ref, out_ref):
        o = lax.axis_index("rows")
        q = lax.axis_index("inner")
        out_ref[...] = jnp.zeros(out_ref.shape, bf16)
        for s in range(slots):
            for i in range(rb):
                c = wrapped(lists_ref[o * rb + i, q * slots + s] - rb * (o - REACH)) * n
                lanes = pl.ds(i * bs, bs)
                add(out_ref, slice_at(c + q), lanes, own_ref[i, s])
                for m in range(1, n):
                    add(out_ref, slice_at(c + lax.rem(q + m, n)), lanes, rest_ref[m - 1, i, s])

    def band_other(lists_ref, in_ref, got_ref, left_ref, out_ref):
        o = lax.axis_index("rows")
        q = lax.axis_index("inner")
        for s in range(slots):
            for i in range(rb):
                lanes = pl.ds(i * bs, bs)
                for m in range(1, n):
                    g = lax.rem(q - m + n, n)
                    c = wrapped(lists_ref[o * rb + i, g * slots + s] - rb * (o - REACH))
                    if n == 2:
                        add(out_ref, slice_at(c * n + q), lanes, got_ref[0, i, s])
                        add(out_ref, slice_at(c * n + g), lanes, left_ref[i, s])
                    else:
                        add(out_ref, pl.ds(pl.multiple_of(c * bs, bs), bs), lanes, left_ref[g, i, s].T)

    band_shape = shape((BAND * width, width), bf16)
    (band,) = call(band_own, [lists, own, rest], [band_shape])

    got = received([send(nth(rest, m - 1), "inner", shift(m)) for m in range(1, n)])
    got = after(got, band)
    x_own = send(own, "rows", flip_x)
    x_got = send(got, "rows", flip_x)
    if n == 2:
        left = send(after(own, got), "inner", shift(1))
    else:
        left = lax.all_gather(p_blocks, "inner", axis=0)
    z_own = send(x_own, "rows", move_z)
    z_got = send(x_got, "rows", move_z)
    c_own, c_got = send(own, "rows", flip_core), send(got, "rows", flip_core)
    cx_own, cx_got = send(x_own, "rows", core_x), send(x_got, "rows", core_x)
    cz_own = send(z_own, "rows", core_z)
    (band,) = call(band_other, [lists, band, got, left], [band_shape], aliases={1: 0})

    span = BAND * rb * part
    wide = WIDE * rb * part
    owner_rows = rb * part
    acc_shape = shape((wide, width), f32)

    def square_term(lists_ref, d, own_ref, got_ref, left_ref, dense, acc_ref, first=False):
        o = lax.axis_index("rows")
        q = lax.axis_index("inner")
        source = lax.rem(o + d + n_rows, n_rows)
        dense[...] = jnp.zeros(dense.shape, bf16)

        def place(k, slot, value):
            c = wrapped(lists_ref[source * rb + k, slot] - rb * (source - REACH))
            add(dense, slice_at(c), pl.ds(k * bs, bs), value)

        for s in range(slots):
            for k in range(rb):
                place(k, q * slots + s, own_ref[k, s])
                for m in range(1, n):
                    place(k, lax.rem(q - m + n, n) * slots + s, got_ref[m - 1, k, s])
        weights = left_ref[pl.ds(pl.multiple_of((d + REACH) * width, width), width), :]
        term = jnp.dot(dense[...], weights, preferred_element_type=f32)
        where = pl.ds(pl.multiple_of((d + REACH) * owner_rows, owner_rows), span)
        if first:
            acc_ref[...] = jnp.zeros(acc_ref.shape, f32)
            acc_ref[where, :] = term
        else:
            acc_ref[where, :] += term

    def square_near(col, w, wg, c, cg, x, xg, cx, cxg, left_ref, acc_ref, dense):
        j = lax.rem(lax.axis_index("rows"), 4)
        d = offsets(j)
        square_term(col, 0, w, wg, left_ref, dense, acc_ref, first=True)
        square_term(col, d["core"], c, cg, left_ref, dense, acc_ref)
        square_term(col, d["x"], x, xg, left_ref, dense, acc_ref)

        @pl.when((j == 1) | (j == 2))
        def _():
            square_term(col, d["core_x"], cx, cxg, left_ref, dense, acc_ref)

    (acc,) = call(
        square_near,
        [lists, own, got, c_own, c_got, x_own, x_got, cx_own, cx_got, band],
        [acc_shape],
        [pltpu.VMEM((span, width), bf16)],
    )
    cz_got = send(after(z_got, acc), "rows", core_z)

    def kept(lists_ref, i, v):
        o = lax.axis_index("rows")
        return slice_at(wrapped(lists_ref[nb + o * rb + i, v] - rb * (o - 2 * REACH)))

    def square_far(col, acc_in, z, zg, cz, czg, left_ref, acc_ref, sq_ref, low0, low1, dense):
        j = lax.rem(lax.axis_index("rows"), 4)
        d = offsets(j)
        square_term(col, d["z"], z, zg, left_ref, dense, acc_ref)

        @pl.when((j == 0) | (j == 3))
        def _():
            square_term(col, d["core_z"], cz, czg, left_ref, dense, acc_ref)

        for v in range(fill):
            for i in range(rb):
                value = acc_ref[kept(col, i, v), pl.ds(i * bs, bs)]
                sq_ref[i, v] = value
                (low0 if v < half else low1)[i, v % half] = value.astype(bf16)

    low_shape = shape((rb, half, part, bs), bf16)
    _, square, low0, low1 = call(
        square_far,
        [lists, acc, z_own, z_got, cz_own, cz_got, band],
        [acc_shape, shape((rb, fill, part, bs), f32), low_shape, low_shape],
        [pltpu.VMEM((span, width), bf16)],
        aliases={1: 0},
    )

    def cube_term(lists_ref, d, reach, ref0, ref1, left_ref, dense, acc_ref, first=False):
        o = lax.axis_index("rows")
        source = lax.rem(o + d + n_rows, n_rows)
        blocks = (WIDE - reach) * rb
        start = jnp.maximum(d, 0) * rb
        rows = blocks * part
        dense[:rows, :] = jnp.zeros((rows, width), bf16)
        for v in range(fill):
            for k in range(rb):
                c = wrapped(lists_ref[nb + source * rb + k, v] - rb * (o - 2 * REACH)) - start

                @pl.when((c >= 0) & (c < blocks))
                def _():
                    dense[slice_at(c), pl.ds(k * bs, bs)] = (ref0 if v < half else ref1)[k, v % half]

        weights = left_ref[pl.ds(pl.multiple_of((d + REACH) * width, width), width), :]
        term = jnp.dot(dense[:rows, :], weights, preferred_element_type=f32)
        if first:
            acc_ref[...] = term
        else:
            acc_ref[pl.ds(pl.multiple_of(start * part, rb * part), rows), :] += term

    def cube_own(lists_ref, w0, w1, c0, c1, left_ref, acc_ref, dense):
        d = offsets(lax.rem(lax.axis_index("rows"), 4))
        cube_term(lists_ref, 0, 0, w0, w1, left_ref, dense, acc_ref, first=True)
        cube_term(lists_ref, d["core"], 1, c0, c1, left_ref, dense, acc_ref)

    def cube_near(lists_ref, acc_in, x0, x1, cx0, cx1, left_ref, acc_ref, dense):
        j = lax.rem(lax.axis_index("rows"), 4)
        d = offsets(j)
        cube_term(lists_ref, d["x"], 2, x0, x1, left_ref, dense, acc_ref)

        @pl.when((j == 1) | (j == 2))
        def _():
            cube_term(lists_ref, d["core_x"], 1, cx0, cx1, left_ref, dense, acc_ref)

    def cube_far(lists_ref, acc_in, z0, z1, cz0, cz1, left_ref, sq_ref, acc_ref, keep_ref, give_ref, dense):
        q = lax.axis_index("inner")
        j = lax.rem(lax.axis_index("rows"), 4)
        d = offsets(j)
        cube_term(lists_ref, d["z"], 2, z0, z1, left_ref, dense, acc_ref)

        @pl.when((j == 0) | (j == 3))
        def _():
            cube_term(lists_ref, d["core_z"], 1, cz0, cz1, left_ref, dense, acc_ref)

        def result(i, v):
            return 3.0 * sq_ref[i, v] - 2.0 * acc_ref[kept(lists_ref, i, v), pl.ds(i * bs, bs)]

        for s in range(slots):
            for i in range(rb):
                keep_ref[i, s] = result(i, q * slots + s)
                for m in range(1, n):
                    give_ref[m - 1, i, s] = result(i, lax.rem(q + m, n) * slots + s).astype(bf16)

    dense = [pltpu.VMEM((wide, width), bf16)]
    x0, x1 = send(low0, "rows", flip_x), send(low1, "rows", flip_x)
    c0, c1 = send(low0, "rows", flip_core), send(low1, "rows", flip_core)
    z0 = send(x0, "rows", move_z)
    (acc,) = call(cube_own, [lists, low0, low1, c0, c1, band], [acc_shape], dense)
    x1 = after(x1, acc)
    z1 = send(x1, "rows", move_z)
    cx0, cx1 = send(x0, "rows", core_x), send(x1, "rows", core_x)
    cz0 = send(z0, "rows", core_z)
    (acc,) = call(
        cube_near, [lists, acc, x0, x1, cx0, cx1, band], [acc_shape], dense, aliases={1: 0}
    )
    z1 = after(z1, acc)
    cz1 = send(z1, "rows", core_z)
    _, keep, give = call(
        cube_far,
        [lists, acc, z0, z1, cz0, cz1, band, square],
        [acc_shape, shape((rb, slots, part, bs), f32), shape((n - 1, rb, slots, part, bs), bf16)],
        dense,
        aliases={1: 0},
    )
    taken = received([send(nth(give, m - 1), "inner", shift(m)) for m in range(1, n)])

    def join(keep_ref, taken_ref, out_ref, turned):
        q = lax.axis_index("inner")
        for i in range(rb):
            for s in range(slots):
                turned[i, s, slice_at(q), :] = keep_ref[i, s]
                for m in range(1, n):
                    turned[i, s, slice_at(lax.rem(q - m + n, n)), :] = taken_ref[m - 1, i, s].astype(f32)
                out_ref[i, s] = turned[i, s].T

    (out,) = call(
        join,
        [keep, taken],
        [shape((rb, slots, bs, bs), f32)],
        [pltpu.VMEM((rb, slots, bs, bs), f32)],
        resident=False,
    )
    return out


def solution(mesh):
    in_specs = (P("rows", "inner", None, None), P(), P())
    out_specs = P("rows", "inner", None, None)
    return jax.shard_map(
        per_device, mesh=mesh, in_specs=in_specs, out_specs=out_specs, check_vma=False
    )
```

time: 132 us -> 112 us (0.85)
  Pallas kernels: 38.6 us -> 25.8 us
  local copies, waits for them, and re-layouts: 6.92 us -> 1.23 us
  waiting for transfers between devices: 57 us -> 55.4 us
    pallas_call x7 -> x9, Pallas kernels: 38.6 us -> 25.8 us  [call(): pl.pallas_call(kernel, out_shape=tuple(outs), in_specs=specs, out_specs=t...]
    unnamed x42 -> x2, local copies, waits for them, and re-layouts: 6.92 us -> 1.13 us
    ppermute x23, waiting for transfers between devices: 57 us -> 55.4 us  [send(): return lax.ppermute(x, axis, pairs)]
  transfers between devices with their start and end apart: 23 -> 23, of which waited for: 9 -> 12; matrix products, arithmetic and copies ran while one was open for 2% -> 1% of each run, Pallas kernels for 14% -> 14%
where the time goes in v2:
time: 112 us; the launch traced here: 111 us
  waiting for transfers between devices  55.4 us (49%)
  starting transfers between devices  27.6 us (25%)
  Pallas kernels  25.8 us (23%)
  local copies, waits for them, and re-layouts  1.23 us (1%)
    ppermute x23, waiting for transfers between devices, send(): return lax.ppermute(x, axis, pairs)  55.4 us
    ppermute x23, starting transfers between devices, send(): return lax.ppermute(x, axis, pairs)  27.6 us
    pallas_call x9, Pallas kernels, call(): pl.pallas_call(kernel, out_shape=tuple(outs), in_specs=specs, out_specs=t...  25.8 us
  transfers between devices with their start and end apart: 23, of which 12 were waited for; matrix products, arithmetic and copies ran while one was open for 1% of the time, Pallas kernels for 14%

profile of v2, /device:TPU:0, one launch (start us, length us, event | category | flops | bytes accessed | tf_op | source)
XLA Modules:
  0.0 111.0 jit_solution(9928358902334306433)
XLA Ops:
  1.6 3.0 %collective-permute-start = (bf16[3,8,64,128]{3,2,1,0:T(8,128)(2,1)S(1)}, bf16[3,8,64,128]{3,2,1,0:T(8,128)(2,1)S(1)}, u32[]{:S(2)}, u32[]{:S(2)}) collective-permute-start(bf16[3,8,64,128]{3,2,1,0:T(8,128)(2,1)S(1)} %bitcast.8), channel_id=1, source_target_pairs={{0,1},{1,0},{2,3},{3,2},{4,5},{5,4},{6,7},{7,6},{8,9},{9,8},{10,11... | collective-permute-start | bytes 1179656 | tf_op jit(solution)/shard_map/ppermute | solution.py:77
  7.0 1.8 %shard_map.38.in_ref = bf16[1920,384]{1,0:T(8,128)(2,1)S(1)} custom-call(s32[96,16]{1,0:T(8,128)S(1)} %copy.16.lists_ref.col, bf16[3,8,64,128]{3,2,1,0:T(8,128)(2,1)S(1)} %get-tuple-element.20.own_ref.w, bf16[1,3,8,64,128]{4,3,2,1,0:T(8,128)(2,1)S(1)} %get-tuple-element.18.rest_ref), custom_call_target="tpu_custom_call" | custom-call | tf_op jit(solution)/shard_map/pallas_call | solution.py:24
  8.9 4.9 %collective-permute-done = bf16[3,8,64,128]{3,2,1,0:T(8,128)(2,1)S(1)} collective-permute-done((bf16[3,8,64,128]{3,2,1,0:T(8,128)(2,1)S(1)}, bf16[3,8,64,128]{3,2,1,0:T(8,128)(2,1)S(1)}, u32[]{:S(2)}, u32[]{:S(2)}) %collective-permute-start) | collective-permute-done | bytes 393248 | tf_op jit(solution)/shard_map/ppermute | solution.py:77
  13.7 1.7 %collective-permute-start.4 = (bf16[1,3,8,64,128]{4,3,2,1,0:T(8,128)(2,1)S(1)}, bf16[1,3,8,64,128]{4,3,2,1,0:T(8,128)(2,1)S(1)}, u32[]{:S(2)}, u32[]{:S(2)}) collective-permute-start(bf16[1,3,8,64,128]{4,3,2,1,0:T(8,128)(2,1)S(1)} %bitcast.4), channel_id=1, source_target_pairs={{0,4},{2,6},{4,0},{6,2},{8,12},{10,14},{12,8},{14,10},{16,20},{18,... | collective-permute-start | bytes 1179656 | tf_op jit(solution)/shard_map/ppermute | solution.py:77
  15.4 1.5 %collective-permute-start.7 = (bf16[3,8,64,128]{3,2,1,0:T(8,128)(2,1)S(1)}, bf16[3,8,64,128]{3,2,1,0:T(8,128)(2,1)S(1)}, u32[]{:S(2)}, u32[]{:S(2)}) collective-permute-start(bf16[3,8,64,128]{3,2,1,0:T(8,128)(2,1)S(1)} %get-tuple-element.20.own_ref.w), channel_id=1, source_target_pairs={{0,1},{1,0},{2,3},{3,2},{4,5},{5,4},{6,7},{7,6},{8,9},{9,8},{10,11... | collective-permute-start | bytes 1179656 | tf_op jit(solution)/shard_map/ppermute | solution.py:77
  17.0 1.6 %collective-permute-start.8 = (bf16[3,8,64,128]{3,2,1,0:T(8,128)(2,1)S(1)}, bf16[3,8,64,128]{3,2,1,0:T(8,128)(2,1)S(1)}, u32[]{:S(2)}, u32[]{:S(2)}) collective-permute-start(bf16[3,8,64,128]{3,2,1,0:T(8,128)(2,1)S(1)} %collective-permute-done.3.x), channel_id=1, source_target_pairs={{0,8},{2,10},{4,28},{6,30},{8,16},{10,18},{12,4},{14,6},{16,24},{1... | collective-permute-start | bytes 1179656 | tf_op jit(solution)/shard_map/ppermute | solution.py:77
  18.6 2.1 %collective-permute-start.5 = (bf16[3,8,64,128]{3,2,1,0:T(8,128)(2,1)S(1)}, bf16[3,8,64,128]{3,2,1,0:T(8,128)(2,1)S(1)}, u32[]{:S(2)}, u32[]{:S(2)}) collective-permute-start(bf16[3,8,64,128]{3,2,1,0:T(8,128)(2,1)S(1)} %collective-permute-done.3.x), channel_id=1, source_target_pairs={{0,2},{6,4},{8,10},{14,12},{16,18},{22,20},{24,26},{30,28},{1,3},{... | collective-permute-start | bytes 1179656 | tf_op jit(solution)/shard_map/ppermute | solution.py:77
  20.7 3.3 %collective-permute-done.4.xg = bf16[1,3,8,64,128]{4,3,2,1,0:T(8,128)(2,1)S(1)} collective-permute-done((bf16[1,3,8,64,128]{4,3,2,1,0:T(8,128)(2,1)S(1)}, bf16[1,3,8,64,128]{4,3,2,1,0:T(8,128)(2,1)S(1)}, u32[]{:S(2)}, u32[]{:S(2)}) %collective-permute-start.4) | collective-permute-done | bytes 393248 | tf_op jit(solution)/shard_map/ppermute | solution.py:77
  26.9 1.7 %shard_map.39.left_ref = bf16[1920,384]{1,0:T(8,128)(2,1)S(1)} custom-call(s32[96,16]{1,0:T(8,128)S(1)} %copy.16.lists_ref.col, bf16[1920,384]{1,0:T(8,128)(2,1)S(1)} %shard_map.38.in_ref, bf16[1,3,8,64,128]{4,3,2,1,0:T(8,128)(2,1)S(1)} %bitcast.6, bf16[3,8,64,128]{3,2,1,0:T(8,128)(2,1)S(1)} %collective-permute-done.7.left_ref), custom_call_target="tpu_custom_call", output_to_operand_aliasing={{}: (1, {})} | custom-call | tf_op jit(solution)/shard_map/pallas_call | solution.py:24
  28.6 2.0 %collective-permute-done.8.z = bf16[3,8,64,128]{3,2,1,0:T(8,128)(2,1)S(1)} collective-permute-done((bf16[3,8,64,128]{3,2,1,0:T(8,128)(2,1)S(1)}, bf16[3,8,64,128]{3,2,1,0:T(8,128)(2,1)S(1)}, u32[]{:S(2)}, u32[]{:S(2)}) %collective-permute-start.8) | collective-permute-done | bytes 393248 | tf_op jit(solution)/shard_map/ppermute | solution.py:77
  32.0 3.8 %shard_map.40.acc_in = f32[1728,384]{1,0:T(8,128)S(1)} custom-call(s32[96,16]{1,0:T(8,128)S(1)} %copy.16.lists_ref.col, bf16[3,8,64,128]{3,2,1,0:T(8,128)(2,1)S(1)} %get-tuple-element.20.own_ref.w, bf16[1,3,8,64,128]{4,3,2,1,0:T(8,128)(2,1)S(1)} %bitcast.7, bf16[3,8,64,128]{3,2,1,0:T(8,128)(2,1)S(1)} %collective-permute-done.1.c, ...), custom_call_target="tpu_custom_call" | custom-call | tf_op jit(solution)/shard_map/pallas_call | solution.py:24
  35.8 3.0 %collective-permute-done.9.zg = bf16[1,3,8,64,128]{4,3,2,1,0:T(8,128)(2,1)S(1)} collective-permute-done((bf16[1,3,8,64,128]{4,3,2,1,0:T(8,128)(2,1)S(1)}, bf16[1,3,8,64,128]{4,3,2,1,0:T(8,128)(2,1)S(1)}, u32[]{:S(2)}, u32[]{:S(2)}) %collective-permute-start.9) | collective-permute-done | bytes 393248 | tf_op jit(solution)/shard_map/ppermute | solution.py:77
  40.1 2.3 %collective-permute-done.11.czg = bf16[1,3,8,64,128]{4,3,2,1,0:T(8,128)(2,1)S(1)} collective-permute-done((bf16[1,3,8,64,128]{4,3,2,1,0:T(8,128)(2,1)S(1)}, bf16[1,3,8,64,128]{4,3,2,1,0:T(8,128)(2,1)S(1)}, u32[]{:S(2)}, u32[]{:S(2)}) %collective-permute-start.11) | collective-permute-done | bytes 393248 | tf_op jit(solution)/shard_map/ppermute | solution.py:77
  42.4 3.6 %shard_map.41 = (f32[1728,384]{1,0:T(8,128)S(1)}, f32[3,16,64,128]{3,2,1,0:T(8,128)S(1)}, bf16[3,8,64,128]{3,2,1,0:T(8,128)(2,1)S(1)}, bf16[3,8,64,128]{3,2,1,0:T(8,128)(2,1)S(1)}) custom-call(s32[96,16]{1,0:T(8,128)S(1)} %copy.16.lists_ref.col, f32[1728,384]{1,0:T(8,128)S(1)} %shard_map.40.acc_in, ...), custom_call_target="tpu_custom_call", output_to_operand_aliasing={{0}: (1, {})} | custom-call | tf_op jit(solution)/shard_map/pallas_call | solution.py:24
  48.6 4.7 %shard_map.42.acc_in = f32[1728,384]{1,0:T(8,128)S(1)} custom-call(s32[96,16]{1,0:T(8,128)S(1)} %copy.16.lists_ref.col, bf16[3,8,64,128]{3,2,1,0:T(8,128)(2,1)S(1)} %get-tuple-element.22.w0, bf16[3,8,64,128]{3,2,1,0:T(8,128)(2,1)S(1)} %get-tuple-element.23.w1, bf16[3,8,64,128]{3,2,1,0:T(8,128)(2,1)S(1)} %collective-permute-done.12.c0, ...), custom_call_target="tpu_custom_call" | custom-call | tf_op jit(solution)/shard_map/pallas_call | solution.py:24
  53.4 5.2 %collective-permute-done.15.x1 = bf16[3,8,64,128]{3,2,1,0:T(8,128)(2,1)S(1)} collective-permute-done((bf16[3,8,64,128]{3,2,1,0:T(8,128)(2,1)S(1)}, bf16[3,8,64,128]{3,2,1,0:T(8,128)(2,1)S(1)}, u32[]{:S(2)}, u32[]{:S(2)}) %collective-permute-start.15) | collective-permute-done | bytes 393248 | tf_op jit(solution)/shard_map/ppermute | solution.py:77
  58.6 7.6 %collective-permute-done.14.x0 = bf16[3,8,64,128]{3,2,1,0:T(8,128)(2,1)S(1)} collective-permute-done((bf16[3,8,64,128]{3,2,1,0:T(8,128)(2,1)S(1)}, bf16[3,8,64,128]{3,2,1,0:T(8,128)(2,1)S(1)}, u32[]{:S(2)}, u32[]{:S(2)}) %collective-permute-start.14) | collective-permute-done | bytes 393248 | tf_op jit(solution)/shard_map/ppermute | solution.py:77
  70.1 3.0 %shard_map.43.acc_in = f32[1728,384]{1,0:T(8,128)S(1)} custom-call(s32[96,16]{1,0:T(8,128)S(1)} %copy.16.lists_ref.col, f32[1728,384]{1,0:T(8,128)S(1)} %shard_map.42.acc_in, bf16[3,8,64,128]{3,2,1,0:T(8,128)(2,1)S(1)} %collective-permute-done.14.x0, bf16[3,8,64,128]{3,2,1,0:T(8,128)(2,1)S(1)} %collective-permute-done.15.x1, ...), custom_call_target="tpu_custom_call", output_to_operand_aliasing={{}: (1, {})} | custom-call | tf_op jit(solution)/shard_map/pallas_call | solution.py:24
  73.2 9.6 %collective-permute-done.19.z1 = bf16[3,8,64,128]{3,2,1,0:T(8,128)(2,1)S(1)} collective-permute-done((bf16[3,8,64,128]{3,2,1,0:T(8,128)(2,1)S(1)}, bf16[3,8,64,128]{3,2,1,0:T(8,128)(2,1)S(1)}, u32[]{:S(2)}, u32[]{:S(2)}) %collective-permute-start.19) | collective-permute-done | bytes 393248 | tf_op jit(solution)/shard_map/ppermute | solution.py:77
  82.8 7.0 %collective-permute-done.18.z0 = bf16[3,8,64,128]{3,2,1,0:T(8,128)(2,1)S(1)} collective-permute-done((bf16[3,8,64,128]{3,2,1,0:T(8,128)(2,1)S(1)}, bf16[3,8,64,128]{3,2,1,0:T(8,128)(2,1)S(1)}, u32[]{:S(2)}, u32[]{:S(2)}) %collective-permute-start.18) | collective-permute-done | bytes 393248 | tf_op jit(solution)/shard_map/ppermute | solution.py:77
  94.8 4.7 %shard_map.44 = (f32[1728,384]{1,0:T(8,128)S(1)}, f32[3,8,64,128]{3,2,1,0:T(8,128)S(1)}, bf16[1,3,8,64,128]{4,3,2,1,0:T(8,128)(2,1)S(1)}) custom-call(s32[96,16]{1,0:T(8,128)S(1)} %copy.16.lists_ref.col, f32[1728,384]{1,0:T(8,128)S(1)} %shard_map.43.acc_in, bf16[3,8,64,128]{3,2,1,0:T(8,128)(2,1)S(1)} %collective-permute-done.18.z0, ...), custom_call_target="tpu_custom_call", output_to_operand_aliasing={{0}: (1, {})} | custom-call | tf_op jit(solution)/shard_map/pallas_call | solution.py:24
  99.4 1.6 %collective-permute-start.22 = (bf16[3,8,64,128]{3,2,1,0:T(8,128)(2,1)S(1)}, bf16[3,8,64,128]{3,2,1,0:T(8,128)(2,1)S(1)}, u32[]{:S(2)}, u32[]{:S(2)}) collective-permute-start(bf16[3,8,64,128]{3,2,1,0:T(8,128)(2,1)S(1)} %bitcast.10), channel_id=1, source_target_pairs={{0,1},{1,0},{2,3},{3,2},{4,5},{5,4},{6,7},{7,6},{8,9},{9,8},{10,11... | collective-permute-start | bytes 1179656 | tf_op jit(solution)/shard_map/ppermute | solution.py:77
  101.0 8.0 %collective-permute-done.22 = bf16[3,8,64,128]{3,2,1,0:T(8,128)(2,1)S(1)} collective-permute-done((bf16[3,8,64,128]{3,2,1,0:T(8,128)(2,1)S(1)}, bf16[3,8,64,128]{3,2,1,0:T(8,128)(2,1)S(1)}, u32[]{:S(2)}, u32[]{:S(2)}) %collective-permute-start.22) | collective-permute-done | bytes 393248 | tf_op jit(solution)/shard_map/ppermute | solution.py:77
  109.1 2.0 %shard_map.45 = f32[3,8,128,128]{3,2,1,0:T(8,128)} custom-call(f32[3,8,64,128]{3,2,1,0:T(8,128)S(1)} %get-tuple-element.27.keep_ref, bf16[1,3,8,64,128]{4,3,2,1,0:T(8,128)(2,1)S(1)} %bitcast.9), custom_call_target="tpu_custom_call" | custom-call | tf_op jit(solution)/shard_map/pallas_call | solution.py:24
  (35 shorter events, 20.8 us)
Async XLA Ops:
  0.0 1.1 %copy-start = (bf16[3,8,128,128]{3,2,1,0:T(8,128)(2,1)S(1)}, bf16[3,8,128,128]{3,2,1,0:T(8,128)(2,1)}, u32[]{:S(2)}) copy-start(bf16[3,8,128,128]{3,2,1,0:T(8,128)(2,1)} %p_ref.1) | copy-start | bytes 2359300
  1.6 12.2 %collective-permute-start = (bf16[3,8,64,128]{3,2,1,0:T(8,128)(2,1)S(1)}, bf16[3,8,64,128]{3,2,1,0:T(8,128)(2,1)S(1)}, u32[]{:S(2)}, u32[]{:S(2)}) collective-permute-start(bf16[3,8,64,128]{3,2,1,0:T(8,128)(2,1)S(1)} %bitcast.8), channel_id=1, source_target_pairs={{0,1},{1,0},{2,3},{3,2},{4,5},{5,4},{6,7},{7,6},{8,9},{9,8},{10,11... | collective-permute-start | bytes 1179656 | tf_op jit(solution)/shard_map/ppermute | solution.py:77
  4.6 12.4 %collective-permute-start.3 = (bf16[3,8,64,128]{3,2,1,0:T(8,128)(2,1)S(1)}, bf16[3,8,64,128]{3,2,1,0:T(8,128)(2,1)S(1)}, u32[]{:S(2)}, u32[]{:S(2)}) collective-permute-start(bf16[3,8,64,128]{3,2,1,0:T(8,128)(2,1)S(1)} %get-tuple-element.20.own_ref.w), channel_id=1, source_target_pairs={{0,4},{2,6},{4,0},{6,2},{8,12},{10,14},{12,8},{14,10},{16,20},{18,... | collective-permute-start | bytes 1179656 | tf_op jit(solution)/shard_map/ppermute | solution.py:77
  6.1 12.4 %collective-permute-start.1 = (bf16[3,8,64,128]{3,2,1,0:T(8,128)(2,1)S(1)}, bf16[3,8,64,128]{3,2,1,0:T(8,128)(2,1)S(1)}, u32[]{:S(2)}, u32[]{:S(2)}) collective-permute-start(bf16[3,8,64,128]{3,2,1,0:T(8,128)(2,1)S(1)} %get-tuple-element.20.own_ref.w), channel_id=1, source_target_pairs={{0,2},{2,0},{4,6},{6,4},{8,10},{10,8},{12,14},{14,12},{16,18},{18,... | collective-permute-start | bytes 1179656 | tf_op jit(solution)/shard_map/ppermute | solution.py:77
  13.7 10.3 %collective-permute-start.4 = (bf16[1,3,8,64,128]{4,3,2,1,0:T(8,128)(2,1)S(1)}, bf16[1,3,8,64,128]{4,3,2,1,0:T(8,128)(2,1)S(1)}, u32[]{:S(2)}, u32[]{:S(2)}) collective-permute-start(bf16[1,3,8,64,128]{4,3,2,1,0:T(8,128)(2,1)S(1)} %bitcast.4), channel_id=1, source_target_pairs={{0,4},{2,6},{4,0},{6,2},{8,12},{10,14},{12,8},{14,10},{16,20},{18,... | collective-permute-start | bytes 1179656 | tf_op jit(solution)/shard_map/ppermute | solution.py:77
  15.4 9.9 %collective-permute-start.7 = (bf16[3,8,64,128]{3,2,1,0:T(8,128)(2,1)S(1)}, bf16[3,8,64,128]{3,2,1,0:T(8,128)(2,1)S(1)}, u32[]{:S(2)}, u32[]{:S(2)}) collective-permute-start(bf16[3,8,64,128]{3,2,1,0:T(8,128)(2,1)S(1)} %get-tuple-element.20.own_ref.w), channel_id=1, source_target_pairs={{0,1},{1,0},{2,3},{3,2},{4,5},{5,4},{6,7},{7,6},{8,9},{9,8},{10,11... | collective-permute-start | bytes 1179656 | tf_op jit(solution)/shard_map/ppermute | solution.py:77
  17.0 15.0 %collective-permute-start.2 = (bf16[1,3,8,64,128]{4,3,2,1,0:T(8,128)(2,1)S(1)}, bf16[1,3,8,64,128]{4,3,2,1,0:T(8,128)(2,1)S(1)}, u32[]{:S(2)}, u32[]{:S(2)}) collective-permute-start(bf16[1,3,8,64,128]{4,3,2,1,0:T(8,128)(2,1)S(1)} %bitcast.5), channel_id=1, source_target_pairs={{0,2},{2,0},{4,6},{6,4},{8,10},{10,8},{12,14},{14,12},{16,18},{18,... | collective-permute-start | bytes 1179656 | tf_op jit(solution)/shard_map/ppermute | solution.py:77
  17.0 13.7 %collective-permute-start.8 = (bf16[3,8,64,128]{3,2,1,0:T(8,128)(2,1)S(1)}, bf16[3,8,64,128]{3,2,1,0:T(8,128)(2,1)S(1)}, u32[]{:S(2)}, u32[]{:S(2)}) collective-permute-start(bf16[3,8,64,128]{3,2,1,0:T(8,128)(2,1)S(1)} %collective-permute-done.3.x), channel_id=1, source_target_pairs={{0,8},{2,10},{4,28},{6,30},{8,16},{10,18},{12,4},{14,6},{16,24},{1... | collective-permute-start | bytes 1179656 | tf_op jit(solution)/shard_map/ppermute | solution.py:77
  18.6 13.4 %collective-permute-start.5 = (bf16[3,8,64,128]{3,2,1,0:T(8,128)(2,1)S(1)}, bf16[3,8,64,128]{3,2,1,0:T(8,128)(2,1)S(1)}, u32[]{:S(2)}, u32[]{:S(2)}) collective-permute-start(bf16[3,8,64,128]{3,2,1,0:T(8,128)(2,1)S(1)} %collective-permute-done.3.x), channel_id=1, source_target_pairs={{0,2},{6,4},{8,10},{14,12},{16,18},{22,20},{24,26},{30,28},{1,3},{... | collective-permute-start | bytes 1179656 | tf_op jit(solution)/shard_map/ppermute | solution.py:77
  24.0 7.9 %collective-permute-start.6 = (bf16[1,3,8,64,128]{4,3,2,1,0:T(8,128)(2,1)S(1)}, bf16[1,3,8,64,128]{4,3,2,1,0:T(8,128)(2,1)S(1)}, u32[]{:S(2)}, u32[]{:S(2)}) collective-permute-start(bf16[1,3,8,64,128]{4,3,2,1,0:T(8,128)(2,1)S(1)} %collective-permute-done.4.xg), channel_id=1, source_target_pairs={{0,2},{6,4},{8,10},{14,12},{16,18},{22,20},{24,26},{30,28},{1,3},{... | collective-permute-start | bytes 1179656 | tf_op jit(solution)/shard_map/ppermute | solution.py:77
  25.4 13.4 %collective-permute-start.9 = (bf16[1,3,8,64,128]{4,3,2,1,0:T(8,128)(2,1)S(1)}, bf16[1,3,8,64,128]{4,3,2,1,0:T(8,128)(2,1)S(1)}, u32[]{:S(2)}, u32[]{:S(2)}) collective-permute-start(bf16[1,3,8,64,128]{4,3,2,1,0:T(8,128)(2,1)S(1)} %collective-permute-done.4.xg), channel_id=1, source_target_pairs={{0,8},{2,10},{4,28},{6,30},{8,16},{10,18},{12,4},{14,6},{16,24},{1... | collective-permute-start | bytes 1179656 | tf_op jit(solution)/shard_map/ppermute | solution.py:77
  30.7 9.4 %collective-permute-start.10 = (bf16[3,8,64,128]{3,2,1,0:T(8,128)(2,1)S(1)}, bf16[3,8,64,128]{3,2,1,0:T(8,128)(2,1)S(1)}, u32[]{:S(2)}, u32[]{:S(2)}) collective-permute-start(bf16[3,8,64,128]{3,2,1,0:T(8,128)(2,1)S(1)} %collective-permute-done.8.z), channel_id=1, source_target_pairs={{2,0},{4,6},{10,8},{12,14},{18,16},{20,22},{26,24},{28,30},{3,1},{... | collective-permute-start | bytes 1179656 | tf_op jit(solution)/shard_map/ppermute | solution.py:77
  38.8 3.6 %collective-permute-start.11 = (bf16[1,3,8,64,128]{4,3,2,1,0:T(8,128)(2,1)S(1)}, bf16[1,3,8,64,128]{4,3,2,1,0:T(8,128)(2,1)S(1)}, u32[]{:S(2)}, u32[]{:S(2)}) collective-permute-start(bf16[1,3,8,64,128]{4,3,2,1,0:T(8,128)(2,1)S(1)} %collective-permute-done.9.zg), channel_id=1, source_target_pairs={{2,0},{4,6},{10,8},{12,14},{18,16},{20,22},{26,24},{28,30},{3,1},{... | collective-permute-start | bytes 1179656 | tf_op jit(solution)/shard_map/ppermute | solution.py:77
  46.0 2.6 %collective-permute-start.12 = (bf16[3,8,64,128]{3,2,1,0:T(8,128)(2,1)S(1)}, bf16[3,8,64,128]{3,2,1,0:T(8,128)(2,1)S(1)}, u32[]{:S(2)}, u32[]{:S(2)}) collective-permute-start(bf16[3,8,64,128]{3,2,1,0:T(8,128)(2,1)S(1)} %get-tuple-element.22.w0), channel_id=1, source_target_pairs={{0,2},{2,0},{4,6},{6,4},{8,10},{10,8},{12,14},{14,12},{16,18},{18,... | collective-permute-start | bytes 1179656 | tf_op jit(solution)/shard_map/ppermute | solution.py:77
  46.1 2.5 %collective-permute-start.13 = (bf16[3,8,64,128]{3,2,1,0:T(8,128)(2,1)S(1)}, bf16[3,8,64,128]{3,2,1,0:T(8,128)(2,1)S(1)}, u32[]{:S(2)}, u32[]{:S(2)}) collective-permute-start(bf16[3,8,64,128]{3,2,1,0:T(8,128)(2,1)S(1)} %get-tuple-element.23.w1), channel_id=1, source_target_pairs={{0,2},{2,0},{4,6},{6,4},{8,10},{10,8},{12,14},{14,12},{16,18},{18,... | collective-permute-start | bytes 1179656 | tf_op jit(solution)/shard_map/ppermute | solution.py:77
  46.6 12.0 %collective-permute-start.15 = (bf16[3,8,64,128]{3,2,1,0:T(8,128)(2,1)S(1)}, bf16[3,8,64,128]{3,2,1,0:T(8,128)(2,1)S(1)}, u32[]{:S(2)}, u32[]{:S(2)}) collective-permute-start(bf16[3,8,64,128]{3,2,1,0:T(8,128)(2,1)S(1)} %get-tuple-element.23.w1), channel_id=1, source_target_pairs={{0,4},{2,6},{4,0},{6,2},{8,12},{10,14},{12,8},{14,10},{16,20},{18,... | collective-permute-start | bytes 1179656 | tf_op jit(solution)/shard_map/ppermute | solution.py:77
  47.4 18.7 %collective-permute-start.14 = (bf16[3,8,64,128]{3,2,1,0:T(8,128)(2,1)S(1)}, bf16[3,8,64,128]{3,2,1,0:T(8,128)(2,1)S(1)}, u32[]{:S(2)}, u32[]{:S(2)}) collective-permute-start(bf16[3,8,64,128]{3,2,1,0:T(8,128)(2,1)S(1)} %get-tuple-element.22.w0), channel_id=1, source_target_pairs={{0,4},{2,6},{4,0},{6,2},{8,12},{10,14},{12,8},{14,10},{16,20},{18,... | collective-permute-start | bytes 1179656 | tf_op jit(solution)/shard_map/ppermute | solution.py:77
  66.1 4.0 %collective-permute-start.16 = (bf16[3,8,64,128]{3,2,1,0:T(8,128)(2,1)S(1)}, bf16[3,8,64,128]{3,2,1,0:T(8,128)(2,1)S(1)}, u32[]{:S(2)}, u32[]{:S(2)}) collective-permute-start(bf16[3,8,64,128]{3,2,1,0:T(8,128)(2,1)S(1)} %collective-permute-done.14.x0), channel_id=1, source_target_pairs={{0,2},{6,4},{8,10},{14,12},{16,18},{22,20},{24,26},{30,28},{1,3},{... | collective-permute-start | bytes 1179656 | tf_op jit(solution)/shard_map/ppermute | solution.py:77
  67.4 2.7 %collective-permute-start.17 = (bf16[3,8,64,128]{3,2,1,0:T(8,128)(2,1)S(1)}, bf16[3,8,64,128]{3,2,1,0:T(8,128)(2,1)S(1)}, u32[]{:S(2)}, u32[]{:S(2)}) collective-permute-start(bf16[3,8,64,128]{3,2,1,0:T(8,128)(2,1)S(1)} %collective-permute-done.15.x1), channel_id=1, source_target_pairs={{0,2},{6,4},{8,10},{14,12},{16,18},{22,20},{24,26},{30,28},{1,3},{... | collective-permute-start | bytes 1179656 | tf_op jit(solution)/shard_map/ppermute | solution.py:77
  68.8 14.0 %collective-permute-start.19 = (bf16[3,8,64,128]{3,2,1,0:T(8,128)(2,1)S(1)}, bf16[3,8,64,128]{3,2,1,0:T(8,128)(2,1)S(1)}, u32[]{:S(2)}, u32[]{:S(2)}) collective-permute-start(bf16[3,8,64,128]{3,2,1,0:T(8,128)(2,1)S(1)} %collective-permute-done.15.x1), channel_id=1, source_target_pairs={{0,8},{2,10},{4,28},{6,30},{8,16},{10,18},{12,4},{14,6},{16,24},{1... | collective-permute-start | bytes 1179656 | tf_op jit(solution)/shard_map/ppermute | solution.py:77
  68.8 21.0 %collective-permute-start.18 = (bf16[3,8,64,128]{3,2,1,0:T(8,128)(2,1)S(1)}, bf16[3,8,64,128]{3,2,1,0:T(8,128)(2,1)S(1)}, u32[]{:S(2)}, u32[]{:S(2)}) collective-permute-start(bf16[3,8,64,128]{3,2,1,0:T(8,128)(2,1)S(1)} %collective-permute-done.14.x0), channel_id=1, source_target_pairs={{0,8},{2,10},{4,28},{6,30},{8,16},{10,18},{12,4},{14,6},{16,24},{1... | collective-permute-start | bytes 1179656 | tf_op jit(solution)/shard_map/ppermute | solution.py:77
  89.8 3.6 %collective-permute-start.20 = (bf16[3,8,64,128]{3,2,1,0:T(8,128)(2,1)S(1)}, bf16[3,8,64,128]{3,2,1,0:T(8,128)(2,1)S(1)}, u32[]{:S(2)}, u32[]{:S(2)}) collective-permute-start(bf16[3,8,64,128]{3,2,1,0:T(8,128)(2,1)S(1)} %collective-permute-done.18.z0), channel_id=1, source_target_pairs={{2,0},{4,6},{10,8},{12,14},{18,16},{20,22},{26,24},{28,30},{3,1},{... | collective-permute-start | bytes 1179656 | tf_op jit(solution)/shard_map/ppermute | solution.py:77
  91.1 3.6 %collective-permute-start.21 = (bf16[3,8,64,128]{3,2,1,0:T(8,128)(2,1)S(1)}, bf16[3,8,64,128]{3,2,1,0:T(8,128)(2,1)S(1)}, u32[]{:S(2)}, u32[]{:S(2)}) collective-permute-start(bf16[3,8,64,128]{3,2,1,0:T(8,128)(2,1)S(1)} %collective-permute-done.19.z1), channel_id=1, source_target_pairs={{2,0},{4,6},{10,8},{12,14},{18,16},{20,22},{26,24},{28,30},{3,1},{... | collective-permute-start | bytes 1179656 | tf_op jit(solution)/shard_map/ppermute | solution.py:77
  99.4 9.6 %collective-permute-start.22 = (bf16[3,8,64,128]{3,2,1,0:T(8,128)(2,1)S(1)}, bf16[3,8,64,128]{3,2,1,0:T(8,128)(2,1)S(1)}, u32[]{:S(2)}, u32[]{:S(2)}) collective-permute-start(bf16[3,8,64,128]{3,2,1,0:T(8,128)(2,1)S(1)} %bitcast.10), channel_id=1, source_target_pairs={{0,1},{1,0},{2,3},{3,2},{4,5},{5,4},{6,7},{7,6},{8,9},{9,8},{10,11... | collective-permute-start | bytes 1179656 | tf_op jit(solution)/shard_map/ppermute | solution.py:77

commit v3 on v2

v3 whole, which is shorter than its diff:
```python
import jax
import jax.numpy as jnp
from jax import lax
from jax.experimental import pallas as pl
from jax.experimental.pallas import tpu as pltpu
from jax.sharding import PartitionSpec as P

REACH = 2
BAND = 2 * REACH + 1
WIDE = 4 * REACH + 1
VMEM = pl.BlockSpec(memory_space=pltpu.VMEM)
SMEM = pl.BlockSpec(memory_space=pltpu.SMEM)
PARAMS = pltpu.CompilerParams(vmem_limit_bytes=16 * 1024 * 1024)


def call(kernel, ins, outs, scratch=(), aliases=None, resident=True):
    specs = [SMEM if x.dtype == jnp.int32 else VMEM for x in ins]
    if resident:
        outs = [pltpu.VMEM(x.shape, x.dtype) for x in outs]
    ins = [
        x if x.dtype == jnp.int32 else pltpu.with_memory_space_constraint(x, pltpu.VMEM)
        for x in ins
    ]
    return pl.pallas_call(
        kernel,
        out_shape=tuple(outs),
        in_specs=specs,
        out_specs=tuple(VMEM for _ in outs),
        scratch_shapes=list(scratch),
        input_output_aliases=aliases or {},
        compiler_params=PARAMS,
    )(*ins)


def after(x, *others):
    return lax.optimization_barrier((x, *others))[0]


def offsets(j):
    first = j < 2
    return {
        "own": 0,
        "x": jnp.where(first, 2, -2),
        "core": jnp.where(j % 2 == 0, 1, -1),
        "core_x": jnp.where(first, 1, -1),
        "z": jnp.where(first, -2, 2),
        "core_z": jnp.where(first, -1, 1),
    }


def per_device(p_blocks, col_lists, fill_lists):
    rb, slots, bs, _ = p_blocks.shape
    nb = col_lists.shape[0]
    fill = fill_lists.shape[1]
    n_rows = lax.axis_size("rows")
    n = lax.axis_size("inner")
    part = bs // n
    cuts = 2 if part % 32 == 0 else 1
    cols = part // cuts
    width = rb * bs
    bf16, f32 = jnp.bfloat16, jnp.float32
    shape = jax.ShapeDtypeStruct
    chunks = range(cuts)

    def shift(m):
        return [(i, (i + m) % n) for i in range(n)]

    def along(r):
        group, j = divmod(r, 4)
        return (group + (1 if j < 2 else -1)) % (n_rows // 4) * 4 + j

    flip_x = [(r, r ^ 2) for r in range(n_rows)]
    flip_core = [(r, r ^ 1) for r in range(n_rows)]
    move_z = [(r, along(r)) for r in range(n_rows)]

    def send(x, pairs, axis="rows"):
        return lax.ppermute(x, axis, pairs)

    def rows_at(index, size):
        return pl.ds(pl.multiple_of(index * size, size), size)

    def wrapped(x):
        return jnp.where(x < 0, x + nb, jnp.where(x >= nb, x - nb, x))

    def received(parts):
        return parts[0][None] if n == 2 else jnp.stack(parts)

    def nth(x, m):
        return x.reshape(x.shape[1:]) if n == 2 else x[m]

    def exchange(x):
        return received([send(nth(x, m - 1), shift(m), "inner") for m in range(1, n)])

    def pack(p_ref, mine_ref, *refs):
        own_refs, rest_refs, turned = refs[:cuts], refs[cuts : 2 * cuts], refs[-1]
        q = lax.axis_index("inner")
        for i in range(rb):
            for s in range(slots):
                turned[i, s] = p_ref[i, s].T
                mine_ref[i, s] = turned[i, s, rows_at(q, part), :]
                for c in chunks:
                    own_refs[c][i, s] = turned[i, s, rows_at(q * cuts + c, cols), :]
                    for m in range(1, n):
                        to = lax.rem(q + m, n)
                        rest_refs[c][m - 1, i, s] = turned[i, s, rows_at(to * cuts + c, cols), :]

    packed = call(
        pack,
        [p_blocks],
        [shape((rb, slots, part, bs), bf16)]
        + [shape((rb, slots, cols, bs), bf16)] * cuts
        + [shape((n - 1, rb, slots, cols, bs), bf16)] * cuts,
        [pltpu.VMEM((rb, slots, bs, bs), bf16)],
    )
    mine, own, rest = packed[0], packed[1 : 1 + cuts], packed[1 + cuts :]
    lists = jnp.concatenate([col_lists, fill_lists], axis=0)

    def add(ref, where, lanes, value):
        ref[where, lanes] = (ref[where, lanes].astype(f32) + value.astype(f32)).astype(bf16)

    def band_own(lists_ref, own_ref, *refs):
        rest_refs, out_ref = refs[:cuts], refs[cuts]
        o = lax.axis_index("rows")
        q = lax.axis_index("inner")
        out_ref[...] = jnp.zeros(out_ref.shape, bf16)
        for s in range(slots):
            for i in range(rb):
                c = wrapped(lists_ref[o * rb + i, q * slots + s] - rb * (o - REACH)) * n
                lanes = pl.ds(i * bs, bs)
                add(out_ref, rows_at(c + q, part), lanes, own_ref[i, s])
                for m in range(1, n):
                    at = (c + lax.rem(q + m, n)) * cuts
                    for k in chunks:
                        add(out_ref, rows_at(at + k, cols), lanes, rest_refs[k][m - 1, i, s])

    def band_other(lists_ref, in_ref, left_ref, *refs):
        got_refs, out_ref = refs[:cuts], refs[cuts]
        o = lax.axis_index("rows")
        q = lax.axis_index("inner")
        for s in range(slots):
            for i in range(rb):
                lanes = pl.ds(i * bs, bs)
                for m in range(1, n):
                    g = lax.rem(q - m + n, n)
                    c = wrapped(lists_ref[o * rb + i, g * slots + s] - rb * (o - REACH))
                    if n == 2:
                        for k in chunks:
                            at = (c * n + q) * cuts + k
                            add(out_ref, rows_at(at, cols), lanes, got_refs[k][0, i, s])
                        add(out_ref, rows_at(c * n + g, part), lanes, left_ref[i, s])
                    else:
                        add(out_ref, rows_at(c, bs), lanes, left_ref[g, i, s].T)

    band_shape = shape((BAND * width, width), bf16)
    (band,) = call(band_own, [lists, mine, *rest], [band_shape])

    got = [exchange(x) for x in rest]
    if n == 2:
        left = send(mine, shift(1), "inner")
    else:
        left = lax.all_gather(p_blocks, "inner", axis=0)
    c_mine = send(mine, flip_core)
    c_got = [send(x, flip_core) for x in got]
    x_own, x_got, z_own, z_got = [], [], [], []
    for c in chunks:
        x_own.append(send(own[c] if c == 0 else after(own[c], x_own[c - 1]), flip_x))
        x_got.append(send(got[c], flip_x))
        z_own.append(send(x_own[c], move_z))
        z_got.append(send(x_got[c], move_z))
    cx_own, cx_got = [send(x, flip_core) for x in x_own], [send(x, flip_core) for x in x_got]
    cz_own, cz_got = [send(x, flip_core) for x in z_own], [send(x, flip_core) for x in z_got]
    (band,) = call(band_other, [lists, band, left, *got], [band_shape], aliases={1: 0})

    span = BAND * rb * cols
    wide = WIDE * rb * cols
    acc_shape = shape((wide, width), f32)

    def weights(left_ref, d):
        return left_ref[rows_at(d + REACH, width), :]

    def square_term(lists_ref, d, own_ref, got_ref, left_ref, dense, acc_ref, first=False, cut=None):
        o = lax.axis_index("rows")
        q = lax.axis_index("inner")
        source = lax.rem(o + d + n_rows, n_rows)
        dense[...] = jnp.zeros(dense.shape, bf16)

        def place(k, slot, value):
            c = wrapped(lists_ref[source * rb + k, slot] - rb * (source - REACH))
            add(dense, rows_at(c, cols), pl.ds(k * bs, bs), value)

        for s in range(slots):
            for k in range(rb):
                value = own_ref[k, s] if cut is None else own_ref[k, s, pl.ds(cut * cols, cols), :]
                place(k, q * slots + s, value)
                for m in range(1, n):
                    place(k, lax.rem(q - m + n, n) * slots + s, got_ref[m - 1, k, s])
        term = jnp.dot(dense[...], weights(left_ref, d), preferred_element_type=f32)
        where = pl.ds(pl.multiple_of((d + REACH) * rb * cols, rb * cols), span)
        if first:
            acc_ref[...] = jnp.zeros(acc_ref.shape, f32)
            acc_ref[where, :] = term
        else:
            acc_ref[where, :] += term

    def kept(lists_ref, i, v):
        o = lax.axis_index("rows")
        return rows_at(wrapped(lists_ref[nb + o * rb + i, v] - rb * (o - 2 * REACH)), cols)

    def square(c, band):
        def near(lists_ref, w, wg, u, ug, x, xg, cx, cxg, left_ref, acc_ref, dense):
            j = lax.rem(lax.axis_index("rows"), 4)
            d = offsets(j)
            square_term(lists_ref, 0, w, wg, left_ref, dense, acc_ref, first=True)
            square_term(lists_ref, d["core"], u, ug, left_ref, dense, acc_ref, cut=c)
            square_term(lists_ref, d["x"], x, xg, left_ref, dense, acc_ref)

            @pl.when((j == 1) | (j == 2))
            def _():
                square_term(lists_ref, d["core_x"], cx, cxg, left_ref, dense, acc_ref)

        def far(lists_ref, acc_in, z, zg, cz, czg, left_ref, acc_ref, sq_ref, low_ref, dense):
            j = lax.rem(lax.axis_index("rows"), 4)
            d = offsets(j)
            square_term(lists_ref, d["z"], z, zg, left_ref, dense, acc_ref)

            @pl.when((j == 0) | (j == 3))
            def _():
                square_term(lists_ref, d["core_z"], cz, czg, left_ref, dense, acc_ref)

            for v in range(fill):
                for i in range(rb):
                    value = acc_ref[kept(lists_ref, i, v), pl.ds(i * bs, bs)]
                    sq_ref[i, v] = value
                    low_ref[i, v] = value.astype(bf16)

        dense = [pltpu.VMEM((span, width), bf16)]
        (acc,) = call(
            near,
            [lists, own[c], got[c], c_mine, c_got[c], x_own[c], x_got[c], cx_own[c], cx_got[c], band],
            [acc_shape],
            dense,
        )
        kept_shape = (rb, fill, cols, bs)
        return call(
            far,
            [lists, acc, z_own[c], z_got[c], cz_own[c], cz_got[c], band],
            [acc_shape, shape(kept_shape, f32), shape(kept_shape, bf16)],
            dense,
            aliases={1: 0},
        )[1:]

    def cube_term(lists_ref, d, reach, low_ref, left_ref, dense, acc_ref, first=False):
        o = lax.axis_index("rows")
        source = lax.rem(o + d + n_rows, n_rows)
        blocks = (WIDE - reach) * rb
        start = jnp.maximum(d, 0) * rb
        rows = blocks * cols
        dense[:rows, :] = jnp.zeros((rows, width), bf16)
        for v in range(fill):
            for k in range(rb):
                c = wrapped(lists_ref[nb + source * rb + k, v] - rb * (o - 2 * REACH)) - start

                @pl.when((c >= 0) & (c < blocks))
                def _():
                    dense[rows_at(c, cols), pl.ds(k * bs, bs)] = low_ref[k, v]

        term = jnp.dot(dense[:rows, :], weights(left_ref, d), preferred_element_type=f32)
        if first:
            acc_ref[...] = term
        else:
            acc_ref[pl.ds(pl.multiple_of(start * cols, rb * cols), rows), :] += term

    def cube_own(lists_ref, w, u, left_ref, acc_ref, dense):
        d = offsets(lax.rem(lax.axis_index("rows"), 4))
        cube_term(lists_ref, 0, 0, w, left_ref, dense, acc_ref, first=True)
        cube_term(lists_ref, d["core"], 1, u, left_ref, dense, acc_ref)

    def cube_near(lists_ref, acc_in, x, cx, left_ref, acc_ref, dense):
        j = lax.rem(lax.axis_index("rows"), 4)
        d = offsets(j)
        cube_term(lists_ref, d["x"], 2, x, left_ref, dense, acc_ref)

        @pl.when((j == 1) | (j == 2))
        def _():
            cube_term(lists_ref, d["core_x"], 1, cx, left_ref, dense, acc_ref)

    def cube_far(lists_ref, acc_in, z, cz, left_ref, sq_ref, acc_ref, keep_ref, give_ref, dense):
        q = lax.axis_index("inner")
        j = lax.rem(lax.axis_index("rows"), 4)
        d = offsets(j)
        cube_term(lists_ref, d["z"], 2, z, left_ref, dense, acc_ref)

        @pl.when((j == 0) | (j == 3))
        def _():
            cube_term(lists_ref, d["core_z"], 1, cz, left_ref, dense, acc_ref)

        def result(i, v):
            return 3.0 * sq_ref[i, v] - 2.0 * acc_ref[kept(lists_ref, i, v), pl.ds(i * bs, bs)]

        for s in range(slots):
            for i in range(rb):
                keep_ref[i, s] = result(i, q * slots + s)
                for m in range(1, n):
                    give_ref[m - 1, i, s] = result(i, lax.rem(q + m, n) * slots + s).astype(bf16)

    def cube(sq, low, x, z, ahead):
        dense = [pltpu.VMEM((wide, width), bf16)]
        u, cx, cz = send(low, flip_core), send(x, flip_core), send(z, flip_core)
        (acc,) = call(cube_own, [lists, low, u, after(band, *ahead)], [acc_shape], dense)
        (acc,) = call(cube_near, [lists, acc, x, cx, band], [acc_shape], dense, aliases={1: 0})
        return call(
            cube_far,
            [lists, acc, z, cz, band, sq],
            [acc_shape, shape((rb, slots, cols, bs), f32), shape((n - 1, rb, slots, cols, bs), bf16)],
            dense,
            aliases={1: 0},
        )[1:]

    sq, low = [], []
    for c in chunks:
        one = square(c, after(band, *low))
        sq.append(one[0])
        low.append(one[1])
    x = [send(v, flip_x) for v in low]
    z = [send(v, move_z) for v in x]
    keep, give = [], []
    for c in chunks:
        one = cube(sq[c], low[c], x[c], z[c], [low[-1]] + give)
        keep.append(one[0])
        give.append(one[1])
    taken = [exchange(v) for v in give]

    def join(*refs):
        keep_refs, taken_refs, out_ref, turned = refs[:cuts], refs[cuts : 2 * cuts], refs[-2], refs[-1]
        q = lax.axis_index("inner")
        for i in range(rb):
            for s in range(slots):
                for c in chunks:
                    turned[i, s, rows_at(q * cuts + c, cols), :] = keep_refs[c][i, s]
                    for m in range(1, n):
                        at = lax.rem(q - m + n, n) * cuts + c
                        turned[i, s, rows_at(at, cols), :] = taken_refs[c][m - 1, i, s].astype(f32)
                out_ref[i, s] = turned[i, s].T

    (out,) = call(
        join,
        [*keep, *taken],
        [shape((rb, slots, bs, bs), f32)],
        [pltpu.VMEM((rb, slots, bs, bs), f32)],
        resident=False,
    )
    return out


def solution(mesh):
    in_specs = (P("rows", "inner", None, None), P(), P())
    out_specs = P("rows", "inner", None, None)
    return jax.shard_map(
        per_device, mesh=mesh, in_specs=in_specs, out_specs=out_specs, check_vma=False
    )
```

time: 112 us -> 126 us (1.12)
  Pallas kernels: 25.8 us -> 38.5 us
  starting transfers between devices: 27.6 us -> 20.5 us
  local copies, waits for them, and re-layouts: 1.23 us -> 7.15 us
  waiting for transfers between devices: 55.4 us -> 58.1 us
    pallas_call x9 -> x14, Pallas kernels: 25.8 us -> 38.5 us  [call(): pl.pallas_call(kernel, out_shape=tuple(outs), in_specs=specs, out_specs=t...]
    ppermute x23 -> x34, starting transfers between devices: 27.6 us -> 20.5 us  [send(): return lax.ppermute(x, axis, pairs)]
    unnamed x2 -> x26, local copies, waits for them, and re-layouts: 1.13 us -> 7.06 us
    ppermute x23 -> x34, waiting for transfers between devices: 55.4 us -> 58.1 us  [send(): return lax.ppermute(x, axis, pairs)]
  transfers between devices with their start and end apart: 23 -> 34, of which waited for: 12 -> 13; matrix products, arithmetic and copies ran while one was open for 1% -> 1% of each run, Pallas kernels for 14% -> 26%
where the time goes in v3:
time: 126 us; the launch traced here: 125 us
  waiting for transfers between devices  58.1 us (46%)
  Pallas kernels  38.5 us (31%)
  starting transfers between devices  20.5 us (16%)
  local copies, waits for them, and re-layouts  7.15 us (6%)
    ppermute x34, waiting for transfers between devices, send(): return lax.ppermute(x, axis, pairs)  58.1 us
    pallas_call x14, Pallas kernels, call(): pl.pallas_call(kernel, out_shape=tuple(outs), in_specs=specs, out_specs=t...  38.5 us
    ppermute x34, starting transfers between devices, send(): return lax.ppermute(x, axis, pairs)  20.5 us
    unnamed x26, local copies, waits for them, and re-layouts  7.06 us
  transfers between devices with their start and end apart: 34, of which 13 were waited for; matrix products, arithmetic and copies ran while one was open for 1% of the time, Pallas kernels for 26%

profile of v3, /device:TPU:0, one launch (start us, length us, event | category | flops | bytes accessed | tf_op | source)
XLA Modules:
  0.0 125.3 jit_solution(15561440790324043291)
XLA Ops:
  1.6 3.0 %collective-permute-start = (bf16[3,8,32,128]{3,2,1,0:T(8,128)(2,1)S(1)}, bf16[3,8,32,128]{3,2,1,0:T(8,128)(2,1)S(1)}, u32[]{:S(2)}, u32[]{:S(2)}) collective-permute-start(bf16[3,8,32,128]{3,2,1,0:T(8,128)(2,1)S(1)} %bitcast.16), channel_id=1, source_target_pairs={{0,1},{1,0},{2,3},{3,2},{4,5},{5,4},{6,7},{7,6},{8,9},{9,8},{10,11... | collective-permute-start | bytes 589832 | tf_op jit(solution)/shard_map/ppermute | solution.py:77
  12.4 9.8 %collective-permute-done.8 = bf16[3,8,32,128]{3,2,1,0:T(8,128)(2,1)S(1)} collective-permute-done((bf16[3,8,32,128]{3,2,1,0:T(8,128)(2,1)S(1)}, bf16[3,8,32,128]{3,2,1,0:T(8,128)(2,1)S(1)}, u32[]{:S(2)}, u32[]{:S(2)}) %collective-permute-start.8) | collective-permute-done | bytes 196640 | tf_op jit(solution)/shard_map/ppermute | solution.py:77
  24.5 3.5 %collective-permute-start.15 = (bf16[3,8,32,128]{3,2,1,0:T(8,128)(2,1)S(1)}, bf16[3,8,32,128]{3,2,1,0:T(8,128)(2,1)S(1)}, u32[]{:S(2)}, u32[]{:S(2)}) collective-permute-start(bf16[3,8,32,128]{3,2,1,0:T(8,128)(2,1)S(1)} %get-tuple-element.28.w), channel_id=1, source_target_pairs={{0,4},{2,6},{4,0},{6,2},{8,12},{10,14},{12,8},{14,10},{16,20},{18,... | collective-permute-start | bytes 589832 | tf_op jit(solution)/shard_map/ppermute | solution.py:77
  28.2 3.5 %collective-permute-done.9.z = bf16[3,8,32,128]{3,2,1,0:T(8,128)(2,1)S(1)} collective-permute-done((bf16[3,8,32,128]{3,2,1,0:T(8,128)(2,1)S(1)}, bf16[3,8,32,128]{3,2,1,0:T(8,128)(2,1)S(1)}, u32[]{:S(2)}, u32[]{:S(2)}) %collective-permute-start.9) | collective-permute-done | bytes 196640 | tf_op jit(solution)/shard_map/ppermute | solution.py:77
  31.6 2.1 %collective-permute-done.15.x = bf16[3,8,32,128]{3,2,1,0:T(8,128)(2,1)S(1)} collective-permute-done((bf16[3,8,32,128]{3,2,1,0:T(8,128)(2,1)S(1)}, bf16[3,8,32,128]{3,2,1,0:T(8,128)(2,1)S(1)}, u32[]{:S(2)}, u32[]{:S(2)}) %collective-permute-start.15) | collective-permute-done | bytes 196640 | tf_op jit(solution)/shard_map/ppermute | solution.py:77
  33.9 3.2 %collective-permute-done.16.xg = bf16[1,3,8,32,128]{4,3,2,1,0:T(8,128)(2,1)S(1)} collective-permute-done((bf16[1,3,8,32,128]{4,3,2,1,0:T(8,128)(2,1)S(1)}, bf16[1,3,8,32,128]{4,3,2,1,0:T(8,128)(2,1)S(1)}, u32[]{:S(2)}, u32[]{:S(2)}) %collective-permute-start.16) | collective-permute-done | bytes 196640 | tf_op jit(solution)/shard_map/ppermute | solution.py:77
  39.6 2.2 %collective-permute-done.19.z = bf16[3,8,32,128]{3,2,1,0:T(8,128)(2,1)} collective-permute-done((bf16[3,8,32,128]{3,2,1,0:T(8,128)(2,1)S(1)}, bf16[3,8,32,128]{3,2,1,0:T(8,128)(2,1)}, u32[]{:S(2)}, u32[]{:S(2)}) %collective-permute-start.19) | collective-permute-done | bytes 196640 | tf_op jit(solution)/shard_map/ppermute | solution.py:77
  41.8 3.7 %collective-permute-done.20.zg = bf16[1,3,8,32,128]{4,3,2,1,0:T(8,128)(2,1)} collective-permute-done((bf16[1,3,8,32,128]{4,3,2,1,0:T(8,128)(2,1)S(1)}, bf16[1,3,8,32,128]{4,3,2,1,0:T(8,128)(2,1)}, u32[]{:S(2)}, u32[]{:S(2)}) %collective-permute-start.20) | collective-permute-done | bytes 196640 | tf_op jit(solution)/shard_map/ppermute | solution.py:77
  53.3 3.1 %shard_map.40.acc_in = f32[864,384]{1,0:T(8,128)S(1)} custom-call(s32[96,16]{1,0:T(8,128)S(1)} %copy.21.lists_ref, bf16[3,8,32,128]{3,2,1,0:T(8,128)(2,1)S(1)} %get-tuple-element.22.w, bf16[1,3,8,32,128]{4,3,2,1,0:T(8,128)(2,1)S(1)} %bitcast.15, bf16[3,8,64,128]{3,2,1,0:T(8,128)(2,1)S(1)} %collective-permute-done.1.u, ...), custom_call_target="tpu_custom_call" | custom-call | tf_op jit(solution)/shard_map/pallas_call | solution.py:24
  56.4 3.0 %shard_map.41 = (f32[864,384]{1,0:T(8,128)S(1)}, f32[3,16,32,128]{3,2,1,0:T(8,128)S(1)}, bf16[3,16,32,128]{3,2,1,0:T(8,128)(2,1)S(1)}) custom-call(s32[96,16]{1,0:T(8,128)S(1)} %copy.21.lists_ref, f32[864,384]{1,0:T(8,128)S(1)} %shard_map.40.acc_in, bf16[3,8,32,128]{3,2,1,0:T(8,128)(2,1)S(1)} %collective-permute-done.9.z, ...), custom_call_target="tpu_custom_call", output_to_operand_aliasing={{0}: (1, {})} | custom-call | tf_op jit(solution)/shard_map/pallas_call | solution.py:24
  60.5 3.1 %shard_map.42.acc_in = f32[864,384]{1,0:T(8,128)S(1)} custom-call(s32[96,16]{1,0:T(8,128)S(1)} %copy.21.lists_ref, bf16[3,8,32,128]{3,2,1,0:T(8,128)(2,1)S(1)} %get-tuple-element.28.w, bf16[1,3,8,32,128]{4,3,2,1,0:T(8,128)(2,1)S(1)} %bitcast.11, bf16[3,8,64,128]{3,2,1,0:T(8,128)(2,1)S(1)} %collective-permute-done.1.u, ...), custom_call_target="tpu_custom_call" | custom-call | tf_op jit(solution)/shard_map/pallas_call | solution.py:24
  63.7 3.0 %shard_map.43 = (f32[864,384]{1,0:T(8,128)S(1)}, f32[3,16,32,128]{3,2,1,0:T(8,128)S(1)}, bf16[3,16,32,128]{3,2,1,0:T(8,128)(2,1)S(1)}) custom-call(s32[96,16]{1,0:T(8,128)S(1)} %copy.21.lists_ref, f32[864,384]{1,0:T(8,128)S(1)} %shard_map.42.acc_in, bf16[3,8,32,128]{3,2,1,0:T(8,128)(2,1)} %collective-permute-done.19.z, ...), custom_call_target="tpu_custom_call", output_to_operand_aliasing={{0}: (1, {})} | custom-call | tf_op jit(solution)/shard_map/pallas_call | solution.py:24
  67.7 3.8 %collective-permute-done.23.x = bf16[3,16,32,128]{3,2,1,0:T(8,128)(2,1)S(1)} collective-permute-done((bf16[3,16,32,128]{3,2,1,0:T(8,128)(2,1)S(1)}, bf16[3,16,32,128]{3,2,1,0:T(8,128)(2,1)S(1)}, u32[]{:S(2)}, u32[]{:S(2)}) %collective-permute-start.23) | collective-permute-done | bytes 393248 | tf_op jit(solution)/shard_map/ppermute | solution.py:77
  71.4 7.5 %collective-permute-done.28.x = bf16[3,16,32,128]{3,2,1,0:T(8,128)(2,1)S(1)} collective-permute-done((bf16[3,16,32,128]{3,2,1,0:T(8,128)(2,1)S(1)}, bf16[3,16,32,128]{3,2,1,0:T(8,128)(2,1)S(1)}, u32[]{:S(2)}, u32[]{:S(2)}) %collective-permute-start.28) | collective-permute-done | bytes 393248 | tf_op jit(solution)/shard_map/ppermute | solution.py:77
  78.9 4.1 %collective-permute-done.25.z = bf16[3,16,32,128]{3,2,1,0:T(8,128)(2,1)S(1)} collective-permute-done((bf16[3,16,32,128]{3,2,1,0:T(8,128)(2,1)S(1)}, bf16[3,16,32,128]{3,2,1,0:T(8,128)(2,1)S(1)}, u32[]{:S(2)}, u32[]{:S(2)}) %collective-permute-start.25) | collective-permute-done | bytes 393248 | tf_op jit(solution)/shard_map/ppermute | solution.py:77
  83.5 7.9 %collective-permute-done.30.z = bf16[3,16,32,128]{3,2,1,0:T(8,128)(2,1)S(1)} collective-permute-done((bf16[3,16,32,128]{3,2,1,0:T(8,128)(2,1)S(1)}, bf16[3,16,32,128]{3,2,1,0:T(8,128)(2,1)S(1)}, u32[]{:S(2)}, u32[]{:S(2)}) %collective-permute-start.30) | collective-permute-done | bytes 393248 | tf_op jit(solution)/shard_map/ppermute | solution.py:77
  91.4 3.9 %shard_map.44.acc_in = f32[864,384]{1,0:T(8,128)S(1)} custom-call(s32[96,16]{1,0:T(8,128)S(1)} %copy.21.lists_ref, bf16[3,16,32,128]{3,2,1,0:T(8,128)(2,1)S(1)} %get-tuple-element.26.w, bf16[3,16,32,128]{3,2,1,0:T(8,128)(2,1)S(1)} %collective-permute-done.13.u, bf16[1920,384]{1,0:T(8,128)(2,1)S(1)} %shard_map.39.left_ref), custom_call_target="tpu_custom_call" | custom-call | tf_op jit(solution)/shard_map/pallas_call | solution.py:24
  95.4 2.4 %shard_map.45.acc_in = f32[864,384]{1,0:T(8,128)S(1)} custom-call(s32[96,16]{1,0:T(8,128)S(1)} %copy.21.lists_ref, f32[864,384]{1,0:T(8,128)S(1)} %shard_map.44.acc_in, bf16[3,16,32,128]{3,2,1,0:T(8,128)(2,1)S(1)} %collective-permute-done.23.x, bf16[3,16,32,128]{3,2,1,0:T(8,128)(2,1)S(1)} %collective-permute-done.24.cx, ...), custom_call_target="tpu_custom_call", output_to_operand_aliasing={{}: (1, {})} | custom-call | tf_op jit(solution)/shard_map/pallas_call | solution.py:24
  97.8 3.8 %shard_map.46 = (f32[864,384]{1,0:T(8,128)S(1)}, f32[3,8,32,128]{3,2,1,0:T(8,128)S(1)}, bf16[1,3,8,32,128]{4,3,2,1,0:T(8,128)(2,1)S(1)}) custom-call(s32[96,16]{1,0:T(8,128)S(1)} %copy.21.lists_ref, f32[864,384]{1,0:T(8,128)S(1)} %shard_map.45.acc_in, bf16[3,16,32,128]{3,2,1,0:T(8,128)(2,1)S(1)} %collective-permute-done.25.z, ...), custom_call_target="tpu_custom_call", output_to_operand_aliasing={{0}: (1, {})} | custom-call | tf_op jit(solution)/shard_map/pallas_call | solution.py:24
  101.7 3.8 %shard_map.47.acc_in = f32[864,384]{1,0:T(8,128)S(1)} custom-call(s32[96,16]{1,0:T(8,128)S(1)} %copy.21.lists_ref, bf16[3,16,32,128]{3,2,1,0:T(8,128)(2,1)S(1)} %get-tuple-element.30.w, bf16[3,16,32,128]{3,2,1,0:T(8,128)(2,1)S(1)} %collective-permute-done.27.u, bf16[1920,384]{1,0:T(8,128)(2,1)S(1)} %shard_map.39.left_ref), custom_call_target="tpu_custom_call" | custom-call | tf_op jit(solution)/shard_map/pallas_call | solution.py:24
  105.4 2.4 %shard_map.48.acc_in = f32[864,384]{1,0:T(8,128)S(1)} custom-call(s32[96,16]{1,0:T(8,128)S(1)} %copy.21.lists_ref, f32[864,384]{1,0:T(8,128)S(1)} %shard_map.47.acc_in, bf16[3,16,32,128]{3,2,1,0:T(8,128)(2,1)S(1)} %collective-permute-done.28.x, bf16[3,16,32,128]{3,2,1,0:T(8,128)(2,1)S(1)} %collective-permute-done.29.cx, ...), custom_call_target="tpu_custom_call", output_to_operand_aliasing={{}: (1, {})} | custom-call | tf_op jit(solution)/shard_map/pallas_call | solution.py:24
  107.9 3.8 %shard_map.49 = (f32[864,384]{1,0:T(8,128)S(1)}, f32[3,8,32,128]{3,2,1,0:T(8,128)S(1)}, bf16[1,3,8,32,128]{4,3,2,1,0:T(8,128)(2,1)S(1)}) custom-call(s32[96,16]{1,0:T(8,128)S(1)} %copy.21.lists_ref, f32[864,384]{1,0:T(8,128)S(1)} %shard_map.48.acc_in, bf16[3,16,32,128]{3,2,1,0:T(8,128)(2,1)S(1)} %collective-permute-done.30.z, ...), custom_call_target="tpu_custom_call", output_to_operand_aliasing={{0}: (1, {})} | custom-call | tf_op jit(solution)/shard_map/pallas_call | solution.py:24
  113.8 5.7 %collective-permute-done.33 = bf16[3,8,32,128]{3,2,1,0:T(8,128)(2,1)S(1)} collective-permute-done((bf16[3,8,32,128]{3,2,1,0:T(8,128)(2,1)S(1)}, bf16[3,8,32,128]{3,2,1,0:T(8,128)(2,1)S(1)}, u32[]{:S(2)}, u32[]{:S(2)}) %collective-permute-start.33) | collective-permute-done | bytes 196640 | tf_op jit(solution)/shard_map/ppermute | solution.py:77
  119.5 3.8 %collective-permute-done.32 = bf16[3,8,32,128]{3,2,1,0:T(8,128)(2,1)S(1)} collective-permute-done((bf16[3,8,32,128]{3,2,1,0:T(8,128)(2,1)S(1)}, bf16[3,8,32,128]{3,2,1,0:T(8,128)(2,1)S(1)}, u32[]{:S(2)}, u32[]{:S(2)}) %collective-permute-start.32) | collective-permute-done | bytes 196640 | tf_op jit(solution)/shard_map/ppermute | solution.py:77
  (86 shorter events, 28.9 us)
Async XLA Ops:
  5.3 17.4 %collective-permute-start.7 = (bf16[3,8,64,128]{3,2,1,0:T(8,128)(2,1)S(1)}, bf16[3,8,64,128]{3,2,1,0:T(8,128)(2,1)S(1)}, u32[]{:S(2)}, u32[]{:S(2)}) collective-permute-start(bf16[3,8,64,128]{3,2,1,0:T(8,128)(2,1)S(1)} %get-tuple-element.24.own_ref), channel_id=1, source_target_pairs={{0,1},{1,0},{2,3},{3,2},{4,5},{5,4},{6,7},{7,6},{8,9},{9,8},{10,11... | collective-permute-start | bytes 1179656 | tf_op jit(solution)/shard_map/ppermute | solution.py:77
  5.3 16.8 %collective-permute-start.8 = (bf16[3,8,32,128]{3,2,1,0:T(8,128)(2,1)S(1)}, bf16[3,8,32,128]{3,2,1,0:T(8,128)(2,1)S(1)}, u32[]{:S(2)}, u32[]{:S(2)}) collective-permute-start(bf16[3,8,32,128]{3,2,1,0:T(8,128)(2,1)S(1)} %bitcast.17), channel_id=1, source_target_pairs={{0,1},{1,0},{2,3},{3,2},{4,5},{5,4},{6,7},{7,6},{8,9},{9,8},{10,11... | collective-permute-start | bytes 589832 | tf_op jit(solution)/shard_map/ppermute | solution.py:77
  8.0 14.2 %collective-permute-start.3 = (bf16[3,8,32,128]{3,2,1,0:T(8,128)(2,1)S(1)}, bf16[3,8,32,128]{3,2,1,0:T(8,128)(2,1)S(1)}, u32[]{:S(2)}, u32[]{:S(2)}) collective-permute-start(bf16[3,8,32,128]{3,2,1,0:T(8,128)(2,1)S(1)} %get-tuple-element.22.w), channel_id=1, source_target_pairs={{0,4},{2,6},{4,0},{6,2},{8,12},{10,14},{12,8},{14,10},{16,20},{18,... | collective-permute-start | bytes 589832 | tf_op jit(solution)/shard_map/ppermute | solution.py:77
  9.5 18.6 %collective-permute-start.1 = (bf16[3,8,64,128]{3,2,1,0:T(8,128)(2,1)S(1)}, bf16[3,8,64,128]{3,2,1,0:T(8,128)(2,1)S(1)}, u32[]{:S(2)}, u32[]{:S(2)}) collective-permute-start(bf16[3,8,64,128]{3,2,1,0:T(8,128)(2,1)S(1)} %get-tuple-element.24.own_ref), channel_id=1, source_target_pairs={{0,2},{2,0},{4,6},{6,4},{8,10},{10,8},{12,14},{14,12},{16,18},{18,... | collective-permute-start | bytes 1179656 | tf_op jit(solution)/shard_map/ppermute | solution.py:77
  10.4 14.1 %collective-permute-start.4 = (bf16[1,3,8,32,128]{4,3,2,1,0:T(8,128)(2,1)S(1)}, bf16[1,3,8,32,128]{4,3,2,1,0:T(8,128)(2,1)S(1)}, u32[]{:S(2)}, u32[]{:S(2)}) collective-permute-start(bf16[1,3,8,32,128]{4,3,2,1,0:T(8,128)(2,1)S(1)} %bitcast.12), channel_id=1, source_target_pairs={{0,4},{2,6},{4,0},{6,2},{8,12},{10,14},{12,8},{14,10},{16,20},{18,... | collective-permute-start | bytes 589832 | tf_op jit(solution)/shard_map/ppermute | solution.py:77
  24.5 9.3 %collective-permute-start.15 = (bf16[3,8,32,128]{3,2,1,0:T(8,128)(2,1)S(1)}, bf16[3,8,32,128]{3,2,1,0:T(8,128)(2,1)S(1)}, u32[]{:S(2)}, u32[]{:S(2)}) collective-permute-start(bf16[3,8,32,128]{3,2,1,0:T(8,128)(2,1)S(1)} %get-tuple-element.28.w), channel_id=1, source_target_pairs={{0,4},{2,6},{4,0},{6,2},{8,12},{10,14},{12,8},{14,10},{16,20},{18,... | collective-permute-start | bytes 589832 | tf_op jit(solution)/shard_map/ppermute | solution.py:77
  28.0 9.1 %collective-permute-start.16 = (bf16[1,3,8,32,128]{4,3,2,1,0:T(8,128)(2,1)S(1)}, bf16[1,3,8,32,128]{4,3,2,1,0:T(8,128)(2,1)S(1)}, u32[]{:S(2)}, u32[]{:S(2)}) collective-permute-start(bf16[1,3,8,32,128]{4,3,2,1,0:T(8,128)(2,1)S(1)} %bitcast.8), channel_id=1, source_target_pairs={{0,4},{2,6},{4,0},{6,2},{8,12},{10,14},{12,8},{14,10},{16,20},{18,... | collective-permute-start | bytes 589832 | tf_op jit(solution)/shard_map/ppermute | solution.py:77
  28.1 9.6 %collective-permute-start.6 = (bf16[1,3,8,32,128]{4,3,2,1,0:T(8,128)(2,1)S(1)}, bf16[1,3,8,32,128]{4,3,2,1,0:T(8,128)(2,1)S(1)}, u32[]{:S(2)}, u32[]{:S(2)}) collective-permute-start(bf16[1,3,8,32,128]{4,3,2,1,0:T(8,128)(2,1)S(1)} %collective-permute-done.4.xg), channel_id=1, source_target_pairs={{0,2},{2,0},{4,6},{6,4},{8,10},{10,8},{12,14},{14,12},{16,18},{18,... | collective-permute-start | bytes 589832 | tf_op jit(solution)/shard_map/ppermute | solution.py:77
  38.4 21.0 %collective-permute-start.14 = (bf16[1,3,8,32,128]{4,3,2,1,0:T(8,128)(2,1)S(1)}, bf16[1,3,8,32,128]{4,3,2,1,0:T(8,128)(2,1)}, u32[]{:S(2)}, u32[]{:S(2)}) collective-permute-start(bf16[1,3,8,32,128]{4,3,2,1,0:T(8,128)(2,1)S(1)} %bitcast.9), channel_id=1, source_target_pairs={{0,2},{2,0},{4,6},{6,4},{8,10},{10,8},{12,14},{14,12},{16,18},{18,... | collective-permute-start | bytes 589832 | tf_op jit(solution)/shard_map/ppermute | solution.py:77
  39.6 20.9 %collective-permute-start.17 = (bf16[3,8,32,128]{3,2,1,0:T(8,128)(2,1)S(1)}, bf16[3,8,32,128]{3,2,1,0:T(8,128)(2,1)}, u32[]{:S(2)}, u32[]{:S(2)}) collective-permute-start(bf16[3,8,32,128]{3,2,1,0:T(8,128)(2,1)S(1)} %collective-permute-done.15.x), channel_id=1, source_target_pairs={{0,2},{2,0},{4,6},{6,4},{8,10},{10,8},{12,14},{14,12},{16,18},{18,... | collective-permute-start | bytes 589832 | tf_op jit(solution)/shard_map/ppermute | solution.py:77
  41.8 18.8 %collective-permute-start.18 = (bf16[1,3,8,32,128]{4,3,2,1,0:T(8,128)(2,1)S(1)}, bf16[1,3,8,32,128]{4,3,2,1,0:T(8,128)(2,1)}, u32[]{:S(2)}, u32[]{:S(2)}) collective-permute-start(bf16[1,3,8,32,128]{4,3,2,1,0:T(8,128)(2,1)S(1)} %collective-permute-done.16.xg), channel_id=1, source_target_pairs={{0,2},{2,0},{4,6},{6,4},{8,10},{10,8},{12,14},{14,12},{16,18},{18,... | collective-permute-start | bytes 589832 | tf_op jit(solution)/shard_map/ppermute | solution.py:77
  45.5 18.1 %collective-permute-start.21 = (bf16[3,8,32,128]{3,2,1,0:T(8,128)(2,1)}, bf16[3,8,32,128]{3,2,1,0:T(8,128)(2,1)}, u32[]{:S(2)}, u32[]{:S(2)}) collective-permute-start(bf16[3,8,32,128]{3,2,1,0:T(8,128)(2,1)} %collective-permute-done.19.z), channel_id=1, source_target_pairs={{0,2},{2,0},{4,6},{6,4},{8,10},{10,8},{12,14},{14,12},{16,18},{18,... | collective-permute-start | bytes 589832 | tf_op jit(solution)/shard_map/ppermute | solution.py:77
  46.2 17.4 %collective-permute-start.22 = (bf16[1,3,8,32,128]{4,3,2,1,0:T(8,128)(2,1)}, bf16[1,3,8,32,128]{4,3,2,1,0:T(8,128)(2,1)}, u32[]{:S(2)}, u32[]{:S(2)}) collective-permute-start(bf16[1,3,8,32,128]{4,3,2,1,0:T(8,128)(2,1)} %collective-permute-done.20.zg), channel_id=1, source_target_pairs={{0,2},{2,0},{4,6},{6,4},{8,10},{10,8},{12,14},{14,12},{16,18},{18,... | collective-permute-start | bytes 589832 | tf_op jit(solution)/shard_map/ppermute | solution.py:77
  59.4 12.0 %collective-permute-start.23 = (bf16[3,16,32,128]{3,2,1,0:T(8,128)(2,1)S(1)}, bf16[3,16,32,128]{3,2,1,0:T(8,128)(2,1)S(1)}, u32[]{:S(2)}, u32[]{:S(2)}) collective-permute-start(bf16[3,16,32,128]{3,2,1,0:T(8,128)(2,1)S(1)} %get-tuple-element.26.w), channel_id=1, source_target_pairs={{0,4},{2,6},{4,0},{6,2},{8,12},{10,14},{12,8},{14,10},{16,20},{18,... | collective-permute-start | bytes 1179656 | tf_op jit(solution)/shard_map/ppermute | solution.py:77
  66.7 12.2 %collective-permute-start.28 = (bf16[3,16,32,128]{3,2,1,0:T(8,128)(2,1)S(1)}, bf16[3,16,32,128]{3,2,1,0:T(8,128)(2,1)S(1)}, u32[]{:S(2)}, u32[]{:S(2)}) collective-permute-start(bf16[3,16,32,128]{3,2,1,0:T(8,128)(2,1)S(1)} %get-tuple-element.30.w), channel_id=1, source_target_pairs={{0,4},{2,6},{4,0},{6,2},{8,12},{10,14},{12,8},{14,10},{16,20},{18,... | collective-permute-start | bytes 1179656 | tf_op jit(solution)/shard_map/ppermute | solution.py:77
  71.4 11.5 %collective-permute-start.25 = (bf16[3,16,32,128]{3,2,1,0:T(8,128)(2,1)S(1)}, bf16[3,16,32,128]{3,2,1,0:T(8,128)(2,1)S(1)}, u32[]{:S(2)}, u32[]{:S(2)}) collective-permute-start(bf16[3,16,32,128]{3,2,1,0:T(8,128)(2,1)S(1)} %collective-permute-done.23.x), channel_id=1, source_target_pairs={{0,8},{2,10},{4,28},{6,30},{8,16},{10,18},{12,4},{14,6},{16,24},{1... | collective-permute-start | bytes 1179656 | tf_op jit(solution)/shard_map/ppermute | solution.py:77
  71.4 12.1 %collective-permute-start.13 = (bf16[3,16,32,128]{3,2,1,0:T(8,128)(2,1)S(1)}, bf16[3,16,32,128]{3,2,1,0:T(8,128)(2,1)S(1)}, u32[]{:S(2)}, u32[]{:S(2)}) collective-permute-start(bf16[3,16,32,128]{3,2,1,0:T(8,128)(2,1)S(1)} %get-tuple-element.26.w), channel_id=1, source_target_pairs={{0,2},{2,0},{4,6},{6,4},{8,10},{10,8},{12,14},{14,12},{16,18},{18,... | collective-permute-start | bytes 1179656 | tf_op jit(solution)/shard_map/ppermute | solution.py:77
  78.9 12.5 %collective-permute-start.30 = (bf16[3,16,32,128]{3,2,1,0:T(8,128)(2,1)S(1)}, bf16[3,16,32,128]{3,2,1,0:T(8,128)(2,1)S(1)}, u32[]{:S(2)}, u32[]{:S(2)}) collective-permute-start(bf16[3,16,32,128]{3,2,1,0:T(8,128)(2,1)S(1)} %collective-permute-done.28.x), channel_id=1, source_target_pairs={{0,8},{2,10},{4,28},{6,30},{8,16},{10,18},{12,4},{14,6},{16,24},{1... | collective-permute-start | bytes 1179656 | tf_op jit(solution)/shard_map/ppermute | solution.py:77
  78.9 16.4 %collective-permute-start.24 = (bf16[3,16,32,128]{3,2,1,0:T(8,128)(2,1)S(1)}, bf16[3,16,32,128]{3,2,1,0:T(8,128)(2,1)S(1)}, u32[]{:S(2)}, u32[]{:S(2)}) collective-permute-start(bf16[3,16,32,128]{3,2,1,0:T(8,128)(2,1)S(1)} %collective-permute-done.23.x), channel_id=1, source_target_pairs={{0,2},{2,0},{4,6},{6,4},{8,10},{10,8},{12,14},{14,12},{16,18},{18,... | collective-permute-start | bytes 1179656 | tf_op jit(solution)/shard_map/ppermute | solution.py:77
  83.0 14.8 %collective-permute-start.26 = (bf16[3,16,32,128]{3,2,1,0:T(8,128)(2,1)S(1)}, bf16[3,16,32,128]{3,2,1,0:T(8,128)(2,1)S(1)}, u32[]{:S(2)}, u32[]{:S(2)}) collective-permute-start(bf16[3,16,32,128]{3,2,1,0:T(8,128)(2,1)S(1)} %collective-permute-done.25.z), channel_id=1, source_target_pairs={{0,2},{2,0},{4,6},{6,4},{8,10},{10,8},{12,14},{14,12},{16,18},{18,... | collective-permute-start | bytes 1179656 | tf_op jit(solution)/shard_map/ppermute | solution.py:77
  83.0 18.7 %collective-permute-start.27 = (bf16[3,16,32,128]{3,2,1,0:T(8,128)(2,1)S(1)}, bf16[3,16,32,128]{3,2,1,0:T(8,128)(2,1)S(1)}, u32[]{:S(2)}, u32[]{:S(2)}) collective-permute-start(bf16[3,16,32,128]{3,2,1,0:T(8,128)(2,1)S(1)} %get-tuple-element.30.w), channel_id=1, source_target_pairs={{0,2},{2,0},{4,6},{6,4},{8,10},{10,8},{12,14},{14,12},{16,18},{18,... | collective-permute-start | bytes 1179656 | tf_op jit(solution)/shard_map/ppermute | solution.py:77
  83.5 21.9 %collective-permute-start.29 = (bf16[3,16,32,128]{3,2,1,0:T(8,128)(2,1)S(1)}, bf16[3,16,32,128]{3,2,1,0:T(8,128)(2,1)S(1)}, u32[]{:S(2)}, u32[]{:S(2)}) collective-permute-start(bf16[3,16,32,128]{3,2,1,0:T(8,128)(2,1)S(1)} %collective-permute-done.28.x), channel_id=1, source_target_pairs={{0,2},{2,0},{4,6},{6,4},{8,10},{10,8},{12,14},{14,12},{16,18},{18,... | collective-permute-start | bytes 1179656 | tf_op jit(solution)/shard_map/ppermute | solution.py:77
  91.4 16.5 %collective-permute-start.31 = (bf16[3,16,32,128]{3,2,1,0:T(8,128)(2,1)S(1)}, bf16[3,16,32,128]{3,2,1,0:T(8,128)(2,1)S(1)}, u32[]{:S(2)}, u32[]{:S(2)}) collective-permute-start(bf16[3,16,32,128]{3,2,1,0:T(8,128)(2,1)S(1)} %collective-permute-done.30.z), channel_id=1, source_target_pairs={{0,2},{2,0},{4,6},{6,4},{8,10},{10,8},{12,14},{14,12},{16,18},{18,... | collective-permute-start | bytes 1179656 | tf_op jit(solution)/shard_map/ppermute | solution.py:77
  113.3 10.0 %collective-permute-start.32 = (bf16[3,8,32,128]{3,2,1,0:T(8,128)(2,1)S(1)}, bf16[3,8,32,128]{3,2,1,0:T(8,128)(2,1)S(1)}, u32[]{:S(2)}, u32[]{:S(2)}) collective-permute-start(bf16[3,8,32,128]{3,2,1,0:T(8,128)(2,1)S(1)} %bitcast.20), channel_id=1, source_target_pairs={{0,1},{1,0},{2,3},{3,2},{4,5},{5,4},{6,7},{7,6},{8,9},{9,8},{10,11... | collective-permute-start | bytes 589832 | tf_op jit(solution)/shard_map/ppermute | solution.py:77
  (23 other events, 96.7 us)

commit v4 on v3

v4 whole, which is shorter than its diff:
```python
import jax
import jax.numpy as jnp
from jax import lax
from jax.experimental import pallas as pl
from jax.experimental.pallas import tpu as pltpu
from jax.sharding import PartitionSpec as P

REACH = 2
BAND = 2 * REACH + 1
WIDE = 4 * REACH + 1
VMEM = pl.BlockSpec(memory_space=pltpu.VMEM)
SMEM = pl.BlockSpec(memory_space=pltpu.SMEM)
PARAMS = pltpu.CompilerParams(vmem_limit_bytes=16 * 1024 * 1024)


def call(kernel, ins, outs, scratch=(), aliases=None, resident=True, us=3):
    specs = [SMEM if x.dtype == jnp.int32 else VMEM for x in ins]
    if resident:
        outs = [pltpu.VMEM(x.shape, x.dtype) for x in outs]
    ins = [
        x if x.dtype == jnp.int32 else pltpu.with_memory_space_constraint(x, pltpu.VMEM)
        for x in ins
    ]
    return pl.pallas_call(
        kernel,
        out_shape=tuple(outs),
        in_specs=specs,
        out_specs=tuple(VMEM for _ in outs),
        scratch_shapes=list(scratch),
        input_output_aliases=aliases or {},
        compiler_params=PARAMS,
    )(*ins)


def after(x, *others):
    return lax.optimization_barrier((x, *others))[0]


def offsets(j):
    first = j < 2
    return {
        "own": 0,
        "x": jnp.where(first, 2, -2),
        "core": jnp.where(j % 2 == 0, 1, -1),
        "core_x": jnp.where(first, 1, -1),
        "z": jnp.where(first, -2, 2),
        "core_z": jnp.where(first, -1, 1),
    }


def per_device(p_blocks, col_lists, fill_lists):
    rb, slots, bs, _ = p_blocks.shape
    nb = col_lists.shape[0]
    fill = fill_lists.shape[1]
    n_rows = lax.axis_size("rows")
    n = lax.axis_size("inner")
    part = bs // n
    cuts = 2 if part % 32 == 0 else 1
    cols = part // cuts
    width = rb * bs
    bf16, f32 = jnp.bfloat16, jnp.float32
    shape = jax.ShapeDtypeStruct
    chunks = range(cuts)

    def shift(m):
        return [(i, (i + m) % n) for i in range(n)]

    def along(r):
        group, j = divmod(r, 4)
        return (group + (1 if j < 2 else -1)) % (n_rows // 4) * 4 + j

    flip_x = [(r, r ^ 2) for r in range(n_rows)]
    flip_core = [(r, r ^ 1) for r in range(n_rows)]
    move_z = [(r, along(r)) for r in range(n_rows)]

    def send(x, pairs, axis="rows"):
        return lax.ppermute(x, axis, pairs)

    def rows_at(index, size):
        return pl.ds(pl.multiple_of(index * size, size), size)

    def wrapped(x):
        return jnp.where(x < 0, x + nb, jnp.where(x >= nb, x - nb, x))

    def received(parts):
        return parts[0][None] if n == 2 else jnp.stack(parts)

    def nth(x, m):
        return x.reshape(x.shape[1:]) if n == 2 else x[m]

    def exchange(x):
        return received([send(nth(x, m - 1), shift(m), "inner") for m in range(1, n)])

    def pack(p_ref, mine_ref, *refs):
        rest_refs, turned = refs[:cuts], refs[-1]
        q = lax.axis_index("inner")
        for i in range(rb):
            for s in range(slots):
                turned[i, s] = p_ref[i, s].T
                mine_ref[i, s] = turned[i, s, rows_at(q, part), :]
                for c in chunks:
                    for m in range(1, n):
                        to = lax.rem(q + m, n)
                        rest_refs[c][m - 1, i, s] = turned[i, s, rows_at(to * cuts + c, cols), :]

    packed = call(
        pack,
        [p_blocks],
        [shape((rb, slots, part, bs), bf16)]
        + [shape((n - 1, rb, slots, cols, bs), bf16)] * cuts,
        [pltpu.VMEM((rb, slots, bs, bs), bf16)],
        us=1,
    )
    mine, rest = packed[0], packed[1:]
    lists = jnp.concatenate([col_lists.T, fill_lists.T], axis=1)

    def add(ref, where, lanes, value):
        ref[where, lanes] = (ref[where, lanes].astype(f32) + value.astype(f32)).astype(bf16)

    def column(lists_ref, i, slot):
        o = lax.axis_index("rows")
        return wrapped(lists_ref[slot, o * rb + i] - rb * (o - REACH))

    def start_rows(lists_ref, mine_ref, *refs):
        out_refs = refs[:cuts]
        q = lax.axis_index("inner")
        for c in chunks:
            out_refs[c][...] = jnp.zeros(out_refs[c].shape, bf16)
        for s in range(slots):
            for i in range(rb):
                at = column(lists_ref, i, q * slots + s)
                for c in chunks:
                    value = mine_ref[i, s, pl.ds(c * cols, cols), :]
                    add(out_refs[c], rows_at(at, cols), pl.ds(i * bs, bs), value)

    def start_band(lists_ref, *refs):
        rest_refs, out_ref = refs[:cuts], refs[-1]
        q = lax.axis_index("inner")
        out_ref[...] = jnp.zeros(out_ref.shape, bf16)
        for s in range(slots):
            for i in range(rb):
                at = column(lists_ref, i, q * slots + s) * n + lax.rem(q + 1, n)
                for c in chunks:
                    value = rest_refs[c][0, i, s]
                    add(out_ref, rows_at(at * cuts + c, cols), pl.ds(i * bs, bs), value)

    def end_rows(lists_ref, in_ref, got_ref, out_ref):
        q = lax.axis_index("inner")
        for s in range(slots):
            for i in range(rb):
                for m in range(1, n):
                    at = column(lists_ref, i, lax.rem(q - m + n, n) * slots + s)
                    add(out_ref, rows_at(at, cols), pl.ds(i * bs, bs), got_ref[m - 1, i, s])

    def end_band(lists_ref, in_ref, left_ref, *refs):
        dense_refs, out_ref = refs[:cuts], refs[-1]
        q = lax.axis_index("inner")
        other = lax.rem(q + 1, n)
        for s in range(slots):
            for i in range(rb):
                at = column(lists_ref, i, other * slots + s) * n + other
                add(out_ref, rows_at(at, part), pl.ds(i * bs, bs), left_ref[i, s])
        for k in range(BAND * rb):
            for c in chunks:
                out_ref[rows_at((k * n + q) * cuts + c, cols), :] = dense_refs[c][pl.ds(k * cols, cols), :]

    def whole_band(lists_ref, left_ref, out_ref):
        out_ref[...] = jnp.zeros(out_ref.shape, bf16)
        for g in range(n):
            for s in range(slots):
                for i in range(rb):
                    at = column(lists_ref, i, g * slots + s)
                    add(out_ref, rows_at(at, bs), pl.ds(i * bs, bs), left_ref[g, i, s].T)

    span = BAND * rb * cols
    wide = WIDE * rb * cols
    acc_shape = shape((wide, width), f32)
    rows_shape = shape((span, width), bf16)
    band_shape = shape((BAND * width, width), bf16)
    own = call(start_rows, [lists, mine], [rows_shape] * cuts, us=1)
    got = [exchange(x) for x in rest]
    if n == 2:
        (band,) = call(start_band, [lists, *rest], [band_shape], us=1)
        left = send(after(mine, got[0]), shift(1), "inner")
    else:
        left = lax.all_gather(p_blocks, "inner", axis=0)
    own = [
        call(end_rows, [lists, own[c], got[c]], [rows_shape], aliases={1: 0}, us=1)[0]
        for c in chunks
    ]
    if n == 2:
        (band,) = call(end_band, [lists, band, left, *own], [band_shape], aliases={1: 0}, us=2)
    else:
        (band,) = call(whole_band, [lists, left], [band_shape], us=2)

    def moved(v):
        x = send(v, flip_x)
        return x, send(x, move_z)

    def weights(left_ref, d):
        return left_ref[rows_at(d + REACH, width), :]

    def square_term(d, rows_ref, left_ref, acc_ref):
        term = jnp.dot(rows_ref[...], weights(left_ref, d), preferred_element_type=f32)
        where = pl.ds(pl.multiple_of((d + REACH) * rb * cols, rb * cols), span)
        acc_ref[where, :] += term

    def square_near(w, u, x, cx, left_ref, acc_ref):
        j = lax.rem(lax.axis_index("rows"), 4)
        d = offsets(j)
        edge = REACH * rb * cols
        acc_ref[:edge, :] = jnp.zeros((edge, width), f32)
        acc_ref[edge : edge + span, :] = jnp.dot(
            w[...], left_ref[REACH * width : (REACH + 1) * width, :], preferred_element_type=f32
        )
        acc_ref[edge + span :, :] = jnp.zeros((edge, width), f32)
        square_term(d["core"], u, left_ref, acc_ref)
        square_term(d["x"], x, left_ref, acc_ref)

        @pl.when((j == 1) | (j == 2))
        def _():
            square_term(d["core_x"], cx, left_ref, acc_ref)

    def square_far(lists_ref, acc_in, z, cz, left_ref, acc_ref, sq_ref, low_ref):
        j = lax.rem(lax.axis_index("rows"), 4)
        d = offsets(j)
        square_term(d["z"], z, left_ref, acc_ref)

        @pl.when((j == 0) | (j == 3))
        def _():
            square_term(d["core_z"], cz, left_ref, acc_ref)

        for v in range(fill):
            for i in range(rb):
                value = acc_ref[kept(lists_ref, i, v), pl.ds(i * bs, bs)]
                sq_ref[i, v] = value
                low_ref[i, v] = value.astype(bf16)

    kept_shape = (rb, fill, cols, bs)

    def square(w, x, z, lead):
        u, cx = send(w, flip_core), send(x, flip_core)
        (acc,) = call(square_near, [after(w, *lead), u, x, cx, band], [acc_shape], us=2)
        z = after(z, acc)
        return call(
            square_far,
            [lists, acc, z, send(z, flip_core), band],
            [acc_shape, shape(kept_shape, f32), shape(kept_shape, bf16)],
            aliases={1: 0},
            us=2,
        )[1:]

    def kept(lists_ref, i, v):
        o = lax.axis_index("rows")
        return rows_at(wrapped(lists_ref[v, nb + o * rb + i] - rb * (o - 2 * REACH)), cols)

    def cube_term(lists_ref, d, reach, low_ref, left_ref, dense, acc_ref, first=False):
        o = lax.axis_index("rows")
        source = lax.rem(o + d + n_rows, n_rows)
        blocks = (WIDE - reach) * rb
        start = jnp.maximum(d, 0) * rb
        rows = blocks * cols
        dense[:rows, :] = jnp.zeros((rows, width), bf16)
        for v in range(fill):
            for k in range(rb):
                c = wrapped(lists_ref[v, nb + source * rb + k] - rb * (o - 2 * REACH)) - start
                c = jnp.where((c >= 0) & (c < blocks), c, blocks)
                dense[rows_at(c, cols), pl.ds(k * bs, bs)] = low_ref[k, v]

        term = jnp.dot(dense[:rows, :], weights(left_ref, d), preferred_element_type=f32)
        if first:
            acc_ref[...] = term
        else:
            acc_ref[pl.ds(pl.multiple_of(start * cols, rb * cols), rows), :] += term

    def cube_own(lists_ref, w, u, left_ref, acc_ref, dense):
        d = offsets(lax.rem(lax.axis_index("rows"), 4))
        cube_term(lists_ref, 0, 0, w, left_ref, dense, acc_ref, first=True)
        cube_term(lists_ref, d["core"], 1, u, left_ref, dense, acc_ref)

    def cube_near(lists_ref, acc_in, x, cx, left_ref, acc_ref, dense):
        j = lax.rem(lax.axis_index("rows"), 4)
        d = offsets(j)
        cube_term(lists_ref, d["x"], 2, x, left_ref, dense, acc_ref)

        @pl.when((j == 1) | (j == 2))
        def _():
            cube_term(lists_ref, d["core_x"], 1, cx, left_ref, dense, acc_ref)

    def cube_far(lists_ref, acc_in, z, cz, left_ref, sq_ref, acc_ref, keep_ref, give_ref, dense):
        q = lax.axis_index("inner")
        j = lax.rem(lax.axis_index("rows"), 4)
        d = offsets(j)
        cube_term(lists_ref, d["z"], 2, z, left_ref, dense, acc_ref)

        @pl.when((j == 0) | (j == 3))
        def _():
            cube_term(lists_ref, d["core_z"], 1, cz, left_ref, dense, acc_ref)

        def result(i, v):
            return 3.0 * sq_ref[i, v] - 2.0 * acc_ref[kept(lists_ref, i, v), pl.ds(i * bs, bs)]

        for s in range(slots):
            for i in range(rb):
                keep_ref[i, s] = result(i, q * slots + s)
                for m in range(1, n):
                    give_ref[m - 1, i, s] = result(i, lax.rem(q + m, n) * slots + s).astype(bf16)

    dense = [pltpu.VMEM((wide + cols, width), bf16)]
    x, z, sq, low, x2, z2 = [], [], [], [], [], []
    for c in chunks:
        x_c, z_c = moved(own[c])
        one = square(own[c], x_c, z_c, low)
        sq.append(one[0])
        low.append(one[1])
    keep, give, near = [], [], []
    for c in chunks:
        x_c = send(low[c], flip_x)
        u = send(low[c], flip_core)
        (acc,) = call(
            cube_own, [lists, low[c], u, after(band, low[-1], *near)], [acc_shape], dense, us=3
        )
        x2.append(x_c)
        z2.append(send(x_c, move_z))
        cx = send(x_c, flip_core)
        (acc,) = call(cube_near, [lists, acc, x_c, cx, band], [acc_shape], dense, aliases={1: 0}, us=2)
        near.append(acc)
    for c in chunks:
        z_c = after(z2[c], near[c], *give)
        one = call(
            cube_far,
            [lists, near[c], z_c, send(z_c, flip_core), band, sq[c]],
            [acc_shape, shape((rb, slots, cols, bs), f32), shape((n - 1, rb, slots, cols, bs), bf16)],
            dense,
            aliases={1: 0},
            us=3,
        )[1:]
        keep.append(one[0])
        give.append(one[1])
    taken = [exchange(v) for v in give]

    def join(*refs):
        keep_refs, taken_refs, out_ref, turned = refs[:cuts], refs[cuts : 2 * cuts], refs[-2], refs[-1]
        q = lax.axis_index("inner")
        for i in range(rb):
            for s in range(slots):
                for c in chunks:
                    turned[i, s, rows_at(q * cuts + c, cols), :] = keep_refs[c][i, s]
                    for m in range(1, n):
                        at = lax.rem(q - m + n, n) * cuts + c
                        turned[i, s, rows_at(at, cols), :] = taken_refs[c][m - 1, i, s].astype(f32)
                out_ref[i, s] = turned[i, s].T

    (out,) = call(
        join,
        [*keep, *taken],
        [shape((rb, slots, bs, bs), f32)],
        [pltpu.VMEM((rb, slots, bs, bs), f32)],
        resident=False,
    )
    return out


def solution(mesh):
    in_specs = (P("rows", "inner", None, None), P(), P())
    out_specs = P("rows", "inner", None, None)
    return jax.shard_map(
        per_device, mesh=mesh, in_specs=in_specs, out_specs=out_specs, check_vma=False
    )
```

time: 126 us -> 91.8 us (0.73)
  Pallas kernels: 38.5 us -> 23.7 us
  waiting for transfers between devices: 58.1 us -> 45.8 us
  local copies, waits for them, and re-layouts: 7.15 us -> 1.13 us
    pallas_call x14 -> x17, Pallas kernels: 38.5 us -> 23.7 us  [call(): pl.pallas_call(kernel, out_shape=tuple(outs), in_specs=specs, out_specs=t...]
    ppermute x34 -> x25, waiting for transfers between devices: 58.1 us -> 45.8 us  [send(): return lax.ppermute(x, axis, pairs)]
    unnamed x26 -> x2, local copies, waits for them, and re-layouts: 7.06 us -> 1.13 us
    ppermute x34 -> x25, starting transfers between devices: 20.5 us -> 19.9 us  [send(): return lax.ppermute(x, axis, pairs)]
  transfers between devices with their start and end apart: 34 -> 25, of which waited for: 13 -> 12; matrix products, arithmetic and copies ran while one was open for 1% -> 1% of each run, Pallas kernels for 26% -> 22%
where the time goes in v4:
time: 91.8 us; the launch traced here: 91.6 us
  waiting for transfers between devices  45.8 us (50%)
  Pallas kernels  23.7 us (26%)
  starting transfers between devices  19.9 us (22%)
  local copies, waits for them, and re-layouts  1.13 us (1%)
    ppermute x25, waiting for transfers between devices, send(): return lax.ppermute(x, axis, pairs)  45.8 us
    pallas_call x17, Pallas kernels, call(): pl.pallas_call(kernel, out_shape=tuple(outs), in_specs=specs, out_specs=t...  23.7 us
    ppermute x25, starting transfers between devices, send(): return lax.ppermute(x, axis, pairs)  19.9 us
  transfers between devices with their start and end apart: 25, of which 12 were waited for; matrix products, arithmetic and copies ran while one was open for 1% of the time, Pallas kernels for 22%

profile of v4, /device:TPU:0, one launch (start us, length us, event | category | flops | bytes accessed | tf_op | source)
XLA Modules:
  0.0 91.6 jit_solution(2008558846220305170)
XLA Ops:
  1.6 3.0 %collective-permute-start = (bf16[3,8,32,128]{3,2,1,0:T(8,128)(2,1)S(1)}, bf16[3,8,32,128]{3,2,1,0:T(8,128)(2,1)S(1)}, u32[]{:S(2)}, u32[]{:S(2)}) collective-permute-start(bf16[3,8,32,128]{3,2,1,0:T(8,128)(2,1)S(1)} %bitcast.10), channel_id=1, source_target_pairs={{0,1},{1,0},{2,3},{3,2},{4,5},{5,4},{6,7},{7,6},{8,9},{9,8},{10,11... | collective-permute-start | bytes 589832 | tf_op jit(solution)/shard_map/ppermute | solution.py:77
  6.3 3.2 %collective-permute-done = bf16[3,8,32,128]{3,2,1,0:T(8,128)(2,1)S(1)} collective-permute-done((bf16[3,8,32,128]{3,2,1,0:T(8,128)(2,1)S(1)}, bf16[3,8,32,128]{3,2,1,0:T(8,128)(2,1)S(1)}, u32[]{:S(2)}, u32[]{:S(2)}) %collective-permute-start) | collective-permute-done | bytes 196640 | tf_op jit(solution)/shard_map/ppermute | solution.py:77
  10.4 1.8 %collective-permute-start.2 = (bf16[480,384]{1,0:T(8,128)(2,1)S(1)}, bf16[480,384]{1,0:T(8,128)(2,1)S(1)}, u32[]{:S(2)}, u32[]{:S(2)}) collective-permute-start(bf16[480,384]{1,0:T(8,128)(2,1)S(1)} %shard_map.39.refs_0_.w), channel_id=1, source_target_pairs={{0,4},{2,6},{4,0},{6,2},{8,12},{10,14},{12,8},{14,10},{16,20},{18,... | collective-permute-start | bytes 1105928 | tf_op jit(solution)/shard_map/ppermute | solution.py:77
  12.2 1.5 %collective-permute-start.5 = (bf16[3,8,32,128]{3,2,1,0:T(8,128)(2,1)S(1)}, bf16[3,8,32,128]{3,2,1,0:T(8,128)(2,1)S(1)}, u32[]{:S(2)}, u32[]{:S(2)}) collective-permute-start(bf16[3,8,32,128]{3,2,1,0:T(8,128)(2,1)S(1)} %bitcast.11), channel_id=1, source_target_pairs={{0,1},{1,0},{2,3},{3,2},{4,5},{5,4},{6,7},{7,6},{8,9},{9,8},{10,11... | collective-permute-start | bytes 589832 | tf_op jit(solution)/shard_map/ppermute | solution.py:77
  14.2 6.0 %collective-permute-done.2.x = bf16[480,384]{1,0:T(8,128)(2,1)S(1)} collective-permute-done((bf16[480,384]{1,0:T(8,128)(2,1)S(1)}, bf16[480,384]{1,0:T(8,128)(2,1)S(1)}, u32[]{:S(2)}, u32[]{:S(2)}) %collective-permute-start.2) | collective-permute-done | bytes 368672 | tf_op jit(solution)/shard_map/ppermute | solution.py:77
  20.2 1.5 %collective-permute-start.6 = (bf16[480,384]{1,0:T(8,128)(2,1)S(1)}, bf16[480,384]{1,0:T(8,128)(2,1)S(1)}, u32[]{:S(2)}, u32[]{:S(2)}) collective-permute-start(bf16[480,384]{1,0:T(8,128)(2,1)S(1)} %collective-permute-done.2.x), channel_id=1, source_target_pairs={{0,8},{2,10},{4,28},{6,30},{8,16},{10,18},{12,4},{14,6},{16,24},{1... | collective-permute-start | bytes 1105928 | tf_op jit(solution)/shard_map/ppermute | solution.py:77
  22.6 3.6 %collective-permute-start.10 = (bf16[480,384]{1,0:T(8,128)(2,1)S(1)}, bf16[480,384]{1,0:T(8,128)(2,1)S(1)}, u32[]{:S(2)}, u32[]{:S(2)}) collective-permute-start(bf16[480,384]{1,0:T(8,128)(2,1)S(1)} %shard_map.41.refs_1_.w), channel_id=1, source_target_pairs={{0,4},{2,6},{4,0},{6,2},{8,12},{10,14},{12,8},{14,10},{16,20},{18,... | collective-permute-start | bytes 1105928 | tf_op jit(solution)/shard_map/ppermute | solution.py:77
  29.1 3.9 %collective-permute-done.6.z = bf16[480,384]{1,0:T(8,128)(2,1)S(1)} collective-permute-done((bf16[480,384]{1,0:T(8,128)(2,1)S(1)}, bf16[480,384]{1,0:T(8,128)(2,1)S(1)}, u32[]{:S(2)}, u32[]{:S(2)}) %collective-permute-start.6) | collective-permute-done | bytes 368672 | tf_op jit(solution)/shard_map/ppermute | solution.py:77
  33.5 1.6 %collective-permute-done.10.x = bf16[480,384]{1,0:T(8,128)(2,1)S(1)} collective-permute-done((bf16[480,384]{1,0:T(8,128)(2,1)S(1)}, bf16[480,384]{1,0:T(8,128)(2,1)S(1)}, u32[]{:S(2)}, u32[]{:S(2)}) %collective-permute-start.10) | collective-permute-done | bytes 368672 | tf_op jit(solution)/shard_map/ppermute | solution.py:77
  35.1 1.6 %shard_map.44 = (f32[864,384]{1,0:T(8,128)S(1)}, f32[3,16,32,128]{3,2,1,0:T(8,128)S(1)}, bf16[3,16,32,128]{3,2,1,0:T(8,128)(2,1)S(1)}) custom-call(s32[16,96]{1,0:T(8,128)S(1)} %pad_add_fusion.lists_ref, f32[864,384]{1,0:T(8,128)S(1)} %shard_map.43.acc_in, bf16[480,384]{1,0:T(8,128)(2,1)S(1)} %collective-permute-done.6.z, ...), custom_call_target="tpu_custom_call", output_to_operand_aliasing={{0}: (1, {})} | custom-call | tf_op jit(solution)/shard_map/pallas_call | solution.py:24
  36.8 3.1 %collective-permute-start.14 = (bf16[3,16,32,128]{3,2,1,0:T(8,128)(2,1)S(1)}, bf16[3,16,32,128]{3,2,1,0:T(8,128)(2,1)S(1)}, u32[]{:S(2)}, u32[]{:S(2)}) collective-permute-start(bf16[3,16,32,128]{3,2,1,0:T(8,128)(2,1)S(1)} %get-tuple-element.33.w), channel_id=1, source_target_pairs={{0,4},{2,6},{4,0},{6,2},{8,12},{10,14},{12,8},{14,10},{16,20},{18,... | collective-permute-start | bytes 1179656 | tf_op jit(solution)/shard_map/ppermute | solution.py:77
  40.7 7.2 %collective-permute-done.12.z = bf16[480,384]{1,0:T(8,128)(2,1)S(1)} collective-permute-done((bf16[480,384]{1,0:T(8,128)(2,1)S(1)}, bf16[480,384]{1,0:T(8,128)(2,1)S(1)}, u32[]{:S(2)}, u32[]{:S(2)}) %collective-permute-start.12) | collective-permute-done | bytes 368672 | tf_op jit(solution)/shard_map/ppermute | solution.py:77
  49.6 1.6 %shard_map.46 = (f32[864,384]{1,0:T(8,128)S(1)}, f32[3,16,32,128]{3,2,1,0:T(8,128)S(1)}, bf16[3,16,32,128]{3,2,1,0:T(8,128)(2,1)S(1)}) custom-call(s32[16,96]{1,0:T(8,128)S(1)} %pad_add_fusion.lists_ref, f32[864,384]{1,0:T(8,128)S(1)} %shard_map.45.acc_in, bf16[480,384]{1,0:T(8,128)(2,1)S(1)} %collective-permute-done.12.z, ...), custom_call_target="tpu_custom_call", output_to_operand_aliasing={{0}: (1, {})} | custom-call | tf_op jit(solution)/shard_map/pallas_call | solution.py:24
  51.9 2.0 %shard_map.47.acc_in = f32[864,384]{1,0:T(8,128)S(1)} custom-call(s32[16,96]{1,0:T(8,128)S(1)} %pad_add_fusion.lists_ref, bf16[3,16,32,128]{3,2,1,0:T(8,128)(2,1)S(1)} %get-tuple-element.33.w, bf16[3,16,32,128]{3,2,1,0:T(8,128)(2,1)S(1)} %collective-permute-done.8.u, bf16[1920,384]{1,0:T(8,128)(2,1)S(1)} %shard_map.42.left_ref), custom_call_target="tpu_custom_call" | custom-call | tf_op jit(solution)/shard_map/pallas_call | solution.py:24
  53.9 8.2 %collective-permute-done.19.x = bf16[3,16,32,128]{3,2,1,0:T(8,128)(2,1)S(1)} collective-permute-done((bf16[3,16,32,128]{3,2,1,0:T(8,128)(2,1)S(1)}, bf16[3,16,32,128]{3,2,1,0:T(8,128)(2,1)S(1)}, u32[]{:S(2)}, u32[]{:S(2)}) %collective-permute-start.19) | collective-permute-done | bytes 393248 | tf_op jit(solution)/shard_map/ppermute | solution.py:77
  64.9 2.0 %shard_map.50.acc_in = f32[864,384]{1,0:T(8,128)S(1)} custom-call(s32[16,96]{1,0:T(8,128)S(1)} %pad_add_fusion.lists_ref, bf16[3,16,32,128]{3,2,1,0:T(8,128)(2,1)S(1)} %get-tuple-element.36.w, bf16[3,16,32,128]{3,2,1,0:T(8,128)(2,1)S(1)} %collective-permute-done.18.u, bf16[1920,384]{1,0:T(8,128)(2,1)S(1)} %shard_map.42.left_ref), custom_call_target="tpu_custom_call" | custom-call | tf_op jit(solution)/shard_map/pallas_call | solution.py:24
  68.3 2.4 %shard_map.49 = (f32[864,384]{1,0:T(8,128)S(1)}, f32[3,8,32,128]{3,2,1,0:T(8,128)S(1)}, bf16[1,3,8,32,128]{4,3,2,1,0:T(8,128)(2,1)S(1)}) custom-call(s32[16,96]{1,0:T(8,128)S(1)} %pad_add_fusion.lists_ref, f32[864,384]{1,0:T(8,128)S(1)} %shard_map.48.acc_in, bf16[3,16,32,128]{3,2,1,0:T(8,128)(2,1)S(1)} %collective-permute-done.16.z, ...), custom_call_target="tpu_custom_call", output_to_operand_aliasing={{0}: (1, {})} | custom-call | tf_op jit(solution)/shard_map/pallas_call | solution.py:24
  70.8 7.3 %collective-permute-done.21.z = bf16[3,16,32,128]{3,2,1,0:T(8,128)(2,1)S(1)} collective-permute-done((bf16[3,16,32,128]{3,2,1,0:T(8,128)(2,1)S(1)}, bf16[3,16,32,128]{3,2,1,0:T(8,128)(2,1)S(1)}, u32[]{:S(2)}, u32[]{:S(2)}) %collective-permute-start.21) | collective-permute-done | bytes 393248 | tf_op jit(solution)/shard_map/ppermute | solution.py:77
  78.1 1.5 %collective-permute-start.23 = (bf16[3,8,32,128]{3,2,1,0:T(8,128)(2,1)S(1)}, bf16[3,8,32,128]{3,2,1,0:T(8,128)(2,1)S(1)}, u32[]{:S(2)}, u32[]{:S(2)}) collective-permute-start(bf16[3,8,32,128]{3,2,1,0:T(8,128)(2,1)S(1)} %bitcast.16), channel_id=1, source_target_pairs={{0,1},{1,0},{2,3},{3,2},{4,5},{5,4},{6,7},{7,6},{8,9},{9,8},{10,11... | collective-permute-start | bytes 589832 | tf_op jit(solution)/shard_map/ppermute | solution.py:77
  79.8 2.4 %shard_map.52 = (f32[864,384]{1,0:T(8,128)S(1)}, f32[3,8,32,128]{3,2,1,0:T(8,128)S(1)}, bf16[1,3,8,32,128]{4,3,2,1,0:T(8,128)(2,1)S(1)}) custom-call(s32[16,96]{1,0:T(8,128)S(1)} %pad_add_fusion.lists_ref, f32[864,384]{1,0:T(8,128)S(1)} %shard_map.51.acc_in, bf16[3,16,32,128]{3,2,1,0:T(8,128)(2,1)S(1)} %collective-permute-done.21.z, ...), custom_call_target="tpu_custom_call", output_to_operand_aliasing={{0}: (1, {})} | custom-call | tf_op jit(solution)/shard_map/pallas_call | solution.py:24
  82.2 1.6 %collective-permute-start.24 = (bf16[3,8,32,128]{3,2,1,0:T(8,128)(2,1)S(1)}, bf16[3,8,32,128]{3,2,1,0:T(8,128)(2,1)S(1)}, u32[]{:S(2)}, u32[]{:S(2)}) collective-permute-start(bf16[3,8,32,128]{3,2,1,0:T(8,128)(2,1)S(1)} %bitcast.17), channel_id=1, source_target_pairs={{0,1},{1,0},{2,3},{3,2},{4,5},{5,4},{6,7},{7,6},{8,9},{9,8},{10,11... | collective-permute-start | bytes 589832 | tf_op jit(solution)/shard_map/ppermute | solution.py:77
  83.8 1.9 %collective-permute-done.23 = bf16[3,8,32,128]{3,2,1,0:T(8,128)(2,1)S(1)} collective-permute-done((bf16[3,8,32,128]{3,2,1,0:T(8,128)(2,1)S(1)}, bf16[3,8,32,128]{3,2,1,0:T(8,128)(2,1)S(1)}, u32[]{:S(2)}, u32[]{:S(2)}) %collective-permute-start.23) | collective-permute-done | bytes 196640 | tf_op jit(solution)/shard_map/ppermute | solution.py:77
  85.8 3.8 %collective-permute-done.24 = bf16[3,8,32,128]{3,2,1,0:T(8,128)(2,1)S(1)} collective-permute-done((bf16[3,8,32,128]{3,2,1,0:T(8,128)(2,1)S(1)}, bf16[3,8,32,128]{3,2,1,0:T(8,128)(2,1)S(1)}, u32[]{:S(2)}, u32[]{:S(2)}) %collective-permute-start.24) | collective-permute-done | bytes 196640 | tf_op jit(solution)/shard_map/ppermute | solution.py:77
  89.6 2.0 %shard_map.53 = f32[3,8,128,128]{3,2,1,0:T(8,128)} custom-call(f32[3,8,32,128]{3,2,1,0:T(8,128)S(1)} %get-tuple-element.40.refs_0_, f32[3,8,32,128]{3,2,1,0:T(8,128)S(1)} %get-tuple-element.45.refs_1_, bf16[1,3,8,32,128]{4,3,2,1,0:T(8,128)(2,1)S(1)} %bitcast.14, bf16[1,3,8,32,128]{4,3,2,1,0:T(8,128)(2,1)S(1)} %bitcast.15), custom_call_target="tpu_custom_call" | custom-call | tf_op jit(solution)/shard_map/pallas_call | solution.py:24
  (46 shorter events, 16.5 us)
Async XLA Ops:
  1.6 7.9 %collective-permute-start = (bf16[3,8,32,128]{3,2,1,0:T(8,128)(2,1)S(1)}, bf16[3,8,32,128]{3,2,1,0:T(8,128)(2,1)S(1)}, u32[]{:S(2)}, u32[]{:S(2)}) collective-permute-start(bf16[3,8,32,128]{3,2,1,0:T(8,128)(2,1)S(1)} %bitcast.10), channel_id=1, source_target_pairs={{0,1},{1,0},{2,3},{3,2},{4,5},{5,4},{6,7},{7,6},{8,9},{9,8},{10,11... | collective-permute-start | bytes 589832 | tf_op jit(solution)/shard_map/ppermute | solution.py:77
  10.4 9.8 %collective-permute-start.2 = (bf16[480,384]{1,0:T(8,128)(2,1)S(1)}, bf16[480,384]{1,0:T(8,128)(2,1)S(1)}, u32[]{:S(2)}, u32[]{:S(2)}) collective-permute-start(bf16[480,384]{1,0:T(8,128)(2,1)S(1)} %shard_map.39.refs_0_.w), channel_id=1, source_target_pairs={{0,4},{2,6},{4,0},{6,2},{8,12},{10,14},{12,8},{14,10},{16,20},{18,... | collective-permute-start | bytes 1105928 | tf_op jit(solution)/shard_map/ppermute | solution.py:77
  12.2 9.5 %collective-permute-start.5 = (bf16[3,8,32,128]{3,2,1,0:T(8,128)(2,1)S(1)}, bf16[3,8,32,128]{3,2,1,0:T(8,128)(2,1)S(1)}, u32[]{:S(2)}, u32[]{:S(2)}) collective-permute-start(bf16[3,8,32,128]{3,2,1,0:T(8,128)(2,1)S(1)} %bitcast.11), channel_id=1, source_target_pairs={{0,1},{1,0},{2,3},{3,2},{4,5},{5,4},{6,7},{7,6},{8,9},{9,8},{10,11... | collective-permute-start | bytes 589832 | tf_op jit(solution)/shard_map/ppermute | solution.py:77
  13.7 13.5 %collective-permute-start.4 = (bf16[3,8,64,128]{3,2,1,0:T(8,128)(2,1)S(1)}, bf16[3,8,64,128]{3,2,1,0:T(8,128)(2,1)S(1)}, u32[]{:S(2)}, u32[]{:S(2)}) collective-permute-start(bf16[3,8,64,128]{3,2,1,0:T(8,128)(2,1)S(1)} %get-tuple-element.30.mine_ref), channel_id=1, source_target_pairs={{0,1},{1,0},{2,3},{3,2},{4,5},{5,4},{6,7},{7,6},{8,9},{9,8},{10,11... | collective-permute-start | bytes 1179656 | tf_op jit(solution)/shard_map/ppermute | solution.py:77
  14.2 14.0 %collective-permute-start.1 = (bf16[480,384]{1,0:T(8,128)(2,1)S(1)}, bf16[480,384]{1,0:T(8,128)(2,1)S(1)}, u32[]{:S(2)}, u32[]{:S(2)}) collective-permute-start(bf16[480,384]{1,0:T(8,128)(2,1)S(1)} %shard_map.39.refs_0_.w), channel_id=1, source_target_pairs={{0,2},{2,0},{4,6},{6,4},{8,10},{10,8},{12,14},{14,12},{16,18},{18,... | collective-permute-start | bytes 1105928 | tf_op jit(solution)/shard_map/ppermute | solution.py:77
  20.2 8.0 %collective-permute-start.3 = (bf16[480,384]{1,0:T(8,128)(2,1)S(1)}, bf16[480,384]{1,0:T(8,128)(2,1)S(1)}, u32[]{:S(2)}, u32[]{:S(2)}) collective-permute-start(bf16[480,384]{1,0:T(8,128)(2,1)S(1)} %collective-permute-done.2.x), channel_id=1, source_target_pairs={{0,2},{2,0},{4,6},{6,4},{8,10},{10,8},{12,14},{14,12},{16,18},{18,... | collective-permute-start | bytes 1105928 | tf_op jit(solution)/shard_map/ppermute | solution.py:77
  20.2 12.8 %collective-permute-start.6 = (bf16[480,384]{1,0:T(8,128)(2,1)S(1)}, bf16[480,384]{1,0:T(8,128)(2,1)S(1)}, u32[]{:S(2)}, u32[]{:S(2)}) collective-permute-start(bf16[480,384]{1,0:T(8,128)(2,1)S(1)} %collective-permute-done.2.x), channel_id=1, source_target_pairs={{0,8},{2,10},{4,28},{6,30},{8,16},{10,18},{12,4},{14,6},{16,24},{1... | collective-permute-start | bytes 1105928 | tf_op jit(solution)/shard_map/ppermute | solution.py:77
  22.6 12.6 %collective-permute-start.10 = (bf16[480,384]{1,0:T(8,128)(2,1)S(1)}, bf16[480,384]{1,0:T(8,128)(2,1)S(1)}, u32[]{:S(2)}, u32[]{:S(2)}) collective-permute-start(bf16[480,384]{1,0:T(8,128)(2,1)S(1)} %shard_map.41.refs_1_.w), channel_id=1, source_target_pairs={{0,4},{2,6},{4,0},{6,2},{8,12},{10,14},{12,8},{14,10},{16,20},{18,... | collective-permute-start | bytes 1105928 | tf_op jit(solution)/shard_map/ppermute | solution.py:77
  33.0 2.1 %collective-permute-start.7 = (bf16[480,384]{1,0:T(8,128)(2,1)S(1)}, bf16[480,384]{1,0:T(8,128)(2,1)S(1)}, u32[]{:S(2)}, u32[]{:S(2)}) collective-permute-start(bf16[480,384]{1,0:T(8,128)(2,1)S(1)} %collective-permute-done.6.z), channel_id=1, source_target_pairs={{0,2},{2,0},{4,6},{6,4},{8,10},{10,8},{12,14},{14,12},{16,18},{18,... | collective-permute-start | bytes 1105928 | tf_op jit(solution)/shard_map/ppermute | solution.py:77
  33.0 6.8 %collective-permute-start.9 = (bf16[480,384]{1,0:T(8,128)(2,1)S(1)}, bf16[480,384]{1,0:T(8,128)(2,1)S(1)}, u32[]{:S(2)}, u32[]{:S(2)}) collective-permute-start(bf16[480,384]{1,0:T(8,128)(2,1)S(1)} %shard_map.41.refs_1_.w), channel_id=1, source_target_pairs={{0,2},{2,0},{4,6},{6,4},{8,10},{10,8},{12,14},{14,12},{16,18},{18,... | collective-permute-start | bytes 1105928 | tf_op jit(solution)/shard_map/ppermute | solution.py:77
  35.1 4.8 %collective-permute-start.11 = (bf16[480,384]{1,0:T(8,128)(2,1)S(1)}, bf16[480,384]{1,0:T(8,128)(2,1)S(1)}, u32[]{:S(2)}, u32[]{:S(2)}) collective-permute-start(bf16[480,384]{1,0:T(8,128)(2,1)S(1)} %collective-permute-done.10.x), channel_id=1, source_target_pairs={{0,2},{2,0},{4,6},{6,4},{8,10},{10,8},{12,14},{14,12},{16,18},{18,... | collective-permute-start | bytes 1105928 | tf_op jit(solution)/shard_map/ppermute | solution.py:77
  35.1 12.8 %collective-permute-start.12 = (bf16[480,384]{1,0:T(8,128)(2,1)S(1)}, bf16[480,384]{1,0:T(8,128)(2,1)S(1)}, u32[]{:S(2)}, u32[]{:S(2)}) collective-permute-start(bf16[480,384]{1,0:T(8,128)(2,1)S(1)} %collective-permute-done.10.x), channel_id=1, source_target_pairs={{0,8},{2,10},{4,28},{6,30},{8,16},{10,18},{12,4},{14,6},{16,24},{1... | collective-permute-start | bytes 1105928 | tf_op jit(solution)/shard_map/ppermute | solution.py:77
  36.8 14.6 %collective-permute-start.14 = (bf16[3,16,32,128]{3,2,1,0:T(8,128)(2,1)S(1)}, bf16[3,16,32,128]{3,2,1,0:T(8,128)(2,1)S(1)}, u32[]{:S(2)}, u32[]{:S(2)}) collective-permute-start(bf16[3,16,32,128]{3,2,1,0:T(8,128)(2,1)S(1)} %get-tuple-element.33.w), channel_id=1, source_target_pairs={{0,4},{2,6},{4,0},{6,2},{8,12},{10,14},{12,8},{14,10},{16,20},{18,... | collective-permute-start | bytes 1179656 | tf_op jit(solution)/shard_map/ppermute | solution.py:77
  47.9 4.0 %collective-permute-start.8 = (bf16[3,16,32,128]{3,2,1,0:T(8,128)(2,1)S(1)}, bf16[3,16,32,128]{3,2,1,0:T(8,128)(2,1)S(1)}, u32[]{:S(2)}, u32[]{:S(2)}) collective-permute-start(bf16[3,16,32,128]{3,2,1,0:T(8,128)(2,1)S(1)} %get-tuple-element.33.w), channel_id=1, source_target_pairs={{0,2},{2,0},{4,6},{6,4},{8,10},{10,8},{12,14},{14,12},{16,18},{18,... | collective-permute-start | bytes 1179656 | tf_op jit(solution)/shard_map/ppermute | solution.py:77
  51.2 10.8 %collective-permute-start.19 = (bf16[3,16,32,128]{3,2,1,0:T(8,128)(2,1)S(1)}, bf16[3,16,32,128]{3,2,1,0:T(8,128)(2,1)S(1)}, u32[]{:S(2)}, u32[]{:S(2)}) collective-permute-start(bf16[3,16,32,128]{3,2,1,0:T(8,128)(2,1)S(1)} %get-tuple-element.36.w), channel_id=1, source_target_pairs={{0,4},{2,6},{4,0},{6,2},{8,12},{10,14},{12,8},{14,10},{16,20},{18,... | collective-permute-start | bytes 1179656 | tf_op jit(solution)/shard_map/ppermute | solution.py:77
  51.3 10.8 %collective-permute-start.15 = (bf16[3,16,32,128]{3,2,1,0:T(8,128)(2,1)S(1)}, bf16[3,16,32,128]{3,2,1,0:T(8,128)(2,1)S(1)}, u32[]{:S(2)}, u32[]{:S(2)}) collective-permute-start(bf16[3,16,32,128]{3,2,1,0:T(8,128)(2,1)S(1)} %collective-permute-done.14.x), channel_id=1, source_target_pairs={{0,2},{2,0},{4,6},{6,4},{8,10},{10,8},{12,14},{14,12},{16,18},{18,... | collective-permute-start | bytes 1179656 | tf_op jit(solution)/shard_map/ppermute | solution.py:77
  51.4 13.3 %collective-permute-start.16 = (bf16[3,16,32,128]{3,2,1,0:T(8,128)(2,1)S(1)}, bf16[3,16,32,128]{3,2,1,0:T(8,128)(2,1)S(1)}, u32[]{:S(2)}, u32[]{:S(2)}) collective-permute-start(bf16[3,16,32,128]{3,2,1,0:T(8,128)(2,1)S(1)} %collective-permute-done.14.x), channel_id=1, source_target_pairs={{0,8},{2,10},{4,28},{6,30},{8,16},{10,18},{12,4},{14,6},{16,24},{1... | collective-permute-start | bytes 1179656 | tf_op jit(solution)/shard_map/ppermute | solution.py:77
  51.5 13.4 %collective-permute-start.18 = (bf16[3,16,32,128]{3,2,1,0:T(8,128)(2,1)S(1)}, bf16[3,16,32,128]{3,2,1,0:T(8,128)(2,1)S(1)}, u32[]{:S(2)}, u32[]{:S(2)}) collective-permute-start(bf16[3,16,32,128]{3,2,1,0:T(8,128)(2,1)S(1)} %get-tuple-element.36.w), channel_id=1, source_target_pairs={{0,2},{2,0},{4,6},{6,4},{8,10},{10,8},{12,14},{14,12},{16,18},{18,... | collective-permute-start | bytes 1179656 | tf_op jit(solution)/shard_map/ppermute | solution.py:77
  62.1 4.8 %collective-permute-start.20 = (bf16[3,16,32,128]{3,2,1,0:T(8,128)(2,1)S(1)}, bf16[3,16,32,128]{3,2,1,0:T(8,128)(2,1)S(1)}, u32[]{:S(2)}, u32[]{:S(2)}) collective-permute-start(bf16[3,16,32,128]{3,2,1,0:T(8,128)(2,1)S(1)} %collective-permute-done.19.x), channel_id=1, source_target_pairs={{0,2},{2,0},{4,6},{6,4},{8,10},{10,8},{12,14},{14,12},{16,18},{18,... | collective-permute-start | bytes 1179656 | tf_op jit(solution)/shard_map/ppermute | solution.py:77
  64.7 3.6 %collective-permute-start.17 = (bf16[3,16,32,128]{3,2,1,0:T(8,128)(2,1)S(1)}, bf16[3,16,32,128]{3,2,1,0:T(8,128)(2,1)S(1)}, u32[]{:S(2)}, u32[]{:S(2)}) collective-permute-start(bf16[3,16,32,128]{3,2,1,0:T(8,128)(2,1)S(1)} %collective-permute-done.16.z), channel_id=1, source_target_pairs={{0,2},{2,0},{4,6},{6,4},{8,10},{10,8},{12,14},{14,12},{16,18},{18,... | collective-permute-start | bytes 1179656 | tf_op jit(solution)/shard_map/ppermute | solution.py:77
  64.9 13.2 %collective-permute-start.21 = (bf16[3,16,32,128]{3,2,1,0:T(8,128)(2,1)S(1)}, bf16[3,16,32,128]{3,2,1,0:T(8,128)(2,1)S(1)}, u32[]{:S(2)}, u32[]{:S(2)}) collective-permute-start(bf16[3,16,32,128]{3,2,1,0:T(8,128)(2,1)S(1)} %collective-permute-done.19.x), channel_id=1, source_target_pairs={{0,8},{2,10},{4,28},{6,30},{8,16},{10,18},{12,4},{14,6},{16,24},{1... | collective-permute-start | bytes 1179656 | tf_op jit(solution)/shard_map/ppermute | solution.py:77
  78.1 1.7 %collective-permute-start.22 = (bf16[3,16,32,128]{3,2,1,0:T(8,128)(2,1)S(1)}, bf16[3,16,32,128]{3,2,1,0:T(8,128)(2,1)S(1)}, u32[]{:S(2)}, u32[]{:S(2)}) collective-permute-start(bf16[3,16,32,128]{3,2,1,0:T(8,128)(2,1)S(1)} %collective-permute-done.21.z), channel_id=1, source_target_pairs={{0,2},{2,0},{4,6},{6,4},{8,10},{10,8},{12,14},{14,12},{16,18},{18,... | collective-permute-start | bytes 1179656 | tf_op jit(solution)/shard_map/ppermute | solution.py:77
  78.1 7.7 %collective-permute-start.23 = (bf16[3,8,32,128]{3,2,1,0:T(8,128)(2,1)S(1)}, bf16[3,8,32,128]{3,2,1,0:T(8,128)(2,1)S(1)}, u32[]{:S(2)}, u32[]{:S(2)}) collective-permute-start(bf16[3,8,32,128]{3,2,1,0:T(8,128)(2,1)S(1)} %bitcast.16), channel_id=1, source_target_pairs={{0,1},{1,0},{2,3},{3,2},{4,5},{5,4},{6,7},{7,6},{8,9},{9,8},{10,11... | collective-permute-start | bytes 589832 | tf_op jit(solution)/shard_map/ppermute | solution.py:77
  82.2 7.4 %collective-permute-start.24 = (bf16[3,8,32,128]{3,2,1,0:T(8,128)(2,1)S(1)}, bf16[3,8,32,128]{3,2,1,0:T(8,128)(2,1)S(1)}, u32[]{:S(2)}, u32[]{:S(2)}) collective-permute-start(bf16[3,8,32,128]{3,2,1,0:T(8,128)(2,1)S(1)} %bitcast.17), channel_id=1, source_target_pairs={{0,1},{1,0},{2,3},{3,2},{4,5},{5,4},{6,7},{7,6},{8,9},{9,8},{10,11... | collective-permute-start | bytes 589832 | tf_op jit(solution)/shard_map/ppermute | solution.py:77
  (2 other events, 2.8 us)

commit v5 on v4

--- a/solution.py
+++ b/solution.py
@@ -9,23 +9,25 @@
 BAND = 2 * REACH + 1
 WIDE = 4 * REACH + 1
 VMEM = pl.BlockSpec(memory_space=pltpu.VMEM)
+HBM = pl.BlockSpec(memory_space=pltpu.HBM)
 SMEM = pl.BlockSpec(memory_space=pltpu.SMEM)
 PARAMS = pltpu.CompilerParams(vmem_limit_bytes=16 * 1024 * 1024)
 
 
-def call(kernel, ins, outs, scratch=(), aliases=None, resident=True, us=3):
-    specs = [SMEM if x.dtype == jnp.int32 else VMEM for x in ins]
-    if resident:
+def call(kernel, ins, outs, scratch=(), aliases=None, hbm_in=False, hbm_out=False):
+    here = HBM if hbm_in else VMEM
+    specs = [SMEM if x.dtype == jnp.int32 else here for x in ins]
+    if not hbm_out:
         outs = [pltpu.VMEM(x.shape, x.dtype) for x in outs]
+    place = pltpu.HBM if hbm_in else pltpu.VMEM
     ins = [
-        x if x.dtype == jnp.int32 else pltpu.with_memory_space_constraint(x, pltpu.VMEM)
-        for x in ins
+        x if x.dtype == jnp.int32 else pltpu.with_memory_space_constraint(x, place) for x in ins
     ]
     return pl.pallas_call(
         kernel,
         out_shape=tuple(outs),
         in_specs=specs,
-        out_specs=tuple(VMEM for _ in outs),
+        out_specs=tuple(HBM if hbm_out else VMEM for _ in outs),
         scratch_shapes=list(scratch),
         input_output_aliases=aliases or {},
         compiler_params=PARAMS,
@@ -55,8 +57,10 @@
     n_rows = lax.axis_size("rows")
     n = lax.axis_size("inner")
     part = bs // n
-    cuts = 2 if part % 32 == 0 else 1
-    cols = part // cuts
+    sizes = [part // 2] * 2 if part % 32 == 0 else [part]
+    cuts = len(sizes)
+    offs = [sum(sizes[:c]) for c in range(cuts)]
+    unit = min(sizes)
     width = rb * bs
     bf16, f32 = jnp.bfloat16, jnp.float32
     shape = jax.ShapeDtypeStruct
@@ -79,6 +83,9 @@
     def rows_at(index, size):
         return pl.ds(pl.multiple_of(index * size, size), size)
 
+    def piece(index, c):
+        return pl.ds(pl.multiple_of(index * part + offs[c], unit), sizes[c])
+
     def wrapped(x):
         return jnp.where(x < 0, x + nb, jnp.where(x >= nb, x - nb, x))
 
@@ -92,24 +99,28 @@
         return received([send(nth(x, m - 1), shift(m), "inner") for m in range(1, n)])
 
     def pack(p_ref, mine_ref, *refs):
-        rest_refs, turned = refs[:cuts], refs[-1]
-        q = lax.axis_index("inner")
+        rest_refs, (raw, turned, sems) = refs[:cuts], refs[-3:]
+        q = lax.axis_index("inner")
+        copies = [pltpu.make_async_copy(p_ref.at[i], raw.at[i], sems.at[i]) for i in range(rb)]
+        for copy in copies:
+            copy.start()
         for i in range(rb):
+            copies[i].wait()
             for s in range(slots):
-                turned[i, s] = p_ref[i, s].T
+                turned[i, s] = raw[i, s].T
                 mine_ref[i, s] = turned[i, s, rows_at(q, part), :]
                 for c in chunks:
                     for m in range(1, n):
-                        to = lax.rem(q + m, n)
-                        rest_refs[c][m - 1, i, s] = turned[i, s, rows_at(to * cuts + c, cols), :]
-
+                        rest_refs[c][m - 1, i, s] = turned[i, s, piece(lax.rem(q + m, n), c), :]
+
+    whole = pltpu.VMEM((rb, slots, bs, bs), bf16)
     packed = call(
         pack,
         [p_blocks],
         [shape((rb, slots, part, bs), bf16)]
-        + [shape((n - 1, rb, slots, cols, bs), bf16)] * cuts,
-        [pltpu.VMEM((rb, slots, bs, bs), bf16)],
-        us=1,
+        + [shape((n - 1, rb, slots, k, bs), bf16) for k in sizes],
+        [whole, whole, pltpu.SemaphoreType.DMA((rb,))],
+        hbm_in=True,
     )
     mine, rest = packed[0], packed[1:]
     lists = jnp.concatenate([col_lists.T, fill_lists.T], axis=1)
@@ -130,8 +141,8 @@
             for i in range(rb):
                 at = column(lists_ref, i, q * slots + s)
                 for c in chunks:
-                    value = mine_ref[i, s, pl.ds(c * cols, cols), :]
-                    add(out_refs[c], rows_at(at, cols), pl.ds(i * bs, bs), value)
+                    value = mine_ref[i, s, pl.ds(offs[c], sizes[c]), :]
+                    add(out_refs[c], rows_at(at, sizes[c]), pl.ds(i * bs, bs), value)
 
     def start_band(lists_ref, *refs):
         rest_refs, out_ref = refs[:cuts], refs[-1]
@@ -142,7 +153,7 @@
                 at = column(lists_ref, i, q * slots + s) * n + lax.rem(q + 1, n)
                 for c in chunks:
                     value = rest_refs[c][0, i, s]
-                    add(out_ref, rows_at(at * cuts + c, cols), pl.ds(i * bs, bs), value)
+                    add(out_ref, piece(at, c), pl.ds(i * bs, bs), value)
 
     def end_rows(lists_ref, in_ref, got_ref, out_ref):
         q = lax.axis_index("inner")
@@ -150,7 +161,7 @@
             for i in range(rb):
                 for m in range(1, n):
                     at = column(lists_ref, i, lax.rem(q - m + n, n) * slots + s)
-                    add(out_ref, rows_at(at, cols), pl.ds(i * bs, bs), got_ref[m - 1, i, s])
+                    add(out_ref, rows_at(at, got_ref.shape[3]), pl.ds(i * bs, bs), got_ref[m - 1, i, s])
 
     def end_band(lists_ref, in_ref, left_ref, *refs):
         dense_refs, out_ref = refs[:cuts], refs[-1]
@@ -162,7 +173,7 @@
                 add(out_ref, rows_at(at, part), pl.ds(i * bs, bs), left_ref[i, s])
         for k in range(BAND * rb):
             for c in chunks:
-                out_ref[rows_at((k * n + q) * cuts + c, cols), :] = dense_refs[c][pl.ds(k * cols, cols), :]
+                out_ref[piece(k * n + q, c), :] = dense_refs[c][pl.ds(k * sizes[c], sizes[c]), :]
 
     def whole_band(lists_ref, left_ref, out_ref):
         out_ref[...] = jnp.zeros(out_ref.shape, bf16)
@@ -172,43 +183,43 @@
                     at = column(lists_ref, i, g * slots + s)
                     add(out_ref, rows_at(at, bs), pl.ds(i * bs, bs), left_ref[g, i, s].T)
 
-    span = BAND * rb * cols
-    wide = WIDE * rb * cols
-    acc_shape = shape((wide, width), f32)
-    rows_shape = shape((span, width), bf16)
     band_shape = shape((BAND * width, width), bf16)
-    own = call(start_rows, [lists, mine], [rows_shape] * cuts, us=1)
+    rows_shapes = [shape((BAND * rb * k, width), bf16) for k in sizes]
+    acc_shapes = [shape((WIDE * rb * k, width), f32) for k in sizes]
+    own = call(start_rows, [lists, mine], rows_shapes)
     got = [exchange(x) for x in rest]
     if n == 2:
-        (band,) = call(start_band, [lists, *rest], [band_shape], us=1)
+        (band,) = call(start_band, [lists, *rest], [band_shape])
         left = send(after(mine, got[0]), shift(1), "inner")
     else:
         left = lax.all_gather(p_blocks, "inner", axis=0)
     own = [
-        call(end_rows, [lists, own[c], got[c]], [rows_shape], aliases={1: 0}, us=1)[0]
+        call(end_rows, [lists, own[c], got[c]], [rows_shapes[c]], aliases={1: 0})[0]
         for c in chunks
     ]
     if n == 2:
-        (band,) = call(end_band, [lists, band, left, *own], [band_shape], aliases={1: 0}, us=2)
+        (band,) = call(end_band, [lists, band, left, *own], [band_shape], aliases={1: 0})
     else:
-        (band,) = call(whole_band, [lists, left], [band_shape], us=2)
-
-    def moved(v):
+        (band,) = call(whole_band, [lists, left], [band_shape])
+
+    def moved(v, *first):
         x = send(v, flip_x)
-        return x, send(x, move_z)
+        return x, send(after(x, *first), move_z)
 
     def weights(left_ref, d):
         return left_ref[rows_at(d + REACH, width), :]
 
     def square_term(d, rows_ref, left_ref, acc_ref):
         term = jnp.dot(rows_ref[...], weights(left_ref, d), preferred_element_type=f32)
-        where = pl.ds(pl.multiple_of((d + REACH) * rb * cols, rb * cols), span)
-        acc_ref[where, :] += term
+        span = rows_ref.shape[0]
+        step = span // BAND
+        acc_ref[pl.ds(pl.multiple_of((d + REACH) * step, step), span), :] += term
 
     def square_near(w, u, x, cx, left_ref, acc_ref):
         j = lax.rem(lax.axis_index("rows"), 4)
         d = offsets(j)
-        edge = REACH * rb * cols
+        span = w.shape[0]
+        edge = span // BAND * REACH
         acc_ref[:edge, :] = jnp.zeros((edge, width), f32)
         acc_ref[edge : edge + span, :] = jnp.dot(
             w[...], left_ref[REACH * width : (REACH + 1) * width, :], preferred_element_type=f32
@@ -232,25 +243,23 @@
 
         for v in range(fill):
             for i in range(rb):
-                value = acc_ref[kept(lists_ref, i, v), pl.ds(i * bs, bs)]
+                value = acc_ref[kept(lists_ref, i, v, sq_ref.shape[2]), pl.ds(i * bs, bs)]
                 sq_ref[i, v] = value
                 low_ref[i, v] = value.astype(bf16)
 
-    kept_shape = (rb, fill, cols, bs)
-
-    def square(w, x, z, lead):
+    def square(c, w, x, z, lead):
+        kept_shape, acc_shape = (rb, fill, sizes[c], bs), acc_shapes[c]
         u, cx = send(w, flip_core), send(x, flip_core)
-        (acc,) = call(square_near, [after(w, *lead), u, x, cx, band], [acc_shape], us=2)
+        (acc,) = call(square_near, [after(w, *lead), u, x, cx, band], [acc_shape])
         z = after(z, acc)
         return call(
             square_far,
             [lists, acc, z, send(z, flip_core), band],
             [acc_shape, shape(kept_shape, f32), shape(kept_shape, bf16)],
             aliases={1: 0},
-            us=2,
         )[1:]
 
-    def kept(lists_ref, i, v):
+    def kept(lists_ref, i, v, cols):
         o = lax.axis_index("rows")
         return rows_at(wrapped(lists_ref[v, nb + o * rb + i] - rb * (o - 2 * REACH)), cols)
 
@@ -258,6 +267,7 @@
         o = lax.axis_index("rows")
         source = lax.rem(o + d + n_rows, n_rows)
         blocks = (WIDE - reach) * rb
+        cols = low_ref.shape[2]
         start = jnp.maximum(d, 0) * rb
         rows = blocks * cols
         dense[:rows, :] = jnp.zeros((rows, width), bf16)
@@ -298,7 +308,7 @@
             cube_term(lists_ref, d["core_z"], 1, cz, left_ref, dense, acc_ref)
 
         def result(i, v):
-            return 3.0 * sq_ref[i, v] - 2.0 * acc_ref[kept(lists_ref, i, v), pl.ds(i * bs, bs)]
+            return 3.0 * sq_ref[i, v] - 2.0 * acc_ref[kept(lists_ref, i, v, sq_ref.shape[2]), pl.ds(i * bs, bs)]
 
         for s in range(slots):
             for i in range(rb):
@@ -306,11 +316,11 @@
                 for m in range(1, n):
                     give_ref[m - 1, i, s] = result(i, lax.rem(q + m, n) * slots + s).astype(bf16)
 
-    dense = [pltpu.VMEM((wide + cols, width), bf16)]
+    dense = [[pltpu.VMEM(((WIDE * rb + 1) * k, width), bf16)] for k in sizes]
     x, z, sq, low, x2, z2 = [], [], [], [], [], []
     for c in chunks:
-        x_c, z_c = moved(own[c])
-        one = square(own[c], x_c, z_c, low)
+        x_c, z_c = moved(own[c], *own[c + 1 : c + 2])
+        one = square(c, own[c], x_c, z_c, low)
         sq.append(one[0])
         low.append(one[1])
     keep, give, near = [], [], []
@@ -318,45 +328,49 @@
         x_c = send(low[c], flip_x)
         u = send(low[c], flip_core)
         (acc,) = call(
-            cube_own, [lists, low[c], u, after(band, low[-1], *near)], [acc_shape], dense, us=3
+            cube_own, [lists, low[c], u, after(band, low[-1], *near)], [acc_shapes[c]], dense[c]
         )
         x2.append(x_c)
         z2.append(send(x_c, move_z))
         cx = send(x_c, flip_core)
-        (acc,) = call(cube_near, [lists, acc, x_c, cx, band], [acc_shape], dense, aliases={1: 0}, us=2)
+        (acc,) = call(cube_near, [lists, acc, x_c, cx, band], [acc_shapes[c]], dense[c], aliases={1: 0})
         near.append(acc)
     for c in chunks:
         z_c = after(z2[c], near[c], *give)
         one = call(
             cube_far,
             [lists, near[c], z_c, send(z_c, flip_core), band, sq[c]],
-            [acc_shape, shape((rb, slots, cols, bs), f32), shape((n - 1, rb, slots, cols, bs), bf16)],
-            dense,
+            [acc_shapes[c], shape((rb, slots, sizes[c], bs), f32), shape((n - 1, rb, slots, sizes[c], bs), bf16)],
+            dense[c],
             aliases={1: 0},
-            us=3,
         )[1:]
         keep.append(one[0])
         give.append(one[1])
     taken = [exchange(v) for v in give]
 
     def join(*refs):
-        keep_refs, taken_refs, out_ref, turned = refs[:cuts], refs[cuts : 2 * cuts], refs[-2], refs[-1]
-        q = lax.axis_index("inner")
+        keep_refs, taken_refs, (out_ref, turned, done, sems) = refs[:cuts], refs[cuts : 2 * cuts], refs[-4:]
+        q = lax.axis_index("inner")
+        copies = [pltpu.make_async_copy(done.at[i], out_ref.at[i], sems.at[i]) for i in range(rb)]
         for i in range(rb):
             for s in range(slots):
                 for c in chunks:
-                    turned[i, s, rows_at(q * cuts + c, cols), :] = keep_refs[c][i, s]
+                    turned[i, s, piece(q, c), :] = keep_refs[c][i, s]
                     for m in range(1, n):
-                        at = lax.rem(q - m + n, n) * cuts + c
-                        turned[i, s, rows_at(at, cols), :] = taken_refs[c][m - 1, i, s].astype(f32)
-                out_ref[i, s] = turned[i, s].T
-
+                        at = piece(lax.rem(q - m + n, n), c)
+                        turned[i, s, at, :] = taken_refs[c][m - 1, i, s].astype(f32)
+                done[i, s] = turned[i, s].T
+            copies[i].start()
+        for copy in copies:
+            copy.wait()
+
+    whole = pltpu.VMEM((rb, slots, bs, bs), f32)
     (out,) = call(
         join,
         [*keep, *taken],
         [shape((rb, slots, bs, bs), f32)],
-        [pltpu.VMEM((rb, slots, bs, bs), f32)],
-        resident=False,
+        [whole, whole, pltpu.SemaphoreType.DMA((rb,))],
+        hbm_out=True,
     )
     return out
 

time: 91.8 us -> 91 us (level)
  local copies, waits for them, and re-layouts: 1.13 us -> 0 us
    unnamed x2 -> x0, local copies, waits for them, and re-layouts: 1.13 us -> none
  transfers between devices with their start and end apart: 25 -> 25, of which waited for: 12 -> 12; matrix products, arithmetic and copies ran while one was open for 1% -> 1% of each run, Pallas kernels for 22% -> 23%
where the time goes in v5:
time: 91 us; the launch traced here: 90.8 us
  waiting for transfers between devices  45.9 us (50%)
  Pallas kernels  24.5 us (27%)
  starting transfers between devices  19.2 us (21%)
    ppermute x25, waiting for transfers between devices, send(): return lax.ppermute(x, axis, pairs)  45.9 us
    pallas_call x17, Pallas kernels, call(): pl.pallas_call(kernel, out_shape=tuple(outs), in_specs=specs, out_specs=t...  24.5 us
    ppermute x25, starting transfers between devices, send(): return lax.ppermute(x, axis, pairs)  19.2 us
  transfers between devices with their start and end apart: 25, of which 12 were waited for; matrix products, arithmetic and copies ran while one was open for 1% of the time, Pallas kernels for 23%

profile of v5, /device:TPU:0, one launch (start us, length us, event | category | flops | bytes accessed | tf_op | source)
XLA Modules:
  0.0 90.8 jit_solution(2010771409116029994)
XLA Ops:
  0.0 1.5 %shard_map.37 = (bf16[3,8,64,128]{3,2,1,0:T(8,128)(2,1)S(1)}, bf16[1,3,8,32,128]{4,3,2,1,0:T(8,128)(2,1)S(1)}, bf16[1,3,8,32,128]{4,3,2,1,0:T(8,128)(2,1)S(1)}) custom-call(bf16[3,8,128,128]{3,2,1,0:T(8,128)(2,1)} %p_ref.1), custom_call_target="tpu_custom_call" | custom-call | tf_op jit(solution)/shard_map/pallas_call | solution.py:26
  1.5 3.0 %collective-permute-start = (bf16[3,8,32,128]{3,2,1,0:T(8,128)(2,1)S(1)}, bf16[3,8,32,128]{3,2,1,0:T(8,128)(2,1)S(1)}, u32[]{:S(2)}, u32[]{:S(2)}) collective-permute-start(bf16[3,8,32,128]{3,2,1,0:T(8,128)(2,1)S(1)} %bitcast.10), channel_id=1, source_target_pairs={{0,1},{1,0},{2,3},{3,2},{4,5},{5,4},{6,7},{7,6},{8,9},{9,8},{10,11... | collective-permute-start | bytes 589832 | tf_op jit(solution)/shard_map/ppermute | solution.py:81
  6.3 3.2 %collective-permute-done = bf16[3,8,32,128]{3,2,1,0:T(8,128)(2,1)S(1)} collective-permute-done((bf16[3,8,32,128]{3,2,1,0:T(8,128)(2,1)S(1)}, bf16[3,8,32,128]{3,2,1,0:T(8,128)(2,1)S(1)}, u32[]{:S(2)}, u32[]{:S(2)}) %collective-permute-start) | collective-permute-done | bytes 196640 | tf_op jit(solution)/shard_map/ppermute | solution.py:81
  10.3 1.8 %collective-permute-start.2 = (bf16[480,384]{1,0:T(8,128)(2,1)S(1)}, bf16[480,384]{1,0:T(8,128)(2,1)S(1)}, u32[]{:S(2)}, u32[]{:S(2)}) collective-permute-start(bf16[480,384]{1,0:T(8,128)(2,1)S(1)} %shard_map.39.refs_0_.w), channel_id=1, source_target_pairs={{0,4},{2,6},{4,0},{6,2},{8,12},{10,14},{12,8},{14,10},{16,20},{18,... | collective-permute-start | bytes 1105928 | tf_op jit(solution)/shard_map/ppermute | solution.py:81
  12.1 1.5 %collective-permute-start.5 = (bf16[3,8,32,128]{3,2,1,0:T(8,128)(2,1)S(1)}, bf16[3,8,32,128]{3,2,1,0:T(8,128)(2,1)S(1)}, u32[]{:S(2)}, u32[]{:S(2)}) collective-permute-start(bf16[3,8,32,128]{3,2,1,0:T(8,128)(2,1)S(1)} %bitcast.11), channel_id=1, source_target_pairs={{0,1},{1,0},{2,3},{3,2},{4,5},{5,4},{6,7},{7,6},{8,9},{9,8},{10,11... | collective-permute-start | bytes 589832 | tf_op jit(solution)/shard_map/ppermute | solution.py:81
  14.1 5.8 %collective-permute-done.5 = bf16[3,8,32,128]{3,2,1,0:T(8,128)(2,1)S(1)} collective-permute-done((bf16[3,8,32,128]{3,2,1,0:T(8,128)(2,1)S(1)}, bf16[3,8,32,128]{3,2,1,0:T(8,128)(2,1)S(1)}, u32[]{:S(2)}, u32[]{:S(2)}) %collective-permute-start.5) | collective-permute-done | bytes 196640 | tf_op jit(solution)/shard_map/ppermute | solution.py:81
  20.9 1.6 %collective-permute-start.6 = (bf16[480,384]{1,0:T(8,128)(2,1)S(1)}, bf16[480,384]{1,0:T(8,128)(2,1)S(1)}, u32[]{:S(2)}, u32[]{:S(2)}) collective-permute-start(bf16[480,384]{1,0:T(8,128)(2,1)S(1)} %collective-permute-done.2.x), channel_id=1, source_target_pairs={{0,8},{2,10},{4,28},{6,30},{8,16},{10,18},{12,4},{14,6},{16,24},{1... | collective-permute-start | bytes 1105928 | tf_op jit(solution)/shard_map/ppermute | solution.py:81
  22.5 2.7 %collective-permute-start.10 = (bf16[480,384]{1,0:T(8,128)(2,1)S(1)}, bf16[480,384]{1,0:T(8,128)(2,1)S(1)}, u32[]{:S(2)}, u32[]{:S(2)}) collective-permute-start(bf16[480,384]{1,0:T(8,128)(2,1)S(1)} %shard_map.41.refs_1_.w), channel_id=1, source_target_pairs={{0,4},{2,6},{4,0},{6,2},{8,12},{10,14},{12,8},{14,10},{16,20},{18,... | collective-permute-start | bytes 1105928 | tf_op jit(solution)/shard_map/ppermute | solution.py:81
  28.1 5.6 %collective-permute-done.6.z = bf16[480,384]{1,0:T(8,128)(2,1)S(1)} collective-permute-done((bf16[480,384]{1,0:T(8,128)(2,1)S(1)}, bf16[480,384]{1,0:T(8,128)(2,1)S(1)}, u32[]{:S(2)}, u32[]{:S(2)}) %collective-permute-start.6) | collective-permute-done | bytes 368672 | tf_op jit(solution)/shard_map/ppermute | solution.py:81
  35.4 1.6 %shard_map.44 = (f32[864,384]{1,0:T(8,128)S(1)}, f32[3,16,32,128]{3,2,1,0:T(8,128)S(1)}, bf16[3,16,32,128]{3,2,1,0:T(8,128)(2,1)S(1)}) custom-call(s32[16,96]{1,0:T(8,128)S(1)} %pad_add_fusion.lists_ref, f32[864,384]{1,0:T(8,128)S(1)} %shard_map.43.acc_in, bf16[480,384]{1,0:T(8,128)(2,1)S(1)} %collective-permute-done.6.z, ...), custom_call_target="tpu_custom_call", output_to_operand_aliasing={{0}: (1, {})} | custom-call | tf_op jit(solution)/shard_map/pallas_call | solution.py:26
  37.0 2.7 %collective-permute-start.14 = (bf16[3,16,32,128]{3,2,1,0:T(8,128)(2,1)S(1)}, bf16[3,16,32,128]{3,2,1,0:T(8,128)(2,1)S(1)}, u32[]{:S(2)}, u32[]{:S(2)}) collective-permute-start(bf16[3,16,32,128]{3,2,1,0:T(8,128)(2,1)S(1)} %get-tuple-element.35.w), channel_id=1, source_target_pairs={{0,4},{2,6},{4,0},{6,2},{8,12},{10,14},{12,8},{14,10},{16,20},{18,... | collective-permute-start | bytes 1179656 | tf_op jit(solution)/shard_map/ppermute | solution.py:81
  40.6 6.4 %collective-permute-done.12.z = bf16[480,384]{1,0:T(8,128)(2,1)S(1)} collective-permute-done((bf16[480,384]{1,0:T(8,128)(2,1)S(1)}, bf16[480,384]{1,0:T(8,128)(2,1)S(1)}, u32[]{:S(2)}, u32[]{:S(2)}) %collective-permute-start.12) | collective-permute-done | bytes 368672 | tf_op jit(solution)/shard_map/ppermute | solution.py:81
  48.7 1.6 %shard_map.46 = (f32[864,384]{1,0:T(8,128)S(1)}, f32[3,16,32,128]{3,2,1,0:T(8,128)S(1)}, bf16[3,16,32,128]{3,2,1,0:T(8,128)(2,1)S(1)}) custom-call(s32[16,96]{1,0:T(8,128)S(1)} %pad_add_fusion.lists_ref, f32[864,384]{1,0:T(8,128)S(1)} %shard_map.45.acc_in, bf16[480,384]{1,0:T(8,128)(2,1)S(1)} %collective-permute-done.12.z, ...), custom_call_target="tpu_custom_call", output_to_operand_aliasing={{0}: (1, {})} | custom-call | tf_op jit(solution)/shard_map/pallas_call | solution.py:26
  51.0 2.0 %shard_map.47.acc_in = f32[864,384]{1,0:T(8,128)S(1)} custom-call(s32[16,96]{1,0:T(8,128)S(1)} %pad_add_fusion.lists_ref, bf16[3,16,32,128]{3,2,1,0:T(8,128)(2,1)S(1)} %get-tuple-element.35.w, bf16[3,16,32,128]{3,2,1,0:T(8,128)(2,1)S(1)} %collective-permute-done.8.u, bf16[1920,384]{1,0:T(8,128)(2,1)S(1)} %shard_map.42.left_ref), custom_call_target="tpu_custom_call" | custom-call | tf_op jit(solution)/shard_map/pallas_call | solution.py:26
  53.0 8.2 %collective-permute-done.19.x = bf16[3,16,32,128]{3,2,1,0:T(8,128)(2,1)S(1)} collective-permute-done((bf16[3,16,32,128]{3,2,1,0:T(8,128)(2,1)S(1)}, bf16[3,16,32,128]{3,2,1,0:T(8,128)(2,1)S(1)}, u32[]{:S(2)}, u32[]{:S(2)}) %collective-permute-start.19) | collective-permute-done | bytes 393248 | tf_op jit(solution)/shard_map/ppermute | solution.py:81
  64.1 2.0 %shard_map.50.acc_in = f32[864,384]{1,0:T(8,128)S(1)} custom-call(s32[16,96]{1,0:T(8,128)S(1)} %pad_add_fusion.lists_ref, bf16[3,16,32,128]{3,2,1,0:T(8,128)(2,1)S(1)} %get-tuple-element.38.w, bf16[3,16,32,128]{3,2,1,0:T(8,128)(2,1)S(1)} %collective-permute-done.18.u, bf16[1920,384]{1,0:T(8,128)(2,1)S(1)} %shard_map.42.left_ref), custom_call_target="tpu_custom_call" | custom-call | tf_op jit(solution)/shard_map/pallas_call | solution.py:26
  67.5 2.4 %shard_map.49 = (f32[864,384]{1,0:T(8,128)S(1)}, f32[3,8,32,128]{3,2,1,0:T(8,128)S(1)}, bf16[1,3,8,32,128]{4,3,2,1,0:T(8,128)(2,1)S(1)}) custom-call(s32[16,96]{1,0:T(8,128)S(1)} %pad_add_fusion.lists_ref, f32[864,384]{1,0:T(8,128)S(1)} %shard_map.48.acc_in, bf16[3,16,32,128]{3,2,1,0:T(8,128)(2,1)S(1)} %collective-permute-done.16.z, ...), custom_call_target="tpu_custom_call", output_to_operand_aliasing={{0}: (1, {})} | custom-call | tf_op jit(solution)/shard_map/pallas_call | solution.py:26
  70.0 7.4 %collective-permute-done.21.z = bf16[3,16,32,128]{3,2,1,0:T(8,128)(2,1)S(1)} collective-permute-done((bf16[3,16,32,128]{3,2,1,0:T(8,128)(2,1)S(1)}, bf16[3,16,32,128]{3,2,1,0:T(8,128)(2,1)S(1)}, u32[]{:S(2)}, u32[]{:S(2)}) %collective-permute-start.21) | collective-permute-done | bytes 393248 | tf_op jit(solution)/shard_map/ppermute | solution.py:81
  77.4 1.5 %collective-permute-start.23 = (bf16[3,8,32,128]{3,2,1,0:T(8,128)(2,1)S(1)}, bf16[3,8,32,128]{3,2,1,0:T(8,128)(2,1)S(1)}, u32[]{:S(2)}, u32[]{:S(2)}) collective-permute-start(bf16[3,8,32,128]{3,2,1,0:T(8,128)(2,1)S(1)} %bitcast.16), channel_id=1, source_target_pairs={{0,1},{1,0},{2,3},{3,2},{4,5},{5,4},{6,7},{7,6},{8,9},{9,8},{10,11... | collective-permute-start | bytes 589832 | tf_op jit(solution)/shard_map/ppermute | solution.py:81
  79.1 2.4 %shard_map.52 = (f32[864,384]{1,0:T(8,128)S(1)}, f32[3,8,32,128]{3,2,1,0:T(8,128)S(1)}, bf16[1,3,8,32,128]{4,3,2,1,0:T(8,128)(2,1)S(1)}) custom-call(s32[16,96]{1,0:T(8,128)S(1)} %pad_add_fusion.lists_ref, f32[864,384]{1,0:T(8,128)S(1)} %shard_map.51.acc_in, bf16[3,16,32,128]{3,2,1,0:T(8,128)(2,1)S(1)} %collective-permute-done.21.z, ...), custom_call_target="tpu_custom_call", output_to_operand_aliasing={{0}: (1, {})} | custom-call | tf_op jit(solution)/shard_map/pallas_call | solution.py:26
  81.6 1.6 %collective-permute-start.24 = (bf16[3,8,32,128]{3,2,1,0:T(8,128)(2,1)S(1)}, bf16[3,8,32,128]{3,2,1,0:T(8,128)(2,1)S(1)}, u32[]{:S(2)}, u32[]{:S(2)}) collective-permute-start(bf16[3,8,32,128]{3,2,1,0:T(8,128)(2,1)S(1)} %bitcast.17), channel_id=1, source_target_pairs={{0,1},{1,0},{2,3},{3,2},{4,5},{5,4},{6,7},{7,6},{8,9},{9,8},{10,11... | collective-permute-start | bytes 589832 | tf_op jit(solution)/shard_map/ppermute | solution.py:81
  83.2 1.9 %collective-permute-done.23 = bf16[3,8,32,128]{3,2,1,0:T(8,128)(2,1)S(1)} collective-permute-done((bf16[3,8,32,128]{3,2,1,0:T(8,128)(2,1)S(1)}, bf16[3,8,32,128]{3,2,1,0:T(8,128)(2,1)S(1)}, u32[]{:S(2)}, u32[]{:S(2)}) %collective-permute-start.23) | collective-permute-done | bytes 196640 | tf_op jit(solution)/shard_map/ppermute | solution.py:81
  85.1 3.8 %collective-permute-done.24 = bf16[3,8,32,128]{3,2,1,0:T(8,128)(2,1)S(1)} collective-permute-done((bf16[3,8,32,128]{3,2,1,0:T(8,128)(2,1)S(1)}, bf16[3,8,32,128]{3,2,1,0:T(8,128)(2,1)S(1)}, u32[]{:S(2)}, u32[]{:S(2)}) %collective-permute-start.24) | collective-permute-done | bytes 196640 | tf_op jit(solution)/shard_map/ppermute | solution.py:81
  88.9 1.7 %shard_map.53 = f32[3,8,128,128]{3,2,1,0:T(8,128)} custom-call(f32[3,8,32,128]{3,2,1,0:T(8,128)S(1)} %get-tuple-element.42.refs_0_, f32[3,8,32,128]{3,2,1,0:T(8,128)S(1)} %get-tuple-element.47.refs_1_, bf16[1,3,8,32,128]{4,3,2,1,0:T(8,128)(2,1)S(1)} %bitcast.14, bf16[1,3,8,32,128]{4,3,2,1,0:T(8,128)(2,1)S(1)} %bitcast.15), custom_call_target="tpu_custom_call" | custom-call | tf_op jit(solution)/shard_map/pallas_call | solution.py:26
  (44 shorter events, 16.2 us)
Async XLA Ops:
  1.5 7.9 %collective-permute-start = (bf16[3,8,32,128]{3,2,1,0:T(8,128)(2,1)S(1)}, bf16[3,8,32,128]{3,2,1,0:T(8,128)(2,1)S(1)}, u32[]{:S(2)}, u32[]{:S(2)}) collective-permute-start(bf16[3,8,32,128]{3,2,1,0:T(8,128)(2,1)S(1)} %bitcast.10), channel_id=1, source_target_pairs={{0,1},{1,0},{2,3},{3,2},{4,5},{5,4},{6,7},{7,6},{8,9},{9,8},{10,11... | collective-permute-start | bytes 589832 | tf_op jit(solution)/shard_map/ppermute | solution.py:81
  10.3 10.5 %collective-permute-start.2 = (bf16[480,384]{1,0:T(8,128)(2,1)S(1)}, bf16[480,384]{1,0:T(8,128)(2,1)S(1)}, u32[]{:S(2)}, u32[]{:S(2)}) collective-permute-start(bf16[480,384]{1,0:T(8,128)(2,1)S(1)} %shard_map.39.refs_0_.w), channel_id=1, source_target_pairs={{0,4},{2,6},{4,0},{6,2},{8,12},{10,14},{12,8},{14,10},{16,20},{18,... | collective-permute-start | bytes 1105928 | tf_op jit(solution)/shard_map/ppermute | solution.py:81
  12.1 7.8 %collective-permute-start.5 = (bf16[3,8,32,128]{3,2,1,0:T(8,128)(2,1)S(1)}, bf16[3,8,32,128]{3,2,1,0:T(8,128)(2,1)S(1)}, u32[]{:S(2)}, u32[]{:S(2)}) collective-permute-start(bf16[3,8,32,128]{3,2,1,0:T(8,128)(2,1)S(1)} %bitcast.11), channel_id=1, source_target_pairs={{0,1},{1,0},{2,3},{3,2},{4,5},{5,4},{6,7},{7,6},{8,9},{9,8},{10,11... | collective-permute-start | bytes 589832 | tf_op jit(solution)/shard_map/ppermute | solution.py:81
  13.6 12.6 %collective-permute-start.4 = (bf16[3,8,64,128]{3,2,1,0:T(8,128)(2,1)S(1)}, bf16[3,8,64,128]{3,2,1,0:T(8,128)(2,1)S(1)}, u32[]{:S(2)}, u32[]{:S(2)}) collective-permute-start(bf16[3,8,64,128]{3,2,1,0:T(8,128)(2,1)S(1)} %get-tuple-element.31.mine_ref), channel_id=1, source_target_pairs={{0,1},{1,0},{2,3},{3,2},{4,5},{5,4},{6,7},{7,6},{8,9},{9,8},{10,11... | collective-permute-start | bytes 1179656 | tf_op jit(solution)/shard_map/ppermute | solution.py:81
  14.1 13.1 %collective-permute-start.1 = (bf16[480,384]{1,0:T(8,128)(2,1)S(1)}, bf16[480,384]{1,0:T(8,128)(2,1)S(1)}, u32[]{:S(2)}, u32[]{:S(2)}) collective-permute-start(bf16[480,384]{1,0:T(8,128)(2,1)S(1)} %shard_map.39.refs_0_.w), channel_id=1, source_target_pairs={{0,2},{2,0},{4,6},{6,4},{8,10},{10,8},{12,14},{14,12},{16,18},{18,... | collective-permute-start | bytes 1105928 | tf_op jit(solution)/shard_map/ppermute | solution.py:81
  20.8 6.5 %collective-permute-start.3 = (bf16[480,384]{1,0:T(8,128)(2,1)S(1)}, bf16[480,384]{1,0:T(8,128)(2,1)S(1)}, u32[]{:S(2)}, u32[]{:S(2)}) collective-permute-start(bf16[480,384]{1,0:T(8,128)(2,1)S(1)} %collective-permute-done.2.x), channel_id=1, source_target_pairs={{0,2},{2,0},{4,6},{6,4},{8,10},{10,8},{12,14},{14,12},{16,18},{18,... | collective-permute-start | bytes 1105928 | tf_op jit(solution)/shard_map/ppermute | solution.py:81
  20.9 12.8 %collective-permute-start.6 = (bf16[480,384]{1,0:T(8,128)(2,1)S(1)}, bf16[480,384]{1,0:T(8,128)(2,1)S(1)}, u32[]{:S(2)}, u32[]{:S(2)}) collective-permute-start(bf16[480,384]{1,0:T(8,128)(2,1)S(1)} %collective-permute-done.2.x), channel_id=1, source_target_pairs={{0,8},{2,10},{4,28},{6,30},{8,16},{10,18},{12,4},{14,6},{16,24},{1... | collective-permute-start | bytes 1105928 | tf_op jit(solution)/shard_map/ppermute | solution.py:81
  22.5 11.7 %collective-permute-start.10 = (bf16[480,384]{1,0:T(8,128)(2,1)S(1)}, bf16[480,384]{1,0:T(8,128)(2,1)S(1)}, u32[]{:S(2)}, u32[]{:S(2)}) collective-permute-start(bf16[480,384]{1,0:T(8,128)(2,1)S(1)} %shard_map.41.refs_1_.w), channel_id=1, source_target_pairs={{0,4},{2,6},{4,0},{6,2},{8,12},{10,14},{12,8},{14,10},{16,20},{18,... | collective-permute-start | bytes 1105928 | tf_op jit(solution)/shard_map/ppermute | solution.py:81
  33.7 1.7 %collective-permute-start.7 = (bf16[480,384]{1,0:T(8,128)(2,1)S(1)}, bf16[480,384]{1,0:T(8,128)(2,1)S(1)}, u32[]{:S(2)}, u32[]{:S(2)}) collective-permute-start(bf16[480,384]{1,0:T(8,128)(2,1)S(1)} %collective-permute-done.6.z), channel_id=1, source_target_pairs={{0,2},{2,0},{4,6},{6,4},{8,10},{10,8},{12,14},{14,12},{16,18},{18,... | collective-permute-start | bytes 1105928 | tf_op jit(solution)/shard_map/ppermute | solution.py:81
  33.7 6.1 %collective-permute-start.9 = (bf16[480,384]{1,0:T(8,128)(2,1)S(1)}, bf16[480,384]{1,0:T(8,128)(2,1)S(1)}, u32[]{:S(2)}, u32[]{:S(2)}) collective-permute-start(bf16[480,384]{1,0:T(8,128)(2,1)S(1)} %shard_map.41.refs_1_.w), channel_id=1, source_target_pairs={{0,2},{2,0},{4,6},{6,4},{8,10},{10,8},{12,14},{14,12},{16,18},{18,... | collective-permute-start | bytes 1105928 | tf_op jit(solution)/shard_map/ppermute | solution.py:81
  34.2 5.6 %collective-permute-start.11 = (bf16[480,384]{1,0:T(8,128)(2,1)S(1)}, bf16[480,384]{1,0:T(8,128)(2,1)S(1)}, u32[]{:S(2)}, u32[]{:S(2)}) collective-permute-start(bf16[480,384]{1,0:T(8,128)(2,1)S(1)} %collective-permute-done.10.x), channel_id=1, source_target_pairs={{0,2},{2,0},{4,6},{6,4},{8,10},{10,8},{12,14},{14,12},{16,18},{18,... | collective-permute-start | bytes 1105928 | tf_op jit(solution)/shard_map/ppermute | solution.py:81
  34.2 12.8 %collective-permute-start.12 = (bf16[480,384]{1,0:T(8,128)(2,1)S(1)}, bf16[480,384]{1,0:T(8,128)(2,1)S(1)}, u32[]{:S(2)}, u32[]{:S(2)}) collective-permute-start(bf16[480,384]{1,0:T(8,128)(2,1)S(1)} %collective-permute-done.10.x), channel_id=1, source_target_pairs={{0,8},{2,10},{4,28},{6,30},{8,16},{10,18},{12,4},{14,6},{16,24},{1... | collective-permute-start | bytes 1105928 | tf_op jit(solution)/shard_map/ppermute | solution.py:81
  37.0 13.4 %collective-permute-start.14 = (bf16[3,16,32,128]{3,2,1,0:T(8,128)(2,1)S(1)}, bf16[3,16,32,128]{3,2,1,0:T(8,128)(2,1)S(1)}, u32[]{:S(2)}, u32[]{:S(2)}) collective-permute-start(bf16[3,16,32,128]{3,2,1,0:T(8,128)(2,1)S(1)} %get-tuple-element.35.w), channel_id=1, source_target_pairs={{0,4},{2,6},{4,0},{6,2},{8,12},{10,14},{12,8},{14,10},{16,20},{18,... | collective-permute-start | bytes 1179656 | tf_op jit(solution)/shard_map/ppermute | solution.py:81
  47.0 4.0 %collective-permute-start.8 = (bf16[3,16,32,128]{3,2,1,0:T(8,128)(2,1)S(1)}, bf16[3,16,32,128]{3,2,1,0:T(8,128)(2,1)S(1)}, u32[]{:S(2)}, u32[]{:S(2)}) collective-permute-start(bf16[3,16,32,128]{3,2,1,0:T(8,128)(2,1)S(1)} %get-tuple-element.35.w), channel_id=1, source_target_pairs={{0,2},{2,0},{4,6},{6,4},{8,10},{10,8},{12,14},{14,12},{16,18},{18,... | collective-permute-start | bytes 1179656 | tf_op jit(solution)/shard_map/ppermute | solution.py:81
  50.4 10.8 %collective-permute-start.19 = (bf16[3,16,32,128]{3,2,1,0:T(8,128)(2,1)S(1)}, bf16[3,16,32,128]{3,2,1,0:T(8,128)(2,1)S(1)}, u32[]{:S(2)}, u32[]{:S(2)}) collective-permute-start(bf16[3,16,32,128]{3,2,1,0:T(8,128)(2,1)S(1)} %get-tuple-element.38.w), channel_id=1, source_target_pairs={{0,4},{2,6},{4,0},{6,2},{8,12},{10,14},{12,8},{14,10},{16,20},{18,... | collective-permute-start | bytes 1179656 | tf_op jit(solution)/shard_map/ppermute | solution.py:81
  50.4 10.8 %collective-permute-start.15 = (bf16[3,16,32,128]{3,2,1,0:T(8,128)(2,1)S(1)}, bf16[3,16,32,128]{3,2,1,0:T(8,128)(2,1)S(1)}, u32[]{:S(2)}, u32[]{:S(2)}) collective-permute-start(bf16[3,16,32,128]{3,2,1,0:T(8,128)(2,1)S(1)} %collective-permute-done.14.x), channel_id=1, source_target_pairs={{0,2},{2,0},{4,6},{6,4},{8,10},{10,8},{12,14},{14,12},{16,18},{18,... | collective-permute-start | bytes 1179656 | tf_op jit(solution)/shard_map/ppermute | solution.py:81
  50.5 13.5 %collective-permute-start.16 = (bf16[3,16,32,128]{3,2,1,0:T(8,128)(2,1)S(1)}, bf16[3,16,32,128]{3,2,1,0:T(8,128)(2,1)S(1)}, u32[]{:S(2)}, u32[]{:S(2)}) collective-permute-start(bf16[3,16,32,128]{3,2,1,0:T(8,128)(2,1)S(1)} %collective-permute-done.14.x), channel_id=1, source_target_pairs={{0,8},{2,10},{4,28},{6,30},{8,16},{10,18},{12,4},{14,6},{16,24},{1... | collective-permute-start | bytes 1179656 | tf_op jit(solution)/shard_map/ppermute | solution.py:81
  50.6 13.5 %collective-permute-start.18 = (bf16[3,16,32,128]{3,2,1,0:T(8,128)(2,1)S(1)}, bf16[3,16,32,128]{3,2,1,0:T(8,128)(2,1)S(1)}, u32[]{:S(2)}, u32[]{:S(2)}) collective-permute-start(bf16[3,16,32,128]{3,2,1,0:T(8,128)(2,1)S(1)} %get-tuple-element.38.w), channel_id=1, source_target_pairs={{0,2},{2,0},{4,6},{6,4},{8,10},{10,8},{12,14},{14,12},{16,18},{18,... | collective-permute-start | bytes 1179656 | tf_op jit(solution)/shard_map/ppermute | solution.py:81
  61.2 4.9 %collective-permute-start.20 = (bf16[3,16,32,128]{3,2,1,0:T(8,128)(2,1)S(1)}, bf16[3,16,32,128]{3,2,1,0:T(8,128)(2,1)S(1)}, u32[]{:S(2)}, u32[]{:S(2)}) collective-permute-start(bf16[3,16,32,128]{3,2,1,0:T(8,128)(2,1)S(1)} %collective-permute-done.19.x), channel_id=1, source_target_pairs={{0,2},{2,0},{4,6},{6,4},{8,10},{10,8},{12,14},{14,12},{16,18},{18,... | collective-permute-start | bytes 1179656 | tf_op jit(solution)/shard_map/ppermute | solution.py:81
  64.1 3.4 %collective-permute-start.17 = (bf16[3,16,32,128]{3,2,1,0:T(8,128)(2,1)S(1)}, bf16[3,16,32,128]{3,2,1,0:T(8,128)(2,1)S(1)}, u32[]{:S(2)}, u32[]{:S(2)}) collective-permute-start(bf16[3,16,32,128]{3,2,1,0:T(8,128)(2,1)S(1)} %collective-permute-done.16.z), channel_id=1, source_target_pairs={{0,2},{2,0},{4,6},{6,4},{8,10},{10,8},{12,14},{14,12},{16,18},{18,... | collective-permute-start | bytes 1179656 | tf_op jit(solution)/shard_map/ppermute | solution.py:81
  64.1 13.3 %collective-permute-start.21 = (bf16[3,16,32,128]{3,2,1,0:T(8,128)(2,1)S(1)}, bf16[3,16,32,128]{3,2,1,0:T(8,128)(2,1)S(1)}, u32[]{:S(2)}, u32[]{:S(2)}) collective-permute-start(bf16[3,16,32,128]{3,2,1,0:T(8,128)(2,1)S(1)} %collective-permute-done.19.x), channel_id=1, source_target_pairs={{0,8},{2,10},{4,28},{6,30},{8,16},{10,18},{12,4},{14,6},{16,24},{1... | collective-permute-start | bytes 1179656 | tf_op jit(solution)/shard_map/ppermute | solution.py:81
  77.4 1.7 %collective-permute-start.22 = (bf16[3,16,32,128]{3,2,1,0:T(8,128)(2,1)S(1)}, bf16[3,16,32,128]{3,2,1,0:T(8,128)(2,1)S(1)}, u32[]{:S(2)}, u32[]{:S(2)}) collective-permute-start(bf16[3,16,32,128]{3,2,1,0:T(8,128)(2,1)S(1)} %collective-permute-done.21.z), channel_id=1, source_target_pairs={{0,2},{2,0},{4,6},{6,4},{8,10},{10,8},{12,14},{14,12},{16,18},{18,... | collective-permute-start | bytes 1179656 | tf_op jit(solution)/shard_map/ppermute | solution.py:81
  77.4 7.7 %collective-permute-start.23 = (bf16[3,8,32,128]{3,2,1,0:T(8,128)(2,1)S(1)}, bf16[3,8,32,128]{3,2,1,0:T(8,128)(2,1)S(1)}, u32[]{:S(2)}, u32[]{:S(2)}) collective-permute-start(bf16[3,8,32,128]{3,2,1,0:T(8,128)(2,1)S(1)} %bitcast.16), channel_id=1, source_target_pairs={{0,1},{1,0},{2,3},{3,2},{4,5},{5,4},{6,7},{7,6},{8,9},{9,8},{10,11... | collective-permute-start | bytes 589832 | tf_op jit(solution)/shard_map/ppermute | solution.py:81
  81.6 7.4 %collective-permute-start.24 = (bf16[3,8,32,128]{3,2,1,0:T(8,128)(2,1)S(1)}, bf16[3,8,32,128]{3,2,1,0:T(8,128)(2,1)S(1)}, u32[]{:S(2)}, u32[]{:S(2)}) collective-permute-start(bf16[3,8,32,128]{3,2,1,0:T(8,128)(2,1)S(1)} %bitcast.17), channel_id=1, source_target_pairs={{0,1},{1,0},{2,3},{3,2},{4,5},{5,4},{6,7},{7,6},{8,9},{9,8},{10,11... | collective-permute-start | bytes 589832 | tf_op jit(solution)/shard_map/ppermute | solution.py:81
  (1 other events, 1.7 us)

commit v6 on v5

--- a/solution.py
+++ b/solution.py
@@ -14,7 +14,7 @@
 PARAMS = pltpu.CompilerParams(vmem_limit_bytes=16 * 1024 * 1024)
 
 
-def call(kernel, ins, outs, scratch=(), aliases=None, hbm_in=False, hbm_out=False):
+def call(kernel, ins, outs, scratch=(), aliases=None, hbm_in=False, hbm_out=False, us=0):
     here = HBM if hbm_in else VMEM
     specs = [SMEM if x.dtype == jnp.int32 else here for x in ins]
     if not hbm_out:
@@ -31,6 +31,7 @@
         scratch_shapes=list(scratch),
         input_output_aliases=aliases or {},
         compiler_params=PARAMS,
+        cost_estimate=us and pl.CostEstimate(flops=int(us * 1.1e9), transcendentals=0, bytes_accessed=1024) or None,
     )(*ins)
 
 
@@ -194,17 +195,13 @@
     else:
         left = lax.all_gather(p_blocks, "inner", axis=0)
     own = [
-        call(end_rows, [lists, own[c], got[c]], [rows_shapes[c]], aliases={1: 0})[0]
+        call(end_rows, [lists, own[c], got[c]], [rows_shapes[c]], aliases={1: 0}, us=20 * c)[0]
         for c in chunks
     ]
     if n == 2:
-        (band,) = call(end_band, [lists, band, left, *own], [band_shape], aliases={1: 0})
+        (band,) = call(end_band, [lists, band, left, *own], [band_shape], aliases={1: 0}, us=20)
     else:
         (band,) = call(whole_band, [lists, left], [band_shape])
-
-    def moved(v, *first):
-        x = send(v, flip_x)
-        return x, send(after(x, *first), move_z)
 
     def weights(left_ref, d):
         return left_ref[rows_at(d + REACH, width), :]
@@ -246,18 +243,6 @@
                 value = acc_ref[kept(lists_ref, i, v, sq_ref.shape[2]), pl.ds(i * bs, bs)]
                 sq_ref[i, v] = value
                 low_ref[i, v] = value.astype(bf16)
-
-    def square(c, w, x, z, lead):
-        kept_shape, acc_shape = (rb, fill, sizes[c], bs), acc_shapes[c]
-        u, cx = send(w, flip_core), send(x, flip_core)
-        (acc,) = call(square_near, [after(w, *lead), u, x, cx, band], [acc_shape])
-        z = after(z, acc)
-        return call(
-            square_far,
-            [lists, acc, z, send(z, flip_core), band],
-            [acc_shape, shape(kept_shape, f32), shape(kept_shape, bf16)],
-            aliases={1: 0},
-        )[1:]
 
     def kept(lists_ref, i, v, cols):
         o = lax.axis_index("rows")
@@ -318,22 +303,37 @@
 
     dense = [[pltpu.VMEM(((WIDE * rb + 1) * k, width), bf16)] for k in sizes]
     x, z, sq, low, x2, z2 = [], [], [], [], [], []
+    close = []
     for c in chunks:
-        x_c, z_c = moved(own[c], *own[c + 1 : c + 2])
-        one = square(c, own[c], x_c, z_c, low)
-        sq.append(one[0])
-        low.append(one[1])
+        u = send(own[c], flip_core)
+        x_c = after(send(own[c], flip_x), *own[c + 1 : c + 2], *close)
+        z.append(send(x_c, move_z))
+        cx = send(x_c, flip_core)
+        close += call(square_near, [own[c], u, x_c, cx, band], [acc_shapes[c]], us=20 * c or 20)
+        x.append(x_c)
+    for c in chunks:
+        z_c = after(z[c], close[c], *x[c + 1 : c + 2])
+        cz = after(send(z_c, flip_core), *close[c + 1 : c + 2])
+        kept_shape = (rb, fill, sizes[c], bs)
+        one = call(
+            square_far,
+            [lists, close[c], z_c, cz, band],
+            [acc_shapes[c], shape(kept_shape, f32), shape(kept_shape, bf16)],
+            aliases={1: 0},
+        )
+        sq.append(one[1])
+        low.append(one[2])
     keep, give, near = [], [], []
     for c in chunks:
         x_c = send(low[c], flip_x)
         u = send(low[c], flip_core)
         (acc,) = call(
-            cube_own, [lists, low[c], u, after(band, low[-1], *near)], [acc_shapes[c]], dense[c]
+            cube_own, [lists, low[c], u, after(band, low[-1], *near)], [acc_shapes[c]], dense[c], us=20 * c
         )
         x2.append(x_c)
         z2.append(send(x_c, move_z))
         cx = send(x_c, flip_core)
-        (acc,) = call(cube_near, [lists, acc, x_c, cx, band], [acc_shapes[c]], dense[c], aliases={1: 0})
+        (acc,) = call(cube_near, [lists, acc, x_c, cx, band], [acc_shapes[c]], dense[c], aliases={1: 0}, us=20 * c)
         near.append(acc)
     for c in chunks:
         z_c = after(z2[c], near[c], *give)

time: 91 us -> 82.2 us (0.903)
  waiting for transfers between devices: 45.9 us -> 39.2 us
  starting transfers between devices: 19.2 us -> 17.1 us
    ppermute x25, waiting for transfers between devices: 45.9 us -> 39.2 us  [send(): return lax.ppermute(x, axis, pairs)]
    ppermute x25, starting transfers between devices: 19.2 us -> 17.1 us  [send(): return lax.ppermute(x, axis, pairs)]
  transfers between devices with their start and end apart: 25 -> 25, of which waited for: 12 -> 15; matrix products, arithmetic and copies ran while one was open for 1% -> 1% of each run, Pallas kernels for 23% -> 26%
where the time goes in v6:
time: 82.2 us; the launch traced here: 82 us
  waiting for transfers between devices  39.2 us (48%)
  Pallas kernels  24.7 us (30%)
  starting transfers between devices  17.1 us (21%)
    ppermute x25, waiting for transfers between devices, send(): return lax.ppermute(x, axis, pairs)  39.2 us
    pallas_call x17, Pallas kernels, call(): pl.pallas_call(kernel, out_shape=tuple(outs), in_specs=specs, out_specs=t...  24.7 us
    ppermute x25, starting transfers between devices, send(): return lax.ppermute(x, axis, pairs)  17.1 us
  transfers between devices with their start and end apart: 25, of which 15 were waited for; matrix products, arithmetic and copies ran while one was open for 1% of the time, Pallas kernels for 26%

profile of v6, /device:TPU:0, one launch (start us, length us, event | category | flops | bytes accessed | tf_op | source)
XLA Modules:
  0.0 82.0 jit_solution(15059358326980829034)
XLA Ops:
  1.5 3.0 %collective-permute-start = (bf16[3,8,32,128]{3,2,1,0:T(8,128)(2,1)S(1)}, bf16[3,8,32,128]{3,2,1,0:T(8,128)(2,1)S(1)}, u32[]{:S(2)}, u32[]{:S(2)}) collective-permute-start(bf16[3,8,32,128]{3,2,1,0:T(8,128)(2,1)S(1)} %bitcast.11), channel_id=1, source_target_pairs={{0,1},{1,0},{2,3},{3,2},{4,5},{5,4},{6,7},{7,6},{8,9},{9,8},{10,11... | collective-permute-start | bytes 589832 | tf_op jit(solution)/shard_map/ppermute | solution.py:82
  7.4 2.9 %collective-permute-done = bf16[3,8,32,128]{3,2,1,0:T(8,128)(2,1)S(1)} collective-permute-done((bf16[3,8,32,128]{3,2,1,0:T(8,128)(2,1)S(1)}, bf16[3,8,32,128]{3,2,1,0:T(8,128)(2,1)S(1)}, u32[]{:S(2)}, u32[]{:S(2)}) %collective-permute-start) | collective-permute-done | bytes 196640 | tf_op jit(solution)/shard_map/ppermute | solution.py:82
  11.1 2.1 %collective-permute-start.2 = (bf16[480,384]{1,0:T(8,128)(2,1)S(1)}, bf16[480,384]{1,0:T(8,128)(2,1)S(1)}, u32[]{:S(2)}, u32[]{:S(2)}) collective-permute-start(bf16[480,384]{1,0:T(8,128)(2,1)S(1)} %shard_map.39.refs_0_.w), channel_id=1, source_target_pairs={{0,4},{2,6},{4,0},{6,2},{8,12},{10,14},{12,8},{14,10},{16,20},{18,... | collective-permute-start | bytes 1105928 | tf_op jit(solution)/shard_map/ppermute | solution.py:82
  13.2 1.5 %collective-permute-start.5 = (bf16[3,8,64,128]{3,2,1,0:T(8,128)(2,1)S(1)}, bf16[3,8,64,128]{3,2,1,0:T(8,128)(2,1)S(1)}, u32[]{:S(2)}, u32[]{:S(2)}) collective-permute-start(bf16[3,8,64,128]{3,2,1,0:T(8,128)(2,1)S(1)} %get-tuple-element.34.mine_ref), channel_id=1, source_target_pairs={{0,1},{1,0},{2,3},{3,2},{4,5},{5,4},{6,7},{7,6},{8,9},{9,8},{10,11... | collective-permute-start | bytes 1179656 | tf_op jit(solution)/shard_map/ppermute | solution.py:82
  16.3 5.4 %collective-permute-done.2.x = bf16[480,384]{1,0:T(8,128)(2,1)S(1)} collective-permute-done((bf16[480,384]{1,0:T(8,128)(2,1)S(1)}, bf16[480,384]{1,0:T(8,128)(2,1)S(1)}, u32[]{:S(2)}, u32[]{:S(2)}) %collective-permute-start.2) | collective-permute-done | bytes 368672 | tf_op jit(solution)/shard_map/ppermute | solution.py:82
  23.1 1.7 %collective-permute-done.5.left_ref = bf16[3,8,64,128]{3,2,1,0:T(8,128)(2,1)S(1)} collective-permute-done((bf16[3,8,64,128]{3,2,1,0:T(8,128)(2,1)S(1)}, bf16[3,8,64,128]{3,2,1,0:T(8,128)(2,1)S(1)}, u32[]{:S(2)}, u32[]{:S(2)}) %collective-permute-start.5) | collective-permute-done | bytes 393248 | tf_op jit(solution)/shard_map/ppermute | solution.py:82
  29.5 1.5 %collective-permute-done.6.z = bf16[480,384]{1,0:T(8,128)(2,1)S(1)} collective-permute-done((bf16[480,384]{1,0:T(8,128)(2,1)S(1)}, bf16[480,384]{1,0:T(8,128)(2,1)S(1)}, u32[]{:S(2)}, u32[]{:S(2)}) %collective-permute-start.6) | collective-permute-done | bytes 368672 | tf_op jit(solution)/shard_map/ppermute | solution.py:82
  32.7 1.6 %shard_map.45 = (f32[864,384]{1,0:T(8,128)S(1)}, f32[3,16,32,128]{3,2,1,0:T(8,128)S(1)}, bf16[3,16,32,128]{3,2,1,0:T(8,128)(2,1)S(1)}) custom-call(s32[16,96]{1,0:T(8,128)S(1)} %pad_add_fusion.lists_ref, f32[864,384]{1,0:T(8,128)S(1)} %shard_map.43.acc_in, bf16[480,384]{1,0:T(8,128)(2,1)S(1)} %collective-permute-done.6.z, ...), custom_call_target="tpu_custom_call", output_to_operand_aliasing={{0}: (1, {})} | custom-call | tf_op jit(solution)/shard_map/pallas_call | solution.py:26
  34.4 1.7 %collective-permute-start.14 = (bf16[3,16,32,128]{3,2,1,0:T(8,128)(2,1)S(1)}, bf16[3,16,32,128]{3,2,1,0:T(8,128)(2,1)S(1)}, u32[]{:S(2)}, u32[]{:S(2)}) collective-permute-start(bf16[3,16,32,128]{3,2,1,0:T(8,128)(2,1)S(1)} %get-tuple-element.38.w), channel_id=1, source_target_pairs={{0,4},{2,6},{4,0},{6,2},{8,12},{10,14},{12,8},{14,10},{16,20},{18,... | collective-permute-start | bytes 1179656 | tf_op jit(solution)/shard_map/ppermute | solution.py:82
  36.1 4.8 %collective-permute-done.12.z = bf16[480,384]{1,0:T(8,128)(2,1)S(1)} collective-permute-done((bf16[480,384]{1,0:T(8,128)(2,1)S(1)}, bf16[480,384]{1,0:T(8,128)(2,1)S(1)}, u32[]{:S(2)}, u32[]{:S(2)}) %collective-permute-start.12) | collective-permute-done | bytes 368672 | tf_op jit(solution)/shard_map/ppermute | solution.py:82
  42.5 1.6 %shard_map.46 = (f32[864,384]{1,0:T(8,128)S(1)}, f32[3,16,32,128]{3,2,1,0:T(8,128)S(1)}, bf16[3,16,32,128]{3,2,1,0:T(8,128)(2,1)S(1)}) custom-call(s32[16,96]{1,0:T(8,128)S(1)} %pad_add_fusion.lists_ref, f32[864,384]{1,0:T(8,128)S(1)} %shard_map.44.acc_in, bf16[480,384]{1,0:T(8,128)(2,1)S(1)} %collective-permute-done.12.z, ...), custom_call_target="tpu_custom_call", output_to_operand_aliasing={{0}: (1, {})} | custom-call | tf_op jit(solution)/shard_map/pallas_call | solution.py:26
  46.5 2.0 %shard_map.47.acc_in = f32[864,384]{1,0:T(8,128)S(1)} custom-call(s32[16,96]{1,0:T(8,128)S(1)} %pad_add_fusion.lists_ref, bf16[3,16,32,128]{3,2,1,0:T(8,128)(2,1)S(1)} %get-tuple-element.38.w, bf16[3,16,32,128]{3,2,1,0:T(8,128)(2,1)S(1)} %collective-permute-done.11.u, bf16[1920,384]{1,0:T(8,128)(2,1)S(1)} %shard_map.42.left_ref), custom_call_target="tpu_custom_call" | custom-call | tf_op jit(solution)/shard_map/pallas_call | solution.py:26
  48.4 6.6 %collective-permute-done.19.x = bf16[3,16,32,128]{3,2,1,0:T(8,128)(2,1)S(1)} collective-permute-done((bf16[3,16,32,128]{3,2,1,0:T(8,128)(2,1)S(1)}, bf16[3,16,32,128]{3,2,1,0:T(8,128)(2,1)S(1)}, u32[]{:S(2)}, u32[]{:S(2)}) %collective-permute-start.19) | collective-permute-done | bytes 393248 | tf_op jit(solution)/shard_map/ppermute | solution.py:82
  55.0 1.6 %shard_map.48.acc_in = f32[864,384]{1,0:T(8,128)S(1)} custom-call(s32[16,96]{1,0:T(8,128)S(1)} %pad_add_fusion.lists_ref, f32[864,384]{1,0:T(8,128)S(1)} %shard_map.47.acc_in, bf16[3,16,32,128]{3,2,1,0:T(8,128)(2,1)S(1)} %collective-permute-done.14.x, bf16[3,16,32,128]{3,2,1,0:T(8,128)(2,1)S(1)} %collective-permute-done.15.cx, ...), custom_call_target="tpu_custom_call", output_to_operand_aliasing={{}: (1, {})} | custom-call | tf_op jit(solution)/shard_map/pallas_call | solution.py:26
  56.7 2.8 %collective-permute-done.16.z = bf16[3,16,32,128]{3,2,1,0:T(8,128)(2,1)S(1)} collective-permute-done((bf16[3,16,32,128]{3,2,1,0:T(8,128)(2,1)S(1)}, bf16[3,16,32,128]{3,2,1,0:T(8,128)(2,1)S(1)}, u32[]{:S(2)}, u32[]{:S(2)}) %collective-permute-start.16) | collective-permute-done | bytes 393248 | tf_op jit(solution)/shard_map/ppermute | solution.py:82
  59.5 2.0 %shard_map.50.acc_in = f32[864,384]{1,0:T(8,128)S(1)} custom-call(s32[16,96]{1,0:T(8,128)S(1)} %pad_add_fusion.lists_ref, bf16[3,16,32,128]{3,2,1,0:T(8,128)(2,1)S(1)} %get-tuple-element.40.w, bf16[3,16,32,128]{3,2,1,0:T(8,128)(2,1)S(1)} %collective-permute-done.18.u, bf16[1920,384]{1,0:T(8,128)(2,1)S(1)} %shard_map.42.left_ref), custom_call_target="tpu_custom_call" | custom-call | flops 22000001024 | bytes 1024 | tf_op jit(solution)/shard_map/pallas_call | solution.py:26
  62.9 2.4 %shard_map.49 = (f32[864,384]{1,0:T(8,128)S(1)}, f32[3,8,32,128]{3,2,1,0:T(8,128)S(1)}, bf16[1,3,8,32,128]{4,3,2,1,0:T(8,128)(2,1)S(1)}) custom-call(s32[16,96]{1,0:T(8,128)S(1)} %pad_add_fusion.lists_ref, f32[864,384]{1,0:T(8,128)S(1)} %shard_map.48.acc_in, bf16[3,16,32,128]{3,2,1,0:T(8,128)(2,1)S(1)} %collective-permute-done.16.z, ...), custom_call_target="tpu_custom_call", output_to_operand_aliasing={{0}: (1, {})} | custom-call | tf_op jit(solution)/shard_map/pallas_call | solution.py:26
  65.4 3.1 %collective-permute-done.21.z = bf16[3,16,32,128]{3,2,1,0:T(8,128)(2,1)S(1)} collective-permute-done((bf16[3,16,32,128]{3,2,1,0:T(8,128)(2,1)S(1)}, bf16[3,16,32,128]{3,2,1,0:T(8,128)(2,1)S(1)}, u32[]{:S(2)}, u32[]{:S(2)}) %collective-permute-start.21) | collective-permute-done | bytes 393248 | tf_op jit(solution)/shard_map/ppermute | solution.py:82
  68.4 1.9 %collective-permute-start.23 = (bf16[3,8,32,128]{3,2,1,0:T(8,128)(2,1)S(1)}, bf16[3,8,32,128]{3,2,1,0:T(8,128)(2,1)S(1)}, u32[]{:S(2)}, u32[]{:S(2)}) collective-permute-start(bf16[3,8,32,128]{3,2,1,0:T(8,128)(2,1)S(1)} %bitcast.15), channel_id=1, source_target_pairs={{0,1},{1,0},{2,3},{3,2},{4,5},{5,4},{6,7},{7,6},{8,9},{9,8},{10,11... | collective-permute-start | bytes 589832 | tf_op jit(solution)/shard_map/ppermute | solution.py:82
  70.4 2.4 %shard_map.52 = (f32[864,384]{1,0:T(8,128)S(1)}, f32[3,8,32,128]{3,2,1,0:T(8,128)S(1)}, bf16[1,3,8,32,128]{4,3,2,1,0:T(8,128)(2,1)S(1)}) custom-call(s32[16,96]{1,0:T(8,128)S(1)} %pad_add_fusion.lists_ref, f32[864,384]{1,0:T(8,128)S(1)} %shard_map.51.acc_in, bf16[3,16,32,128]{3,2,1,0:T(8,128)(2,1)S(1)} %collective-permute-done.21.z, ...), custom_call_target="tpu_custom_call", output_to_operand_aliasing={{0}: (1, {})} | custom-call | tf_op jit(solution)/shard_map/pallas_call | solution.py:26
  72.8 1.8 %collective-permute-start.24 = (bf16[3,8,32,128]{3,2,1,0:T(8,128)(2,1)S(1)}, bf16[3,8,32,128]{3,2,1,0:T(8,128)(2,1)S(1)}, u32[]{:S(2)}, u32[]{:S(2)}) collective-permute-start(bf16[3,8,32,128]{3,2,1,0:T(8,128)(2,1)S(1)} %bitcast.17), channel_id=1, source_target_pairs={{0,1},{1,0},{2,3},{3,2},{4,5},{5,4},{6,7},{7,6},{8,9},{9,8},{10,11... | collective-permute-start | bytes 589832 | tf_op jit(solution)/shard_map/ppermute | solution.py:82
  74.6 1.6 %collective-permute-done.23 = bf16[3,8,32,128]{3,2,1,0:T(8,128)(2,1)S(1)} collective-permute-done((bf16[3,8,32,128]{3,2,1,0:T(8,128)(2,1)S(1)}, bf16[3,8,32,128]{3,2,1,0:T(8,128)(2,1)S(1)}, u32[]{:S(2)}, u32[]{:S(2)}) %collective-permute-start.23) | collective-permute-done | bytes 196640 | tf_op jit(solution)/shard_map/ppermute | solution.py:82
  76.2 3.9 %collective-permute-done.24 = bf16[3,8,32,128]{3,2,1,0:T(8,128)(2,1)S(1)} collective-permute-done((bf16[3,8,32,128]{3,2,1,0:T(8,128)(2,1)S(1)}, bf16[3,8,32,128]{3,2,1,0:T(8,128)(2,1)S(1)}, u32[]{:S(2)}, u32[]{:S(2)}) %collective-permute-start.24) | collective-permute-done | bytes 196640 | tf_op jit(solution)/shard_map/ppermute | solution.py:82
  80.2 1.7 %shard_map.53 = f32[3,8,128,128]{3,2,1,0:T(8,128)} custom-call(f32[3,8,32,128]{3,2,1,0:T(8,128)S(1)} %get-tuple-element.44.refs_0_, f32[3,8,32,128]{3,2,1,0:T(8,128)S(1)} %get-tuple-element.49.refs_1_, bf16[1,3,8,32,128]{4,3,2,1,0:T(8,128)(2,1)S(1)} %bitcast.13, bf16[1,3,8,32,128]{4,3,2,1,0:T(8,128)(2,1)S(1)} %bitcast.14), custom_call_target="tpu_custom_call" | custom-call | tf_op jit(solution)/shard_map/pallas_call | solution.py:26
  (44 shorter events, 20.0 us)
Async XLA Ops:
  1.5 8.8 %collective-permute-start = (bf16[3,8,32,128]{3,2,1,0:T(8,128)(2,1)S(1)}, bf16[3,8,32,128]{3,2,1,0:T(8,128)(2,1)S(1)}, u32[]{:S(2)}, u32[]{:S(2)}) collective-permute-start(bf16[3,8,32,128]{3,2,1,0:T(8,128)(2,1)S(1)} %bitcast.11), channel_id=1, source_target_pairs={{0,1},{1,0},{2,3},{3,2},{4,5},{5,4},{6,7},{7,6},{8,9},{9,8},{10,11... | collective-permute-start | bytes 589832 | tf_op jit(solution)/shard_map/ppermute | solution.py:82
  4.6 10.2 %collective-permute-start.3 = (bf16[3,8,32,128]{3,2,1,0:T(8,128)(2,1)S(1)}, bf16[3,8,32,128]{3,2,1,0:T(8,128)(2,1)S(1)}, u32[]{:S(2)}, u32[]{:S(2)}) collective-permute-start(bf16[3,8,32,128]{3,2,1,0:T(8,128)(2,1)S(1)} %bitcast.10), channel_id=1, source_target_pairs={{0,1},{1,0},{2,3},{3,2},{4,5},{5,4},{6,7},{7,6},{8,9},{9,8},{10,11... | collective-permute-start | bytes 589832 | tf_op jit(solution)/shard_map/ppermute | solution.py:82
  11.1 10.6 %collective-permute-start.2 = (bf16[480,384]{1,0:T(8,128)(2,1)S(1)}, bf16[480,384]{1,0:T(8,128)(2,1)S(1)}, u32[]{:S(2)}, u32[]{:S(2)}) collective-permute-start(bf16[480,384]{1,0:T(8,128)(2,1)S(1)} %shard_map.39.refs_0_.w), channel_id=1, source_target_pairs={{0,4},{2,6},{4,0},{6,2},{8,12},{10,14},{12,8},{14,10},{16,20},{18,... | collective-permute-start | bytes 1105928 | tf_op jit(solution)/shard_map/ppermute | solution.py:82
  13.2 12.5 %collective-permute-start.1 = (bf16[480,384]{1,0:T(8,128)(2,1)S(1)}, bf16[480,384]{1,0:T(8,128)(2,1)S(1)}, u32[]{:S(2)}, u32[]{:S(2)}) collective-permute-start(bf16[480,384]{1,0:T(8,128)(2,1)S(1)} %shard_map.39.refs_0_.w), channel_id=1, source_target_pairs={{0,2},{2,0},{4,6},{6,4},{8,10},{10,8},{12,14},{14,12},{16,18},{18,... | collective-permute-start | bytes 1105928 | tf_op jit(solution)/shard_map/ppermute | solution.py:82
  13.2 11.5 %collective-permute-start.5 = (bf16[3,8,64,128]{3,2,1,0:T(8,128)(2,1)S(1)}, bf16[3,8,64,128]{3,2,1,0:T(8,128)(2,1)S(1)}, u32[]{:S(2)}, u32[]{:S(2)}) collective-permute-start(bf16[3,8,64,128]{3,2,1,0:T(8,128)(2,1)S(1)} %get-tuple-element.34.mine_ref), channel_id=1, source_target_pairs={{0,1},{1,0},{2,3},{3,2},{4,5},{5,4},{6,7},{7,6},{8,9},{9,8},{10,11... | collective-permute-start | bytes 1179656 | tf_op jit(solution)/shard_map/ppermute | solution.py:82
  15.6 12.4 %collective-permute-start.7 = (bf16[480,384]{1,0:T(8,128)(2,1)S(1)}, bf16[480,384]{1,0:T(8,128)(2,1)S(1)}, u32[]{:S(2)}, u32[]{:S(2)}) collective-permute-start(bf16[480,384]{1,0:T(8,128)(2,1)S(1)} %shard_map.40.refs_1_.w), channel_id=1, source_target_pairs={{0,4},{2,6},{4,0},{6,2},{8,12},{10,14},{12,8},{14,10},{16,20},{18,... | collective-permute-start | bytes 1105928 | tf_op jit(solution)/shard_map/ppermute | solution.py:82
  16.3 14.8 %collective-permute-start.9 = (bf16[480,384]{1,0:T(8,128)(2,1)S(1)}, bf16[480,384]{1,0:T(8,128)(2,1)S(1)}, u32[]{:S(2)}, u32[]{:S(2)}) collective-permute-start(bf16[480,384]{1,0:T(8,128)(2,1)S(1)} %shard_map.40.refs_1_.w), channel_id=1, source_target_pairs={{0,2},{2,0},{4,6},{6,4},{8,10},{10,8},{12,14},{14,12},{16,18},{18,... | collective-permute-start | bytes 1105928 | tf_op jit(solution)/shard_map/ppermute | solution.py:82
  21.7 9.3 %collective-permute-start.6 = (bf16[480,384]{1,0:T(8,128)(2,1)S(1)}, bf16[480,384]{1,0:T(8,128)(2,1)S(1)}, u32[]{:S(2)}, u32[]{:S(2)}) collective-permute-start(bf16[480,384]{1,0:T(8,128)(2,1)S(1)} %collective-permute-done.2.x), channel_id=1, source_target_pairs={{0,8},{2,10},{4,28},{6,30},{8,16},{10,18},{12,4},{14,6},{16,24},{1... | collective-permute-start | bytes 1105928 | tf_op jit(solution)/shard_map/ppermute | solution.py:82
  24.8 1.7 %collective-permute-start.4 = (bf16[480,384]{1,0:T(8,128)(2,1)S(1)}, bf16[480,384]{1,0:T(8,128)(2,1)S(1)}, u32[]{:S(2)}, u32[]{:S(2)}) collective-permute-start(bf16[480,384]{1,0:T(8,128)(2,1)S(1)} %collective-permute-done.2.x), channel_id=1, source_target_pairs={{0,2},{2,0},{4,6},{6,4},{8,10},{10,8},{12,14},{14,12},{16,18},{18,... | collective-permute-start | bytes 1105928 | tf_op jit(solution)/shard_map/ppermute | solution.py:82
  28.1 3.0 %collective-permute-start.10 = (bf16[480,384]{1,0:T(8,128)(2,1)S(1)}, bf16[480,384]{1,0:T(8,128)(2,1)S(1)}, u32[]{:S(2)}, u32[]{:S(2)}) collective-permute-start(bf16[480,384]{1,0:T(8,128)(2,1)S(1)} %collective-permute-done.7.x), channel_id=1, source_target_pairs={{0,2},{2,0},{4,6},{6,4},{8,10},{10,8},{12,14},{14,12},{16,18},{18,... | collective-permute-start | bytes 1105928 | tf_op jit(solution)/shard_map/ppermute | solution.py:82
  28.1 12.8 %collective-permute-start.12 = (bf16[480,384]{1,0:T(8,128)(2,1)S(1)}, bf16[480,384]{1,0:T(8,128)(2,1)S(1)}, u32[]{:S(2)}, u32[]{:S(2)}) collective-permute-start(bf16[480,384]{1,0:T(8,128)(2,1)S(1)} %collective-permute-done.7.x), channel_id=1, source_target_pairs={{0,8},{2,10},{4,28},{6,30},{8,16},{10,18},{12,4},{14,6},{16,24},{1... | collective-permute-start | bytes 1105928 | tf_op jit(solution)/shard_map/ppermute | solution.py:82
  31.1 1.7 %collective-permute-start.8 = (bf16[480,384]{1,0:T(8,128)(2,1)S(1)}, bf16[480,384]{1,0:T(8,128)(2,1)S(1)}, u32[]{:S(2)}, u32[]{:S(2)}) collective-permute-start(bf16[480,384]{1,0:T(8,128)(2,1)S(1)} %collective-permute-done.6.z), channel_id=1, source_target_pairs={{0,2},{2,0},{4,6},{6,4},{8,10},{10,8},{12,14},{14,12},{16,18},{18,... | collective-permute-start | bytes 1105928 | tf_op jit(solution)/shard_map/ppermute | solution.py:82
  34.4 11.6 %collective-permute-start.14 = (bf16[3,16,32,128]{3,2,1,0:T(8,128)(2,1)S(1)}, bf16[3,16,32,128]{3,2,1,0:T(8,128)(2,1)S(1)}, u32[]{:S(2)}, u32[]{:S(2)}) collective-permute-start(bf16[3,16,32,128]{3,2,1,0:T(8,128)(2,1)S(1)} %get-tuple-element.38.w), channel_id=1, source_target_pairs={{0,4},{2,6},{4,0},{6,2},{8,12},{10,14},{12,8},{14,10},{16,20},{18,... | collective-permute-start | bytes 1179656 | tf_op jit(solution)/shard_map/ppermute | solution.py:82
  40.9 5.6 %collective-permute-start.11 = (bf16[3,16,32,128]{3,2,1,0:T(8,128)(2,1)S(1)}, bf16[3,16,32,128]{3,2,1,0:T(8,128)(2,1)S(1)}, u32[]{:S(2)}, u32[]{:S(2)}) collective-permute-start(bf16[3,16,32,128]{3,2,1,0:T(8,128)(2,1)S(1)} %get-tuple-element.38.w), channel_id=1, source_target_pairs={{0,2},{2,0},{4,6},{6,4},{8,10},{10,8},{12,14},{14,12},{16,18},{18,... | collective-permute-start | bytes 1179656 | tf_op jit(solution)/shard_map/ppermute | solution.py:82
  44.2 10.8 %collective-permute-start.19 = (bf16[3,16,32,128]{3,2,1,0:T(8,128)(2,1)S(1)}, bf16[3,16,32,128]{3,2,1,0:T(8,128)(2,1)S(1)}, u32[]{:S(2)}, u32[]{:S(2)}) collective-permute-start(bf16[3,16,32,128]{3,2,1,0:T(8,128)(2,1)S(1)} %get-tuple-element.40.w), channel_id=1, source_target_pairs={{0,4},{2,6},{4,0},{6,2},{8,12},{10,14},{12,8},{14,10},{16,20},{18,... | collective-permute-start | bytes 1179656 | tf_op jit(solution)/shard_map/ppermute | solution.py:82
  46.0 9.1 %collective-permute-start.15 = (bf16[3,16,32,128]{3,2,1,0:T(8,128)(2,1)S(1)}, bf16[3,16,32,128]{3,2,1,0:T(8,128)(2,1)S(1)}, u32[]{:S(2)}, u32[]{:S(2)}) collective-permute-start(bf16[3,16,32,128]{3,2,1,0:T(8,128)(2,1)S(1)} %collective-permute-done.14.x), channel_id=1, source_target_pairs={{0,2},{2,0},{4,6},{6,4},{8,10},{10,8},{12,14},{14,12},{16,18},{18,... | collective-permute-start | bytes 1179656 | tf_op jit(solution)/shard_map/ppermute | solution.py:82
  46.0 13.5 %collective-permute-start.16 = (bf16[3,16,32,128]{3,2,1,0:T(8,128)(2,1)S(1)}, bf16[3,16,32,128]{3,2,1,0:T(8,128)(2,1)S(1)}, u32[]{:S(2)}, u32[]{:S(2)}) collective-permute-start(bf16[3,16,32,128]{3,2,1,0:T(8,128)(2,1)S(1)} %collective-permute-done.14.x), channel_id=1, source_target_pairs={{0,8},{2,10},{4,28},{6,30},{8,16},{10,18},{12,4},{14,6},{16,24},{1... | collective-permute-start | bytes 1179656 | tf_op jit(solution)/shard_map/ppermute | solution.py:82
  46.0 13.5 %collective-permute-start.18 = (bf16[3,16,32,128]{3,2,1,0:T(8,128)(2,1)S(1)}, bf16[3,16,32,128]{3,2,1,0:T(8,128)(2,1)S(1)}, u32[]{:S(2)}, u32[]{:S(2)}) collective-permute-start(bf16[3,16,32,128]{3,2,1,0:T(8,128)(2,1)S(1)} %get-tuple-element.40.w), channel_id=1, source_target_pairs={{0,2},{2,0},{4,6},{6,4},{8,10},{10,8},{12,14},{14,12},{16,18},{18,... | collective-permute-start | bytes 1179656 | tf_op jit(solution)/shard_map/ppermute | solution.py:82
  55.0 6.4 %collective-permute-start.20 = (bf16[3,16,32,128]{3,2,1,0:T(8,128)(2,1)S(1)}, bf16[3,16,32,128]{3,2,1,0:T(8,128)(2,1)S(1)}, u32[]{:S(2)}, u32[]{:S(2)}) collective-permute-start(bf16[3,16,32,128]{3,2,1,0:T(8,128)(2,1)S(1)} %collective-permute-done.19.x), channel_id=1, source_target_pairs={{0,2},{2,0},{4,6},{6,4},{8,10},{10,8},{12,14},{14,12},{16,18},{18,... | collective-permute-start | bytes 1179656 | tf_op jit(solution)/shard_map/ppermute | solution.py:82
  55.0 13.4 %collective-permute-start.21 = (bf16[3,16,32,128]{3,2,1,0:T(8,128)(2,1)S(1)}, bf16[3,16,32,128]{3,2,1,0:T(8,128)(2,1)S(1)}, u32[]{:S(2)}, u32[]{:S(2)}) collective-permute-start(bf16[3,16,32,128]{3,2,1,0:T(8,128)(2,1)S(1)} %collective-permute-done.19.x), channel_id=1, source_target_pairs={{0,8},{2,10},{4,28},{6,30},{8,16},{10,18},{12,4},{14,6},{16,24},{1... | collective-permute-start | bytes 1179656 | tf_op jit(solution)/shard_map/ppermute | solution.py:82
  59.5 3.4 %collective-permute-start.17 = (bf16[3,16,32,128]{3,2,1,0:T(8,128)(2,1)S(1)}, bf16[3,16,32,128]{3,2,1,0:T(8,128)(2,1)S(1)}, u32[]{:S(2)}, u32[]{:S(2)}) collective-permute-start(bf16[3,16,32,128]{3,2,1,0:T(8,128)(2,1)S(1)} %collective-permute-done.16.z), channel_id=1, source_target_pairs={{0,2},{2,0},{4,6},{6,4},{8,10},{10,8},{12,14},{14,12},{16,18},{18,... | collective-permute-start | bytes 1179656 | tf_op jit(solution)/shard_map/ppermute | solution.py:82
  68.4 1.9 %collective-permute-start.22 = (bf16[3,16,32,128]{3,2,1,0:T(8,128)(2,1)S(1)}, bf16[3,16,32,128]{3,2,1,0:T(8,128)(2,1)S(1)}, u32[]{:S(2)}, u32[]{:S(2)}) collective-permute-start(bf16[3,16,32,128]{3,2,1,0:T(8,128)(2,1)S(1)} %collective-permute-done.21.z), channel_id=1, source_target_pairs={{0,2},{2,0},{4,6},{6,4},{8,10},{10,8},{12,14},{14,12},{16,18},{18,... | collective-permute-start | bytes 1179656 | tf_op jit(solution)/shard_map/ppermute | solution.py:82
  68.4 7.8 %collective-permute-start.23 = (bf16[3,8,32,128]{3,2,1,0:T(8,128)(2,1)S(1)}, bf16[3,8,32,128]{3,2,1,0:T(8,128)(2,1)S(1)}, u32[]{:S(2)}, u32[]{:S(2)}) collective-permute-start(bf16[3,8,32,128]{3,2,1,0:T(8,128)(2,1)S(1)} %bitcast.15), channel_id=1, source_target_pairs={{0,1},{1,0},{2,3},{3,2},{4,5},{5,4},{6,7},{7,6},{8,9},{9,8},{10,11... | collective-permute-start | bytes 589832 | tf_op jit(solution)/shard_map/ppermute | solution.py:82
  72.8 7.3 %collective-permute-start.24 = (bf16[3,8,32,128]{3,2,1,0:T(8,128)(2,1)S(1)}, bf16[3,8,32,128]{3,2,1,0:T(8,128)(2,1)S(1)}, u32[]{:S(2)}, u32[]{:S(2)}) collective-permute-start(bf16[3,8,32,128]{3,2,1,0:T(8,128)(2,1)S(1)} %bitcast.17), channel_id=1, source_target_pairs={{0,1},{1,0},{2,3},{3,2},{4,5},{5,4},{6,7},{7,6},{8,9},{9,8},{10,11... | collective-permute-start | bytes 589832 | tf_op jit(solution)/shard_map/ppermute | solution.py:82
  (1 other events, 1.7 us)

commit v7 on v6

--- a/solution.py
+++ b/solution.py
@@ -14,20 +14,21 @@
 PARAMS = pltpu.CompilerParams(vmem_limit_bytes=16 * 1024 * 1024)
 
 
-def call(kernel, ins, outs, scratch=(), aliases=None, hbm_in=False, hbm_out=False, us=0):
-    here = HBM if hbm_in else VMEM
-    specs = [SMEM if x.dtype == jnp.int32 else here for x in ins]
+def call(kernel, ins, outs, scratch=(), aliases=None, hbm_in=(), hbm_out=False, us=0):
+    specs = [SMEM if x.dtype == jnp.int32 else HBM if a in hbm_in else VMEM for a, x in enumerate(ins)]
     if not hbm_out:
-        outs = [pltpu.VMEM(x.shape, x.dtype) for x in outs]
-    place = pltpu.HBM if hbm_in else pltpu.VMEM
+        outs = [(pltpu.SMEM if x.dtype == jnp.int32 else pltpu.VMEM)(x.shape, x.dtype) for x in outs]
     ins = [
-        x if x.dtype == jnp.int32 else pltpu.with_memory_space_constraint(x, place) for x in ins
+        pltpu.with_memory_space_constraint(
+            x, pltpu.SMEM if x.dtype == jnp.int32 else pltpu.HBM if a in hbm_in else pltpu.VMEM
+        )
+        for a, x in enumerate(ins)
     ]
     return pl.pallas_call(
         kernel,
         out_shape=tuple(outs),
         in_specs=specs,
-        out_specs=tuple(HBM if hbm_out else VMEM for _ in outs),
+        out_specs=tuple(SMEM if x.dtype == jnp.int32 else HBM if hbm_out else VMEM for x in outs),
         scratch_shapes=list(scratch),
         input_output_aliases=aliases or {},
         compiler_params=PARAMS,
@@ -121,13 +122,32 @@
         [shape((rb, slots, part, bs), bf16)]
         + [shape((n - 1, rb, slots, k, bs), bf16) for k in sizes],
         [whole, whole, pltpu.SemaphoreType.DMA((rb,))],
-        hbm_in=True,
+        hbm_in=(0,),
     )
     mine, rest = packed[0], packed[1:]
     lists = jnp.concatenate([col_lists.T, fill_lists.T], axis=1)
 
+    def keep_lists(in_ref, out_ref, sem):
+        copy = pltpu.make_async_copy(in_ref, out_ref, sem)
+        copy.start()
+        copy.wait()
+
+    (lists,) = pl.pallas_call(
+        keep_lists,
+        out_shape=(pltpu.SMEM(lists.shape, lists.dtype),),
+        in_specs=[VMEM],
+        out_specs=(SMEM,),
+        scratch_shapes=[pltpu.SemaphoreType.DMA],
+        compiler_params=PARAMS,
+    )(lists)
+
     def add(ref, where, lanes, value):
         ref[where, lanes] = (ref[where, lanes].astype(f32) + value.astype(f32)).astype(bf16)
+
+    def add_apart(terms):
+        sums = [(ref[at].astype(f32) + value.astype(f32)).astype(bf16) for ref, at, value in terms]
+        for (ref, at, _), value in zip(terms, sums):
+            ref[at] = value
 
     def column(lists_ref, i, slot):
         o = lax.axis_index("rows")
@@ -139,39 +159,47 @@
         for c in chunks:
             out_refs[c][...] = jnp.zeros(out_refs[c].shape, bf16)
         for s in range(slots):
+            terms = []
             for i in range(rb):
                 at = column(lists_ref, i, q * slots + s)
                 for c in chunks:
                     value = mine_ref[i, s, pl.ds(offs[c], sizes[c]), :]
-                    add(out_refs[c], rows_at(at, sizes[c]), pl.ds(i * bs, bs), value)
+                    terms.append((out_refs[c], (rows_at(at, sizes[c]), pl.ds(i * bs, bs)), value))
+            add_apart(terms)
 
     def start_band(lists_ref, *refs):
         rest_refs, out_ref = refs[:cuts], refs[-1]
         q = lax.axis_index("inner")
         out_ref[...] = jnp.zeros(out_ref.shape, bf16)
         for s in range(slots):
+            terms = []
             for i in range(rb):
                 at = column(lists_ref, i, q * slots + s) * n + lax.rem(q + 1, n)
                 for c in chunks:
-                    value = rest_refs[c][0, i, s]
-                    add(out_ref, piece(at, c), pl.ds(i * bs, bs), value)
+                    terms.append((out_ref, (piece(at, c), pl.ds(i * bs, bs)), rest_refs[c][0, i, s]))
+            add_apart(terms)
 
     def end_rows(lists_ref, in_ref, got_ref, out_ref):
         q = lax.axis_index("inner")
         for s in range(slots):
-            for i in range(rb):
-                for m in range(1, n):
+            for m in range(1, n):
+                terms = []
+                for i in range(rb):
                     at = column(lists_ref, i, lax.rem(q - m + n, n) * slots + s)
-                    add(out_ref, rows_at(at, got_ref.shape[3]), pl.ds(i * bs, bs), got_ref[m - 1, i, s])
+                    place = rows_at(at, got_ref.shape[3]), pl.ds(i * bs, bs)
+                    terms.append((out_ref, place, got_ref[m - 1, i, s]))
+                add_apart(terms)
 
     def end_band(lists_ref, in_ref, left_ref, *refs):
         dense_refs, out_ref = refs[:cuts], refs[-1]
         q = lax.axis_index("inner")
         other = lax.rem(q + 1, n)
         for s in range(slots):
+            terms = []
             for i in range(rb):
                 at = column(lists_ref, i, other * slots + s) * n + other
-                add(out_ref, rows_at(at, part), pl.ds(i * bs, bs), left_ref[i, s])
+                terms.append((out_ref, (rows_at(at, part), pl.ds(i * bs, bs)), left_ref[i, s]))
+            add_apart(terms)
         for k in range(BAND * rb):
             for c in chunks:
                 out_ref[piece(k * n + q, c), :] = dense_refs[c][pl.ds(k * sizes[c], sizes[c]), :]
@@ -188,9 +216,11 @@
     rows_shapes = [shape((BAND * rb * k, width), bf16) for k in sizes]
     acc_shapes = [shape((WIDE * rb * k, width), f32) for k in sizes]
     own = call(start_rows, [lists, mine], rows_shapes)
+    if n == 2:
+        (band,) = call(start_band, [lists, *rest], [band_shape])
+        rest = [rest[0], *(after(x, band) for x in rest[1:])]
     got = [exchange(x) for x in rest]
     if n == 2:
-        (band,) = call(start_band, [lists, *rest], [band_shape])
         left = send(after(mine, got[0]), shift(1), "inner")
     else:
         left = lax.all_gather(p_blocks, "inner", axis=0)
@@ -229,44 +259,55 @@
         def _():
             square_term(d["core_x"], cx, left_ref, acc_ref)
 
-    def square_far(lists_ref, acc_in, z, cz, left_ref, acc_ref, sq_ref, low_ref):
-        j = lax.rem(lax.axis_index("rows"), 4)
-        d = offsets(j)
-        square_term(d["z"], z, left_ref, acc_ref)
+    def square_z(acc_in, z, left_ref, acc_ref):
+        square_term(offsets(lax.rem(lax.axis_index("rows"), 4))["z"], z, left_ref, acc_ref)
+
+    def square_far(lists_ref, acc_in, cz, left_ref, acc_ref, low_ref):
+        j = lax.rem(lax.axis_index("rows"), 4)
 
         @pl.when((j == 0) | (j == 3))
         def _():
-            square_term(d["core_z"], cz, left_ref, acc_ref)
+            square_term(offsets(j)["core_z"], cz, left_ref, acc_ref)
 
         for v in range(fill):
             for i in range(rb):
-                value = acc_ref[kept(lists_ref, i, v, sq_ref.shape[2]), pl.ds(i * bs, bs)]
-                sq_ref[i, v] = value
-                low_ref[i, v] = value.astype(bf16)
+                where = kept(lists_ref, i, v, low_ref.shape[2])
+                low_ref[i, v] = acc_ref[where, pl.ds(i * bs, bs)].astype(bf16)
 
     def kept(lists_ref, i, v, cols):
         o = lax.axis_index("rows")
         return rows_at(wrapped(lists_ref[v, nb + o * rb + i] - rb * (o - 2 * REACH)), cols)
 
-    def cube_term(lists_ref, d, reach, low_ref, left_ref, dense, acc_ref, first=False):
+    def window(d, reach):
+        return (WIDE - reach) * rb, jnp.maximum(d, 0) * rb
+
+    def spread(lists_ref, d, reach, low_ref, dense):
         o = lax.axis_index("rows")
         source = lax.rem(o + d + n_rows, n_rows)
-        blocks = (WIDE - reach) * rb
+        blocks, start = window(d, reach)
         cols = low_ref.shape[2]
-        start = jnp.maximum(d, 0) * rb
-        rows = blocks * cols
-        dense[:rows, :] = jnp.zeros((rows, width), bf16)
+        dense[: blocks * cols, :] = jnp.zeros((blocks * cols, width), bf16)
         for v in range(fill):
             for k in range(rb):
                 c = wrapped(lists_ref[v, nb + source * rb + k] - rb * (o - 2 * REACH)) - start
                 c = jnp.where((c >= 0) & (c < blocks), c, blocks)
                 dense[rows_at(c, cols), pl.ds(k * bs, bs)] = low_ref[k, v]
 
-        term = jnp.dot(dense[:rows, :], weights(left_ref, d), preferred_element_type=f32)
-        if first:
+    def multiply(d, reach, dense, left_ref, acc_ref, first=0, end=rb, fresh=False):
+        blocks, start = window(d, reach)
+        cols = dense.shape[0] // (WIDE * rb + 1)
+        rows, lanes = blocks * cols, pl.ds(first * bs, (end - first) * bs)
+        term = jnp.dot(
+            dense[:rows, :], left_ref[rows_at(d + REACH, width), lanes], preferred_element_type=f32
+        )
+        if fresh:
             acc_ref[...] = term
         else:
-            acc_ref[pl.ds(pl.multiple_of(start * cols, rb * cols), rows), :] += term
+            acc_ref[pl.ds(pl.multiple_of(start * cols, rb * cols), rows), lanes] += term
+
+    def cube_term(lists_ref, d, reach, low_ref, left_ref, dense, acc_ref, first=False):
+        spread(lists_ref, d, reach, low_ref, dense)
+        multiply(d, reach, dense, left_ref, acc_ref, fresh=first)
 
     def cube_own(lists_ref, w, u, left_ref, acc_ref, dense):
         d = offsets(lax.rem(lax.axis_index("rows"), 4))
@@ -282,8 +323,7 @@
         def _():
             cube_term(lists_ref, d["core_x"], 1, cx, left_ref, dense, acc_ref)
 
-    def cube_far(lists_ref, acc_in, z, cz, left_ref, sq_ref, acc_ref, keep_ref, give_ref, dense):
-        q = lax.axis_index("inner")
+    def cube_far(lists_ref, acc_in, z, cz, left_ref, square_ref, acc_ref, keep_ref, give_ref, dense):
         j = lax.rem(lax.axis_index("rows"), 4)
         d = offsets(j)
         cube_term(lists_ref, d["z"], 2, z, left_ref, dense, acc_ref)
@@ -292,14 +332,45 @@
         def _():
             cube_term(lists_ref, d["core_z"], 1, cz, left_ref, dense, acc_ref)
 
+        results(0, rb, lists_ref, square_ref, acc_ref, keep_ref, give_ref)
+
+    def results(first, end, lists_ref, square_ref, acc_ref, keep_ref, give_ref):
+        q = lax.axis_index("inner")
+
         def result(i, v):
-            return 3.0 * sq_ref[i, v] - 2.0 * acc_ref[kept(lists_ref, i, v, sq_ref.shape[2]), pl.ds(i * bs, bs)]
+            at = kept(lists_ref, i, v, keep_ref.shape[2]), pl.ds(i * bs, bs)
+            return 3.0 * square_ref[at] - 2.0 * acc_ref[at]
 
         for s in range(slots):
-            for i in range(rb):
-                keep_ref[i, s] = result(i, q * slots + s)
+            for i in range(first, end):
+                keep_ref[i - first, s] = result(i, q * slots + s)
                 for m in range(1, n):
-                    give_ref[m - 1, i, s] = result(i, lax.rem(q + m, n) * slots + s).astype(bf16)
+                    v = lax.rem(q + m, n) * slots + s
+                    give_ref[m - 1, i - first, s] = result(i, v).astype(bf16)
+
+    def cube_last(lists_ref, acc_in, z, cz, left_ref, square_ref, acc_ref, dense_z, dense_cz, keep_ref, give_ref):
+        j = lax.rem(lax.axis_index("rows"), 4)
+        d = offsets(j)
+        spread(lists_ref, d["z"], 2, z, dense_z)
+        multiply(d["z"], 2, dense_z, left_ref, acc_ref, 0, early)
+
+        @pl.when((j == 0) | (j == 3))
+        def _():
+            spread(lists_ref, d["core_z"], 1, cz, dense_cz)
+            multiply(d["core_z"], 1, dense_cz, left_ref, acc_ref, 0, early)
+
+        results(0, early, lists_ref, square_ref, acc_ref, keep_ref, give_ref)
+
+    def cube_end(lists_ref, acc_in, dense_z, dense_cz, left_ref, square_ref, acc_ref, keep_ref, give_ref):
+        j = lax.rem(lax.axis_index("rows"), 4)
+        d = offsets(j)
+        multiply(d["z"], 2, dense_z, left_ref, acc_ref, early)
+
+        @pl.when((j == 0) | (j == 3))
+        def _():
+            multiply(d["core_z"], 1, dense_cz, left_ref, acc_ref, early)
+
+        results(early, rb, lists_ref, square_ref, acc_ref, keep_ref, give_ref)
 
     dense = [[pltpu.VMEM(((WIDE * rb + 1) * k, width), bf16)] for k in sizes]
     x, z, sq, low, x2, z2 = [], [], [], [], [], []
@@ -314,15 +385,15 @@
     for c in chunks:
         z_c = after(z[c], close[c], *x[c + 1 : c + 2])
         cz = after(send(z_c, flip_core), *close[c + 1 : c + 2])
-        kept_shape = (rb, fill, sizes[c], bs)
+        (acc,) = call(square_z, [close[c], z_c, band], [acc_shapes[c]], aliases={0: 0})
         one = call(
             square_far,
-            [lists, close[c], z_c, cz, band],
-            [acc_shapes[c], shape(kept_shape, f32), shape(kept_shape, bf16)],
+            [lists, acc, cz, band],
+            [acc_shapes[c], shape((rb, fill, sizes[c], bs), bf16)],
             aliases={1: 0},
         )
-        sq.append(one[1])
-        low.append(one[2])
+        sq.append(one[0])
+        low.append(one[1])
     keep, give, near = [], [], []
     for c in chunks:
         x_c = send(low[c], flip_x)
@@ -335,41 +406,76 @@
         cx = send(x_c, flip_core)
         (acc,) = call(cube_near, [lists, acc, x_c, cx, band], [acc_shapes[c]], dense[c], aliases={1: 0}, us=20 * c)
         near.append(acc)
-    for c in chunks:
+    early = rb - rb // 3
+
+    def result_shapes(c, count):
+        kept_shape = (count, slots, sizes[c], bs)
+        return [shape(kept_shape, f32), shape((n - 1, *kept_shape), bf16)]
+
+    taken = []
+    for c in chunks[:-1]:
         z_c = after(z2[c], near[c], *give)
         one = call(
             cube_far,
             [lists, near[c], z_c, send(z_c, flip_core), band, sq[c]],
-            [acc_shapes[c], shape((rb, slots, sizes[c], bs), f32), shape((n - 1, rb, slots, sizes[c], bs), bf16)],
+            [acc_shapes[c], *result_shapes(c, rb)],
             dense[c],
             aliases={1: 0},
         )[1:]
         keep.append(one[0])
         give.append(one[1])
-    taken = [exchange(v) for v in give]
-
-    def join(*refs):
-        keep_refs, taken_refs, (out_ref, turned, done, sems) = refs[:cuts], refs[cuts : 2 * cuts], refs[-4:]
-        q = lax.axis_index("inner")
-        copies = [pltpu.make_async_copy(done.at[i], out_ref.at[i], sems.at[i]) for i in range(rb)]
-        for i in range(rb):
+        taken.append(exchange(one[1]))
+    c = cuts - 1
+    z_c = after(z2[c], near[c], *give)
+    dense_shape = shape(dense[c][0].shape, bf16)
+    acc, dense_z, dense_cz, keep_a, give_a = call(
+        cube_last,
+        [lists, near[c], z_c, send(z_c, flip_core), band, sq[c]],
+        [acc_shapes[c], dense_shape, dense_shape, *result_shapes(c, early)],
+        aliases={1: 0},
+    )
+    taken_a = exchange(give_a)
+    _, keep_b, give_b = call(
+        cube_end,
+        [lists, acc, dense_z, dense_cz, band, sq[c]],
+        [acc_shapes[c], *result_shapes(c, rb - early)],
+        aliases={1: 0},
+    )
+    taken_b = exchange(give_b)
+
+    def join(first, end, keep_refs, taken_refs, out_ref, turned, done, sems):
+        q = lax.axis_index("inner")
+        copies = {i: pltpu.make_async_copy(done.at[i], out_ref.at[i], sems.at[i]) for i in range(first, end)}
+        for i in range(first, end):
             for s in range(slots):
                 for c in chunks:
-                    turned[i, s, piece(q, c), :] = keep_refs[c][i, s]
+                    k = i - first if c == cuts - 1 else i
+                    turned[i, s, piece(q, c), :] = keep_refs[c][k, s]
                     for m in range(1, n):
                         at = piece(lax.rem(q - m + n, n), c)
-                        turned[i, s, at, :] = taken_refs[c][m - 1, i, s].astype(f32)
+                        turned[i, s, at, :] = taken_refs[c][m - 1, k, s].astype(f32)
                 done[i, s] = turned[i, s].T
             copies[i].start()
-        for copy in copies:
+        for copy in copies.values():
             copy.wait()
 
+    def join_first(*refs):
+        join(0, early, refs[:cuts], refs[cuts : 2 * cuts], *refs[2 * cuts :])
+
+    def join_rest(*refs):
+        join(early, rb, refs[:cuts], refs[cuts : 2 * cuts], *refs[2 * cuts + 1 :])
+
     whole = pltpu.VMEM((rb, slots, bs, bs), f32)
+    scratch = [whole, whole, pltpu.SemaphoreType.DMA((rb,))]
+    out_shape = [shape((rb, slots, bs, bs), f32)]
+    (out,) = call(join_first, [*keep, keep_a, *taken, taken_a], out_shape, scratch, hbm_out=True)
     (out,) = call(
-        join,
-        [*keep, *taken],
-        [shape((rb, slots, bs, bs), f32)],
-        [whole, whole, pltpu.SemaphoreType.DMA((rb,))],
+        join_rest,
+        [*keep, keep_b, *taken, taken_b, out],
+        out_shape,
+        scratch,
+        aliases={2 * cuts: 0},
+        hbm_in=(2 * cuts,),
         hbm_out=True,
     )
     return out

time: 82.2 us -> 80.4 us (0.978)
  Pallas kernels: 24.7 us -> 17.2 us
  waiting for transfers between devices: 39.2 us -> 43.1 us
  starting transfers between devices: 17.1 us -> 18.7 us
    pallas_call x17 -> x21, Pallas kernels: 24.7 us -> 16.5 us  [call(): pl.pallas_call(kernel, out_shape=tuple(outs), in_specs=specs, out_specs=t...]
    ppermute x25 -> x26, waiting for transfers between devices: 39.2 us -> 43.1 us  [send(): return lax.ppermute(x, axis, pairs)]
    ppermute x25 -> x26, starting transfers between devices: 17.1 us -> 18.7 us  [send(): return lax.ppermute(x, axis, pairs)]
  transfers between devices with their start and end apart: 25 -> 26, of which waited for: 15 -> 15; matrix products, arithmetic and copies ran while one was open for 1% -> 1% of each run, Pallas kernels for 26% -> 18%
where the time goes in v7:
time: 80.4 us; the launch traced here: 80.2 us
  waiting for transfers between devices  43.1 us (54%)
  starting transfers between devices  18.7 us (23%)
  Pallas kernels  17.2 us (21%)
    ppermute x26, waiting for transfers between devices, send(): return lax.ppermute(x, axis, pairs)  43.1 us
    ppermute x26, starting transfers between devices, send(): return lax.ppermute(x, axis, pairs)  18.7 us
    pallas_call x21, Pallas kernels, call(): pl.pallas_call(kernel, out_shape=tuple(outs), in_specs=specs, out_specs=t...  16.5 us
  transfers between devices with their start and end apart: 26, of which 15 were waited for; matrix products, arithmetic and copies ran while one was open for 1% of the time, Pallas kernels for 18%

profile of v7, /device:TPU:0, one launch (start us, length us, event | category | flops | bytes accessed | tf_op | source)
XLA Modules:
  0.0 80.2 jit_solution(15512519972656617941)
XLA Ops:
  0.0 1.5 %shard_map.38 = (bf16[3,8,64,128]{3,2,1,0:T(8,128)(2,1)S(1)}, bf16[1,3,8,32,128]{4,3,2,1,0:T(8,128)(2,1)S(1)}, bf16[1,3,8,32,128]{4,3,2,1,0:T(8,128)(2,1)S(1)}) custom-call(bf16[3,8,128,128]{3,2,1,0:T(8,128)(2,1)} %p_ref.1), custom_call_target="tpu_custom_call" | custom-call | tf_op jit(solution)/shard_map/pallas_call | solution.py:27
  1.5 3.0 %collective-permute-start = (bf16[3,8,32,128]{3,2,1,0:T(8,128)(2,1)S(1)}, bf16[3,8,32,128]{3,2,1,0:T(8,128)(2,1)S(1)}, u32[]{:S(2)}, u32[]{:S(2)}) collective-permute-start(bf16[3,8,32,128]{3,2,1,0:T(8,128)(2,1)S(1)} %bitcast.15), channel_id=1, source_target_pairs={{0,1},{1,0},{2,3},{3,2},{4,5},{5,4},{6,7},{7,6},{8,9},{9,8},{10,11... | collective-permute-start | bytes 589832 | tf_op jit(solution)/shard_map/ppermute | solution.py:83
  6.6 3.7 %collective-permute-done = bf16[3,8,32,128]{3,2,1,0:T(8,128)(2,1)S(1)} collective-permute-done((bf16[3,8,32,128]{3,2,1,0:T(8,128)(2,1)S(1)}, bf16[3,8,32,128]{3,2,1,0:T(8,128)(2,1)S(1)}, u32[]{:S(2)}, u32[]{:S(2)}) %collective-permute-start) | collective-permute-done | bytes 196640 | tf_op jit(solution)/shard_map/ppermute | solution.py:83
  10.4 2.1 %collective-permute-start.2 = (bf16[480,384]{1,0:T(8,128)(2,1)S(1)}, bf16[480,384]{1,0:T(8,128)(2,1)S(1)}, u32[]{:S(2)}, u32[]{:S(2)}) collective-permute-start(bf16[480,384]{1,0:T(8,128)(2,1)S(1)} %shard_map.40.refs_0_.w), channel_id=1, source_target_pairs={{0,4},{2,6},{4,0},{6,2},{8,12},{10,14},{12,8},{14,10},{16,20},{18,... | collective-permute-start | bytes 1105928 | tf_op jit(solution)/shard_map/ppermute | solution.py:83
  12.5 1.5 %collective-permute-start.5 = (bf16[3,8,64,128]{3,2,1,0:T(8,128)(2,1)S(1)}, bf16[3,8,64,128]{3,2,1,0:T(8,128)(2,1)S(1)}, u32[]{:S(2)}, u32[]{:S(2)}) collective-permute-start(bf16[3,8,64,128]{3,2,1,0:T(8,128)(2,1)S(1)} %get-tuple-element.41.mine_ref), channel_id=1, source_target_pairs={{0,1},{1,0},{2,3},{3,2},{4,5},{5,4},{6,7},{7,6},{8,9},{9,8},{10,11... | collective-permute-start | bytes 1179656 | tf_op jit(solution)/shard_map/ppermute | solution.py:83
  14.1 1.4 %collective-permute-start.7 = (bf16[480,384]{1,0:T(8,128)(2,1)S(1)}, bf16[480,384]{1,0:T(8,128)(2,1)S(1)}, u32[]{:S(2)}, u32[]{:S(2)}) collective-permute-start(bf16[480,384]{1,0:T(8,128)(2,1)S(1)} %shard_map.42.refs_1_.w), channel_id=1, source_target_pairs={{0,4},{2,6},{4,0},{6,2},{8,12},{10,14},{12,8},{14,10},{16,20},{18,... | collective-permute-start | bytes 1105928 | tf_op jit(solution)/shard_map/ppermute | solution.py:83
  15.5 6.2 %collective-permute-done.2.x = bf16[480,384]{1,0:T(8,128)(2,1)S(1)} collective-permute-done((bf16[480,384]{1,0:T(8,128)(2,1)S(1)}, bf16[480,384]{1,0:T(8,128)(2,1)S(1)}, u32[]{:S(2)}, u32[]{:S(2)}) %collective-permute-start.2) | collective-permute-done | bytes 368672 | tf_op jit(solution)/shard_map/ppermute | solution.py:83
  21.7 1.4 %collective-permute-start.6 = (bf16[480,384]{1,0:T(8,128)(2,1)S(1)}, bf16[480,384]{1,0:T(8,128)(2,1)S(1)}, u32[]{:S(2)}, u32[]{:S(2)}) collective-permute-start(bf16[480,384]{1,0:T(8,128)(2,1)S(1)} %collective-permute-done.2.x), channel_id=1, source_target_pairs={{0,8},{2,10},{4,28},{6,30},{8,16},{10,18},{12,4},{14,6},{16,24},{1... | collective-permute-start | bytes 1105928 | tf_op jit(solution)/shard_map/ppermute | solution.py:83
  24.2 1.5 %collective-permute-done.4.cx = bf16[480,384]{1,0:T(8,128)(2,1)S(1)} collective-permute-done((bf16[480,384]{1,0:T(8,128)(2,1)S(1)}, bf16[480,384]{1,0:T(8,128)(2,1)S(1)}, u32[]{:S(2)}, u32[]{:S(2)}) %collective-permute-start.4) | collective-permute-done | bytes 368672 | tf_op jit(solution)/shard_map/ppermute | solution.py:83
  27.3 1.5 %collective-permute-start.12 = (bf16[480,384]{1,0:T(8,128)(2,1)S(1)}, bf16[480,384]{1,0:T(8,128)(2,1)S(1)}, u32[]{:S(2)}, u32[]{:S(2)}) collective-permute-start(bf16[480,384]{1,0:T(8,128)(2,1)S(1)} %collective-permute-done.7.x), channel_id=1, source_target_pairs={{0,8},{2,10},{4,28},{6,30},{8,16},{10,18},{12,4},{14,6},{16,24},{1... | collective-permute-start | bytes 1105928 | tf_op jit(solution)/shard_map/ppermute | solution.py:83
  28.8 2.3 %collective-permute-done.6.z = bf16[480,384]{1,0:T(8,128)(2,1)S(1)} collective-permute-done((bf16[480,384]{1,0:T(8,128)(2,1)S(1)}, bf16[480,384]{1,0:T(8,128)(2,1)S(1)}, u32[]{:S(2)}, u32[]{:S(2)}) %collective-permute-start.6) | collective-permute-done | bytes 368672 | tf_op jit(solution)/shard_map/ppermute | solution.py:83
  34.6 5.5 %collective-permute-done.12.z = bf16[480,384]{1,0:T(8,128)(2,1)S(1)} collective-permute-done((bf16[480,384]{1,0:T(8,128)(2,1)S(1)}, bf16[480,384]{1,0:T(8,128)(2,1)S(1)}, u32[]{:S(2)}, u32[]{:S(2)}) %collective-permute-start.12) | collective-permute-done | bytes 368672 | tf_op jit(solution)/shard_map/ppermute | solution.py:83
  45.2 1.3 %shard_map.50.acc_in = f32[864,384]{1,0:T(8,128)S(1)} custom-call(s32[16,96]{1,0:T(8,128)S(4)} %shard_map.37.lists_ref, bf16[3,16,32,128]{3,2,1,0:T(8,128)(2,1)S(1)} %get-tuple-element.45.w, bf16[3,16,32,128]{3,2,1,0:T(8,128)(2,1)S(1)} %collective-permute-done.11.u, bf16[1920,384]{1,0:T(8,128)(2,1)S(1)} %shard_map.43.left_ref), custom_call_target="tpu_custom_call" | custom-call | tf_op jit(solution)/shard_map/pallas_call | solution.py:27
  46.5 6.8 %collective-permute-done.19.x = bf16[3,16,32,128]{3,2,1,0:T(8,128)(2,1)S(1)} collective-permute-done((bf16[3,16,32,128]{3,2,1,0:T(8,128)(2,1)S(1)}, bf16[3,16,32,128]{3,2,1,0:T(8,128)(2,1)S(1)}, u32[]{:S(2)}, u32[]{:S(2)}) %collective-permute-start.19) | collective-permute-done | bytes 393248 | tf_op jit(solution)/shard_map/ppermute | solution.py:83
  54.1 4.6 %collective-permute-done.16.z = bf16[3,16,32,128]{3,2,1,0:T(8,128)(2,1)S(1)} collective-permute-done((bf16[3,16,32,128]{3,2,1,0:T(8,128)(2,1)S(1)}, bf16[3,16,32,128]{3,2,1,0:T(8,128)(2,1)S(1)}, u32[]{:S(2)}, u32[]{:S(2)}) %collective-permute-start.16) | collective-permute-done | bytes 393248 | tf_op jit(solution)/shard_map/ppermute | solution.py:83
  58.7 1.3 %shard_map.53.acc_in = f32[864,384]{1,0:T(8,128)S(1)} custom-call(s32[16,96]{1,0:T(8,128)S(4)} %shard_map.37.lists_ref, bf16[3,16,32,128]{3,2,1,0:T(8,128)(2,1)S(1)} %get-tuple-element.47.w, bf16[3,16,32,128]{3,2,1,0:T(8,128)(2,1)S(1)} %collective-permute-done.18.u, bf16[1920,384]{1,0:T(8,128)(2,1)S(1)} %shard_map.43.left_ref), custom_call_target="tpu_custom_call" | custom-call | flops 22000001024 | bytes 1024 | tf_op jit(solution)/shard_map/pallas_call | solution.py:27
  60.9 1.8 %shard_map.52 = (f32[864,384]{1,0:T(8,128)S(1)}, f32[3,8,32,128]{3,2,1,0:T(8,128)S(1)}, bf16[1,3,8,32,128]{4,3,2,1,0:T(8,128)(2,1)S(1)}) custom-call(s32[16,96]{1,0:T(8,128)S(4)} %shard_map.37.lists_ref, f32[864,384]{1,0:T(8,128)S(1)} %shard_map.51.acc_in, bf16[3,16,32,128]{3,2,1,0:T(8,128)(2,1)S(1)} %collective-permute-done.16.z, ...), custom_call_target="tpu_custom_call", output_to_operand_aliasing={{0}: (1, {})} | custom-call | tf_op jit(solution)/shard_map/pallas_call | solution.py:27
  62.7 4.3 %collective-permute-done.21.z = bf16[3,16,32,128]{3,2,1,0:T(8,128)(2,1)S(1)} collective-permute-done((bf16[3,16,32,128]{3,2,1,0:T(8,128)(2,1)S(1)}, bf16[3,16,32,128]{3,2,1,0:T(8,128)(2,1)S(1)}, u32[]{:S(2)}, u32[]{:S(2)}) %collective-permute-start.21) | collective-permute-done | bytes 393248 | tf_op jit(solution)/shard_map/ppermute | solution.py:83
  67.0 1.8 %collective-permute-start.23 = (bf16[3,8,32,128]{3,2,1,0:T(8,128)(2,1)S(1)}, bf16[3,8,32,128]{3,2,1,0:T(8,128)(2,1)S(1)}, u32[]{:S(2)}, u32[]{:S(2)}) collective-permute-start(bf16[3,8,32,128]{3,2,1,0:T(8,128)(2,1)S(1)} %bitcast.19), channel_id=1, source_target_pairs={{0,1},{1,0},{2,3},{3,2},{4,5},{5,4},{6,7},{7,6},{8,9},{9,8},{10,11... | collective-permute-start | bytes 589832 | tf_op jit(solution)/shard_map/ppermute | solution.py:83
  68.8 1.4 %shard_map.55 = (f32[864,384]{1,0:T(8,128)S(1)}, bf16[896,384]{1,0:T(8,128)(2,1)S(1)}, bf16[896,384]{1,0:T(8,128)(2,1)S(1)}, f32[2,8,32,128]{3,2,1,0:T(8,128)S(1)}, bf16[1,2,8,32,128]{4,3,2,1,0:T(8,128)(2,1)S(1)}) custom-call(s32[16,96]{1,0:T(8,128)S(4)} %shard_map.37.lists_ref, f32[864,384]{1,0:T(8,128)S(1)} %shard_map.54.acc_in, ...), custom_call_target="tpu_custom_call", output_to_operand_aliasing={{0}: (1, {})} | custom-call | tf_op jit(solution)/shard_map/pallas_call | solution.py:27
  70.3 1.8 %collective-permute-start.25 = (bf16[2,8,32,128]{3,2,1,0:T(8,128)(2,1)S(1)}, bf16[2,8,32,128]{3,2,1,0:T(8,128)(2,1)S(1)}, u32[]{:S(2)}, u32[]{:S(2)}) collective-permute-start(bf16[2,8,32,128]{3,2,1,0:T(8,128)(2,1)S(1)} %bitcast.21), channel_id=1, source_target_pairs={{0,1},{1,0},{2,3},{3,2},{4,5},{5,4},{6,7},{7,6},{8,9},{9,8},{10,11... | collective-permute-start | bytes 393224 | tf_op jit(solution)/shard_map/ppermute | solution.py:83
  73.2 1.6 %collective-permute-done.23 = bf16[3,8,32,128]{3,2,1,0:T(8,128)(2,1)S(1)} collective-permute-done((bf16[3,8,32,128]{3,2,1,0:T(8,128)(2,1)S(1)}, bf16[3,8,32,128]{3,2,1,0:T(8,128)(2,1)S(1)}, u32[]{:S(2)}, u32[]{:S(2)}) %collective-permute-start.23) | collective-permute-done | bytes 196640 | tf_op jit(solution)/shard_map/ppermute | solution.py:83
  74.7 2.8 %collective-permute-done.25 = bf16[2,8,32,128]{3,2,1,0:T(8,128)(2,1)S(1)} collective-permute-done((bf16[2,8,32,128]{3,2,1,0:T(8,128)(2,1)S(1)}, bf16[2,8,32,128]{3,2,1,0:T(8,128)(2,1)S(1)}, u32[]{:S(2)}, u32[]{:S(2)}) %collective-permute-start.25) | collective-permute-done | bytes 131104 | tf_op jit(solution)/shard_map/ppermute | solution.py:83
  77.5 1.4 %shard_map.57.refs_4_ = f32[3,8,128,128]{3,2,1,0:T(8,128)} custom-call(f32[3,8,32,128]{3,2,1,0:T(8,128)S(1)} %get-tuple-element.51.refs_0_, f32[2,8,32,128]{3,2,1,0:T(8,128)S(1)} %get-tuple-element.61.refs_1_, bf16[1,3,8,32,128]{4,3,2,1,0:T(8,128)(2,1)S(1)} %bitcast.12, bf16[1,2,8,32,128]{4,3,2,1,0:T(8,128)(2,1)S(1)} %bitcast.17), custom_call_target="tpu_custom_call" | custom-call | tf_op jit(solution)/shard_map/pallas_call | solution.py:27
  (51 shorter events, 17.4 us)
Async XLA Ops:
  1.5 8.8 %collective-permute-start = (bf16[3,8,32,128]{3,2,1,0:T(8,128)(2,1)S(1)}, bf16[3,8,32,128]{3,2,1,0:T(8,128)(2,1)S(1)}, u32[]{:S(2)}, u32[]{:S(2)}) collective-permute-start(bf16[3,8,32,128]{3,2,1,0:T(8,128)(2,1)S(1)} %bitcast.15), channel_id=1, source_target_pairs={{0,1},{1,0},{2,3},{3,2},{4,5},{5,4},{6,7},{7,6},{8,9},{9,8},{10,11... | collective-permute-start | bytes 589832 | tf_op jit(solution)/shard_map/ppermute | solution.py:83
  6.3 7.7 %collective-permute-start.3 = (bf16[3,8,32,128]{3,2,1,0:T(8,128)(2,1)S(1)}, bf16[3,8,32,128]{3,2,1,0:T(8,128)(2,1)S(1)}, u32[]{:S(2)}, u32[]{:S(2)}) collective-permute-start(bf16[3,8,32,128]{3,2,1,0:T(8,128)(2,1)S(1)} %bitcast.14), channel_id=1, source_target_pairs={{0,1},{1,0},{2,3},{3,2},{4,5},{5,4},{6,7},{7,6},{8,9},{9,8},{10,11... | collective-permute-start | bytes 589832 | tf_op jit(solution)/shard_map/ppermute | solution.py:83
  10.4 11.3 %collective-permute-start.2 = (bf16[480,384]{1,0:T(8,128)(2,1)S(1)}, bf16[480,384]{1,0:T(8,128)(2,1)S(1)}, u32[]{:S(2)}, u32[]{:S(2)}) collective-permute-start(bf16[480,384]{1,0:T(8,128)(2,1)S(1)} %shard_map.40.refs_0_.w), channel_id=1, source_target_pairs={{0,4},{2,6},{4,0},{6,2},{8,12},{10,14},{12,8},{14,10},{16,20},{18,... | collective-permute-start | bytes 1105928 | tf_op jit(solution)/shard_map/ppermute | solution.py:83
  12.5 11.7 %collective-permute-start.1 = (bf16[480,384]{1,0:T(8,128)(2,1)S(1)}, bf16[480,384]{1,0:T(8,128)(2,1)S(1)}, u32[]{:S(2)}, u32[]{:S(2)}) collective-permute-start(bf16[480,384]{1,0:T(8,128)(2,1)S(1)} %shard_map.40.refs_0_.w), channel_id=1, source_target_pairs={{0,2},{2,0},{4,6},{6,4},{8,10},{10,8},{12,14},{14,12},{16,18},{18,... | collective-permute-start | bytes 1105928 | tf_op jit(solution)/shard_map/ppermute | solution.py:83
  12.5 11.5 %collective-permute-start.5 = (bf16[3,8,64,128]{3,2,1,0:T(8,128)(2,1)S(1)}, bf16[3,8,64,128]{3,2,1,0:T(8,128)(2,1)S(1)}, u32[]{:S(2)}, u32[]{:S(2)}) collective-permute-start(bf16[3,8,64,128]{3,2,1,0:T(8,128)(2,1)S(1)} %get-tuple-element.41.mine_ref), channel_id=1, source_target_pairs={{0,1},{1,0},{2,3},{3,2},{4,5},{5,4},{6,7},{7,6},{8,9},{9,8},{10,11... | collective-permute-start | bytes 1179656 | tf_op jit(solution)/shard_map/ppermute | solution.py:83
  14.1 13.2 %collective-permute-start.7 = (bf16[480,384]{1,0:T(8,128)(2,1)S(1)}, bf16[480,384]{1,0:T(8,128)(2,1)S(1)}, u32[]{:S(2)}, u32[]{:S(2)}) collective-permute-start(bf16[480,384]{1,0:T(8,128)(2,1)S(1)} %shard_map.42.refs_1_.w), channel_id=1, source_target_pairs={{0,4},{2,6},{4,0},{6,2},{8,12},{10,14},{12,8},{14,10},{16,20},{18,... | collective-permute-start | bytes 1105928 | tf_op jit(solution)/shard_map/ppermute | solution.py:83
  15.5 15.9 %collective-permute-start.9 = (bf16[480,384]{1,0:T(8,128)(2,1)S(1)}, bf16[480,384]{1,0:T(8,128)(2,1)S(1)}, u32[]{:S(2)}, u32[]{:S(2)}) collective-permute-start(bf16[480,384]{1,0:T(8,128)(2,1)S(1)} %shard_map.42.refs_1_.w), channel_id=1, source_target_pairs={{0,2},{2,0},{4,6},{6,4},{8,10},{10,8},{12,14},{14,12},{16,18},{18,... | collective-permute-start | bytes 1105928 | tf_op jit(solution)/shard_map/ppermute | solution.py:83
  21.7 9.3 %collective-permute-start.6 = (bf16[480,384]{1,0:T(8,128)(2,1)S(1)}, bf16[480,384]{1,0:T(8,128)(2,1)S(1)}, u32[]{:S(2)}, u32[]{:S(2)}) collective-permute-start(bf16[480,384]{1,0:T(8,128)(2,1)S(1)} %collective-permute-done.2.x), channel_id=1, source_target_pairs={{0,8},{2,10},{4,28},{6,30},{8,16},{10,18},{12,4},{14,6},{16,24},{1... | collective-permute-start | bytes 1105928 | tf_op jit(solution)/shard_map/ppermute | solution.py:83
  24.0 1.7 %collective-permute-start.4 = (bf16[480,384]{1,0:T(8,128)(2,1)S(1)}, bf16[480,384]{1,0:T(8,128)(2,1)S(1)}, u32[]{:S(2)}, u32[]{:S(2)}) collective-permute-start(bf16[480,384]{1,0:T(8,128)(2,1)S(1)} %collective-permute-done.2.x), channel_id=1, source_target_pairs={{0,2},{2,0},{4,6},{6,4},{8,10},{10,8},{12,14},{14,12},{16,18},{18,... | collective-permute-start | bytes 1105928 | tf_op jit(solution)/shard_map/ppermute | solution.py:83
  27.3 4.2 %collective-permute-start.10 = (bf16[480,384]{1,0:T(8,128)(2,1)S(1)}, bf16[480,384]{1,0:T(8,128)(2,1)S(1)}, u32[]{:S(2)}, u32[]{:S(2)}) collective-permute-start(bf16[480,384]{1,0:T(8,128)(2,1)S(1)} %collective-permute-done.7.x), channel_id=1, source_target_pairs={{0,2},{2,0},{4,6},{6,4},{8,10},{10,8},{12,14},{14,12},{16,18},{18,... | collective-permute-start | bytes 1105928 | tf_op jit(solution)/shard_map/ppermute | solution.py:83
  27.3 12.8 %collective-permute-start.12 = (bf16[480,384]{1,0:T(8,128)(2,1)S(1)}, bf16[480,384]{1,0:T(8,128)(2,1)S(1)}, u32[]{:S(2)}, u32[]{:S(2)}) collective-permute-start(bf16[480,384]{1,0:T(8,128)(2,1)S(1)} %collective-permute-done.7.x), channel_id=1, source_target_pairs={{0,8},{2,10},{4,28},{6,30},{8,16},{10,18},{12,4},{14,6},{16,24},{1... | collective-permute-start | bytes 1105928 | tf_op jit(solution)/shard_map/ppermute | solution.py:83
  33.3 11.2 %collective-permute-start.14 = (bf16[3,16,32,128]{3,2,1,0:T(8,128)(2,1)S(1)}, bf16[3,16,32,128]{3,2,1,0:T(8,128)(2,1)S(1)}, u32[]{:S(2)}, u32[]{:S(2)}) collective-permute-start(bf16[3,16,32,128]{3,2,1,0:T(8,128)(2,1)S(1)} %get-tuple-element.45.w), channel_id=1, source_target_pairs={{0,4},{2,6},{4,0},{6,2},{8,12},{10,14},{12,8},{14,10},{16,20},{18,... | collective-permute-start | bytes 1179656 | tf_op jit(solution)/shard_map/ppermute | solution.py:83
  40.5 4.7 %collective-permute-start.11 = (bf16[3,16,32,128]{3,2,1,0:T(8,128)(2,1)S(1)}, bf16[3,16,32,128]{3,2,1,0:T(8,128)(2,1)S(1)}, u32[]{:S(2)}, u32[]{:S(2)}) collective-permute-start(bf16[3,16,32,128]{3,2,1,0:T(8,128)(2,1)S(1)} %get-tuple-element.45.w), channel_id=1, source_target_pairs={{0,2},{2,0},{4,6},{6,4},{8,10},{10,8},{12,14},{14,12},{16,18},{18,... | collective-permute-start | bytes 1179656 | tf_op jit(solution)/shard_map/ppermute | solution.py:83
  42.4 11.0 %collective-permute-start.19 = (bf16[3,16,32,128]{3,2,1,0:T(8,128)(2,1)S(1)}, bf16[3,16,32,128]{3,2,1,0:T(8,128)(2,1)S(1)}, u32[]{:S(2)}, u32[]{:S(2)}) collective-permute-start(bf16[3,16,32,128]{3,2,1,0:T(8,128)(2,1)S(1)} %get-tuple-element.47.w), channel_id=1, source_target_pairs={{0,4},{2,6},{4,0},{6,2},{8,12},{10,14},{12,8},{14,10},{16,20},{18,... | collective-permute-start | bytes 1179656 | tf_op jit(solution)/shard_map/ppermute | solution.py:83
  44.5 8.8 %collective-permute-start.15 = (bf16[3,16,32,128]{3,2,1,0:T(8,128)(2,1)S(1)}, bf16[3,16,32,128]{3,2,1,0:T(8,128)(2,1)S(1)}, u32[]{:S(2)}, u32[]{:S(2)}) collective-permute-start(bf16[3,16,32,128]{3,2,1,0:T(8,128)(2,1)S(1)} %collective-permute-done.14.x), channel_id=1, source_target_pairs={{0,2},{2,0},{4,6},{6,4},{8,10},{10,8},{12,14},{14,12},{16,18},{18,... | collective-permute-start | bytes 1179656 | tf_op jit(solution)/shard_map/ppermute | solution.py:83
  44.5 14.2 %collective-permute-start.16 = (bf16[3,16,32,128]{3,2,1,0:T(8,128)(2,1)S(1)}, bf16[3,16,32,128]{3,2,1,0:T(8,128)(2,1)S(1)}, u32[]{:S(2)}, u32[]{:S(2)}) collective-permute-start(bf16[3,16,32,128]{3,2,1,0:T(8,128)(2,1)S(1)} %collective-permute-done.14.x), channel_id=1, source_target_pairs={{0,8},{2,10},{4,28},{6,30},{8,16},{10,18},{12,4},{14,6},{16,24},{1... | collective-permute-start | bytes 1179656 | tf_op jit(solution)/shard_map/ppermute | solution.py:83
  45.0 13.7 %collective-permute-start.18 = (bf16[3,16,32,128]{3,2,1,0:T(8,128)(2,1)S(1)}, bf16[3,16,32,128]{3,2,1,0:T(8,128)(2,1)S(1)}, u32[]{:S(2)}, u32[]{:S(2)}) collective-permute-start(bf16[3,16,32,128]{3,2,1,0:T(8,128)(2,1)S(1)} %get-tuple-element.47.w), channel_id=1, source_target_pairs={{0,2},{2,0},{4,6},{6,4},{8,10},{10,8},{12,14},{14,12},{16,18},{18,... | collective-permute-start | bytes 1179656 | tf_op jit(solution)/shard_map/ppermute | solution.py:83
  53.3 6.6 %collective-permute-start.20 = (bf16[3,16,32,128]{3,2,1,0:T(8,128)(2,1)S(1)}, bf16[3,16,32,128]{3,2,1,0:T(8,128)(2,1)S(1)}, u32[]{:S(2)}, u32[]{:S(2)}) collective-permute-start(bf16[3,16,32,128]{3,2,1,0:T(8,128)(2,1)S(1)} %collective-permute-done.19.x), channel_id=1, source_target_pairs={{0,2},{2,0},{4,6},{6,4},{8,10},{10,8},{12,14},{14,12},{16,18},{18,... | collective-permute-start | bytes 1179656 | tf_op jit(solution)/shard_map/ppermute | solution.py:83
  53.3 13.7 %collective-permute-start.21 = (bf16[3,16,32,128]{3,2,1,0:T(8,128)(2,1)S(1)}, bf16[3,16,32,128]{3,2,1,0:T(8,128)(2,1)S(1)}, u32[]{:S(2)}, u32[]{:S(2)}) collective-permute-start(bf16[3,16,32,128]{3,2,1,0:T(8,128)(2,1)S(1)} %collective-permute-done.19.x), channel_id=1, source_target_pairs={{0,8},{2,10},{4,28},{6,30},{8,16},{10,18},{12,4},{14,6},{16,24},{1... | collective-permute-start | bytes 1179656 | tf_op jit(solution)/shard_map/ppermute | solution.py:83
  58.7 2.2 %collective-permute-start.17 = (bf16[3,16,32,128]{3,2,1,0:T(8,128)(2,1)S(1)}, bf16[3,16,32,128]{3,2,1,0:T(8,128)(2,1)S(1)}, u32[]{:S(2)}, u32[]{:S(2)}) collective-permute-start(bf16[3,16,32,128]{3,2,1,0:T(8,128)(2,1)S(1)} %collective-permute-done.16.z), channel_id=1, source_target_pairs={{0,2},{2,0},{4,6},{6,4},{8,10},{10,8},{12,14},{14,12},{16,18},{18,... | collective-permute-start | bytes 1179656 | tf_op jit(solution)/shard_map/ppermute | solution.py:83
  67.0 1.8 %collective-permute-start.22 = (bf16[3,16,32,128]{3,2,1,0:T(8,128)(2,1)S(1)}, bf16[3,16,32,128]{3,2,1,0:T(8,128)(2,1)S(1)}, u32[]{:S(2)}, u32[]{:S(2)}) collective-permute-start(bf16[3,16,32,128]{3,2,1,0:T(8,128)(2,1)S(1)} %collective-permute-done.21.z), channel_id=1, source_target_pairs={{0,2},{2,0},{4,6},{6,4},{8,10},{10,8},{12,14},{14,12},{16,18},{18,... | collective-permute-start | bytes 1179656 | tf_op jit(solution)/shard_map/ppermute | solution.py:83
  67.0 7.7 %collective-permute-start.23 = (bf16[3,8,32,128]{3,2,1,0:T(8,128)(2,1)S(1)}, bf16[3,8,32,128]{3,2,1,0:T(8,128)(2,1)S(1)}, u32[]{:S(2)}, u32[]{:S(2)}) collective-permute-start(bf16[3,8,32,128]{3,2,1,0:T(8,128)(2,1)S(1)} %bitcast.19), channel_id=1, source_target_pairs={{0,1},{1,0},{2,3},{3,2},{4,5},{5,4},{6,7},{7,6},{8,9},{9,8},{10,11... | collective-permute-start | bytes 589832 | tf_op jit(solution)/shard_map/ppermute | solution.py:83
  70.3 7.3 %collective-permute-start.25 = (bf16[2,8,32,128]{3,2,1,0:T(8,128)(2,1)S(1)}, bf16[2,8,32,128]{3,2,1,0:T(8,128)(2,1)S(1)}, u32[]{:S(2)}, u32[]{:S(2)}) collective-permute-start(bf16[2,8,32,128]{3,2,1,0:T(8,128)(2,1)S(1)} %bitcast.21), channel_id=1, source_target_pairs={{0,1},{1,0},{2,3},{3,2},{4,5},{5,4},{6,7},{7,6},{8,9},{9,8},{10,11... | collective-permute-start | bytes 393224 | tf_op jit(solution)/shard_map/ppermute | solution.py:83
  72.8 6.2 %collective-permute-start.24 = (bf16[1,8,32,128]{3,2,1,0:T(8,128)(2,1)S(1)}, bf16[1,8,32,128]{3,2,1,0:T(8,128)(2,1)S(1)}, u32[]{:S(2)}, u32[]{:S(2)}) collective-permute-start(bf16[1,8,32,128]{3,2,1,0:T(8,128)(2,1)S(1)} %bitcast.22), channel_id=1, source_target_pairs={{0,1},{1,0},{2,3},{3,2},{4,5},{5,4},{6,7},{7,6},{8,9},{9,8},{10,11... | collective-permute-start | bytes 196616 | tf_op jit(solution)/shard_map/ppermute | solution.py:83
  (2 other events, 3.4 us)

commit v8 on v7

--- a/solution.py
+++ b/solution.py
@@ -383,7 +383,7 @@
         close += call(square_near, [own[c], u, x_c, cx, band], [acc_shapes[c]], us=20 * c or 20)
         x.append(x_c)
     for c in chunks:
-        z_c = after(z[c], close[c], *x[c + 1 : c + 2])
+        z_c = after(z[c], close[c])
         cz = after(send(z_c, flip_core), *close[c + 1 : c + 2])
         (acc,) = call(square_z, [close[c], z_c, band], [acc_shapes[c]], aliases={0: 0})
         one = call(

time: 80.4 us -> 80 us (level)
  starting transfers between devices: 18.7 us -> 17.7 us
    ppermute x26, starting transfers between devices: 18.7 us -> 17.7 us  [send(): return lax.ppermute(x, axis, pairs)]
  transfers between devices with their start and end apart: 26 -> 26, of which waited for: 15 -> 16; matrix products, arithmetic and copies ran while one was open for 1% -> 1% of each run, Pallas kernels for 18% -> 18%
where the time goes in v8:
time: 80 us; the launch traced here: 79.8 us
  waiting for transfers between devices  43.8 us (55%)
  starting transfers between devices  17.7 us (22%)
  Pallas kernels  17.2 us (22%)
    ppermute x26, waiting for transfers between devices, send(): return lax.ppermute(x, axis, pairs)  43.8 us
    ppermute x26, starting transfers between devices, send(): return lax.ppermute(x, axis, pairs)  17.7 us
    pallas_call x21, Pallas kernels, call(): pl.pallas_call(kernel, out_shape=tuple(outs), in_specs=specs, out_specs=t...  16.6 us
  transfers between devices with their start and end apart: 26, of which 16 were waited for; matrix products, arithmetic and copies ran while one was open for 1% of the time, Pallas kernels for 18%

profile of v8, /device:TPU:0, one launch (start us, length us, event | category | flops | bytes accessed | tf_op | source)
XLA Modules:
  0.0 79.8 jit_solution(2408341382400821175)
XLA Ops:
  0.0 1.5 %shard_map.38 = (bf16[3,8,64,128]{3,2,1,0:T(8,128)(2,1)S(1)}, bf16[1,3,8,32,128]{4,3,2,1,0:T(8,128)(2,1)S(1)}, bf16[1,3,8,32,128]{4,3,2,1,0:T(8,128)(2,1)S(1)}) custom-call(bf16[3,8,128,128]{3,2,1,0:T(8,128)(2,1)} %p_ref.1), custom_call_target="tpu_custom_call" | custom-call | tf_op jit(solution)/shard_map/pallas_call | solution.py:27
  1.5 3.0 %collective-permute-start = (bf16[3,8,32,128]{3,2,1,0:T(8,128)(2,1)S(1)}, bf16[3,8,32,128]{3,2,1,0:T(8,128)(2,1)S(1)}, u32[]{:S(2)}, u32[]{:S(2)}) collective-permute-start(bf16[3,8,32,128]{3,2,1,0:T(8,128)(2,1)S(1)} %bitcast.15), channel_id=1, source_target_pairs={{0,1},{1,0},{2,3},{3,2},{4,5},{5,4},{6,7},{7,6},{8,9},{9,8},{10,11... | collective-permute-start | bytes 589832 | tf_op jit(solution)/shard_map/ppermute | solution.py:83
  6.6 3.7 %collective-permute-done = bf16[3,8,32,128]{3,2,1,0:T(8,128)(2,1)S(1)} collective-permute-done((bf16[3,8,32,128]{3,2,1,0:T(8,128)(2,1)S(1)}, bf16[3,8,32,128]{3,2,1,0:T(8,128)(2,1)S(1)}, u32[]{:S(2)}, u32[]{:S(2)}) %collective-permute-start) | collective-permute-done | bytes 196640 | tf_op jit(solution)/shard_map/ppermute | solution.py:83
  10.4 2.1 %collective-permute-start.2 = (bf16[480,384]{1,0:T(8,128)(2,1)S(1)}, bf16[480,384]{1,0:T(8,128)(2,1)S(1)}, u32[]{:S(2)}, u32[]{:S(2)}) collective-permute-start(bf16[480,384]{1,0:T(8,128)(2,1)S(1)} %shard_map.40.refs_0_.w), channel_id=1, source_target_pairs={{0,4},{2,6},{4,0},{6,2},{8,12},{10,14},{12,8},{14,10},{16,20},{18,... | collective-permute-start | bytes 1105928 | tf_op jit(solution)/shard_map/ppermute | solution.py:83
  12.5 1.5 %collective-permute-start.5 = (bf16[3,8,64,128]{3,2,1,0:T(8,128)(2,1)S(1)}, bf16[3,8,64,128]{3,2,1,0:T(8,128)(2,1)S(1)}, u32[]{:S(2)}, u32[]{:S(2)}) collective-permute-start(bf16[3,8,64,128]{3,2,1,0:T(8,128)(2,1)S(1)} %get-tuple-element.41.mine_ref), channel_id=1, source_target_pairs={{0,1},{1,0},{2,3},{3,2},{4,5},{5,4},{6,7},{7,6},{8,9},{9,8},{10,11... | collective-permute-start | bytes 1179656 | tf_op jit(solution)/shard_map/ppermute | solution.py:83
  15.6 5.8 %collective-permute-done.2.x = bf16[480,384]{1,0:T(8,128)(2,1)S(1)} collective-permute-done((bf16[480,384]{1,0:T(8,128)(2,1)S(1)}, bf16[480,384]{1,0:T(8,128)(2,1)S(1)}, u32[]{:S(2)}, u32[]{:S(2)}) %collective-permute-start.2) | collective-permute-done | bytes 368672 | tf_op jit(solution)/shard_map/ppermute | solution.py:83
  21.5 1.4 %collective-permute-start.6 = (bf16[480,384]{1,0:T(8,128)(2,1)S(1)}, bf16[480,384]{1,0:T(8,128)(2,1)S(1)}, u32[]{:S(2)}, u32[]{:S(2)}) collective-permute-start(bf16[480,384]{1,0:T(8,128)(2,1)S(1)} %collective-permute-done.2.x), channel_id=1, source_target_pairs={{0,8},{2,10},{4,28},{6,30},{8,16},{10,18},{12,4},{14,6},{16,24},{1... | collective-permute-start | bytes 1105928 | tf_op jit(solution)/shard_map/ppermute | solution.py:83
  24.2 1.5 %collective-permute-done.4.cx = bf16[480,384]{1,0:T(8,128)(2,1)S(1)} collective-permute-done((bf16[480,384]{1,0:T(8,128)(2,1)S(1)}, bf16[480,384]{1,0:T(8,128)(2,1)S(1)}, u32[]{:S(2)}, u32[]{:S(2)}) %collective-permute-start.4) | collective-permute-done | bytes 368672 | tf_op jit(solution)/shard_map/ppermute | solution.py:83
  27.3 1.5 %collective-permute-start.12 = (bf16[480,384]{1,0:T(8,128)(2,1)S(1)}, bf16[480,384]{1,0:T(8,128)(2,1)S(1)}, u32[]{:S(2)}, u32[]{:S(2)}) collective-permute-start(bf16[480,384]{1,0:T(8,128)(2,1)S(1)} %collective-permute-done.9.x), channel_id=1, source_target_pairs={{0,8},{2,10},{4,28},{6,30},{8,16},{10,18},{12,4},{14,6},{16,24},{1... | collective-permute-start | bytes 1105928 | tf_op jit(solution)/shard_map/ppermute | solution.py:83
  28.8 2.0 %collective-permute-done.6.z = bf16[480,384]{1,0:T(8,128)(2,1)S(1)} collective-permute-done((bf16[480,384]{1,0:T(8,128)(2,1)S(1)}, bf16[480,384]{1,0:T(8,128)(2,1)S(1)}, u32[]{:S(2)}, u32[]{:S(2)}) %collective-permute-start.6) | collective-permute-done | bytes 368672 | tf_op jit(solution)/shard_map/ppermute | solution.py:83
  33.0 1.4 %collective-permute-start.14 = (bf16[3,16,32,128]{3,2,1,0:T(8,128)(2,1)S(1)}, bf16[3,16,32,128]{3,2,1,0:T(8,128)(2,1)S(1)}, u32[]{:S(2)}, u32[]{:S(2)}) collective-permute-start(bf16[3,16,32,128]{3,2,1,0:T(8,128)(2,1)S(1)} %get-tuple-element.45.w), channel_id=1, source_target_pairs={{0,4},{2,6},{4,0},{6,2},{8,12},{10,14},{12,8},{14,10},{16,20},{18,... | collective-permute-start | bytes 1179656 | tf_op jit(solution)/shard_map/ppermute | solution.py:83
  34.4 5.7 %collective-permute-done.12.z = bf16[480,384]{1,0:T(8,128)(2,1)S(1)} collective-permute-done((bf16[480,384]{1,0:T(8,128)(2,1)S(1)}, bf16[480,384]{1,0:T(8,128)(2,1)S(1)}, u32[]{:S(2)}, u32[]{:S(2)}) %collective-permute-start.12) | collective-permute-done | bytes 368672 | tf_op jit(solution)/shard_map/ppermute | solution.py:83
  42.7 1.5 %collective-permute-done.14.x = bf16[3,16,32,128]{3,2,1,0:T(8,128)(2,1)S(1)} collective-permute-done((bf16[3,16,32,128]{3,2,1,0:T(8,128)(2,1)S(1)}, bf16[3,16,32,128]{3,2,1,0:T(8,128)(2,1)S(1)}, u32[]{:S(2)}, u32[]{:S(2)}) %collective-permute-start.14) | collective-permute-done | bytes 393248 | tf_op jit(solution)/shard_map/ppermute | solution.py:83
  46.0 7.2 %collective-permute-done.19.x = bf16[3,16,32,128]{3,2,1,0:T(8,128)(2,1)S(1)} collective-permute-done((bf16[3,16,32,128]{3,2,1,0:T(8,128)(2,1)S(1)}, bf16[3,16,32,128]{3,2,1,0:T(8,128)(2,1)S(1)}, u32[]{:S(2)}, u32[]{:S(2)}) %collective-permute-start.19) | collective-permute-done | bytes 393248 | tf_op jit(solution)/shard_map/ppermute | solution.py:83
  54.0 3.6 %collective-permute-done.16.z = bf16[3,16,32,128]{3,2,1,0:T(8,128)(2,1)S(1)} collective-permute-done((bf16[3,16,32,128]{3,2,1,0:T(8,128)(2,1)S(1)}, bf16[3,16,32,128]{3,2,1,0:T(8,128)(2,1)S(1)}, u32[]{:S(2)}, u32[]{:S(2)}) %collective-permute-start.16) | collective-permute-done | bytes 393248 | tf_op jit(solution)/shard_map/ppermute | solution.py:83
  57.5 1.3 %shard_map.53.acc_in = f32[864,384]{1,0:T(8,128)S(1)} custom-call(s32[16,96]{1,0:T(8,128)S(4)} %shard_map.37.lists_ref, bf16[3,16,32,128]{3,2,1,0:T(8,128)(2,1)S(1)} %get-tuple-element.47.w, bf16[3,16,32,128]{3,2,1,0:T(8,128)(2,1)S(1)} %collective-permute-done.18.u, bf16[1920,384]{1,0:T(8,128)(2,1)S(1)} %shard_map.43.left_ref), custom_call_target="tpu_custom_call" | custom-call | flops 22000001024 | bytes 1024 | tf_op jit(solution)/shard_map/pallas_call | solution.py:27
  59.8 1.8 %shard_map.52 = (f32[864,384]{1,0:T(8,128)S(1)}, f32[3,8,32,128]{3,2,1,0:T(8,128)S(1)}, bf16[1,3,8,32,128]{4,3,2,1,0:T(8,128)(2,1)S(1)}) custom-call(s32[16,96]{1,0:T(8,128)S(4)} %shard_map.37.lists_ref, f32[864,384]{1,0:T(8,128)S(1)} %shard_map.51.acc_in, bf16[3,16,32,128]{3,2,1,0:T(8,128)(2,1)S(1)} %collective-permute-done.16.z, ...), custom_call_target="tpu_custom_call", output_to_operand_aliasing={{0}: (1, {})} | custom-call | tf_op jit(solution)/shard_map/pallas_call | solution.py:27
  61.6 5.0 %collective-permute-done.21.z = bf16[3,16,32,128]{3,2,1,0:T(8,128)(2,1)S(1)} collective-permute-done((bf16[3,16,32,128]{3,2,1,0:T(8,128)(2,1)S(1)}, bf16[3,16,32,128]{3,2,1,0:T(8,128)(2,1)S(1)}, u32[]{:S(2)}, u32[]{:S(2)}) %collective-permute-start.21) | collective-permute-done | bytes 393248 | tf_op jit(solution)/shard_map/ppermute | solution.py:83
  66.6 1.5 %collective-permute-start.23 = (bf16[3,8,32,128]{3,2,1,0:T(8,128)(2,1)S(1)}, bf16[3,8,32,128]{3,2,1,0:T(8,128)(2,1)S(1)}, u32[]{:S(2)}, u32[]{:S(2)}) collective-permute-start(bf16[3,8,32,128]{3,2,1,0:T(8,128)(2,1)S(1)} %bitcast.19), channel_id=1, source_target_pairs={{0,1},{1,0},{2,3},{3,2},{4,5},{5,4},{6,7},{7,6},{8,9},{9,8},{10,11... | collective-permute-start | bytes 589832 | tf_op jit(solution)/shard_map/ppermute | solution.py:83
  68.3 1.4 %shard_map.55 = (f32[864,384]{1,0:T(8,128)S(1)}, bf16[896,384]{1,0:T(8,128)(2,1)S(1)}, bf16[896,384]{1,0:T(8,128)(2,1)S(1)}, f32[2,8,32,128]{3,2,1,0:T(8,128)S(1)}, bf16[1,2,8,32,128]{4,3,2,1,0:T(8,128)(2,1)S(1)}) custom-call(s32[16,96]{1,0:T(8,128)S(4)} %shard_map.37.lists_ref, f32[864,384]{1,0:T(8,128)S(1)} %shard_map.54.acc_in, ...), custom_call_target="tpu_custom_call", output_to_operand_aliasing={{0}: (1, {})} | custom-call | tf_op jit(solution)/shard_map/pallas_call | solution.py:27
  69.8 1.6 %collective-permute-start.25 = (bf16[2,8,32,128]{3,2,1,0:T(8,128)(2,1)S(1)}, bf16[2,8,32,128]{3,2,1,0:T(8,128)(2,1)S(1)}, u32[]{:S(2)}, u32[]{:S(2)}) collective-permute-start(bf16[2,8,32,128]{3,2,1,0:T(8,128)(2,1)S(1)} %bitcast.21), channel_id=1, source_target_pairs={{0,1},{1,0},{2,3},{3,2},{4,5},{5,4},{6,7},{7,6},{8,9},{9,8},{10,11... | collective-permute-start | bytes 393224 | tf_op jit(solution)/shard_map/ppermute | solution.py:83
  72.7 1.7 %collective-permute-done.23 = bf16[3,8,32,128]{3,2,1,0:T(8,128)(2,1)S(1)} collective-permute-done((bf16[3,8,32,128]{3,2,1,0:T(8,128)(2,1)S(1)}, bf16[3,8,32,128]{3,2,1,0:T(8,128)(2,1)S(1)}, u32[]{:S(2)}, u32[]{:S(2)}) %collective-permute-start.23) | collective-permute-done | bytes 196640 | tf_op jit(solution)/shard_map/ppermute | solution.py:83
  74.3 2.8 %collective-permute-done.25 = bf16[2,8,32,128]{3,2,1,0:T(8,128)(2,1)S(1)} collective-permute-done((bf16[2,8,32,128]{3,2,1,0:T(8,128)(2,1)S(1)}, bf16[2,8,32,128]{3,2,1,0:T(8,128)(2,1)S(1)}, u32[]{:S(2)}, u32[]{:S(2)}) %collective-permute-start.25) | collective-permute-done | bytes 131104 | tf_op jit(solution)/shard_map/ppermute | solution.py:83
  77.1 1.4 %shard_map.57.refs_4_ = f32[3,8,128,128]{3,2,1,0:T(8,128)} custom-call(f32[3,8,32,128]{3,2,1,0:T(8,128)S(1)} %get-tuple-element.51.refs_0_, f32[2,8,32,128]{3,2,1,0:T(8,128)S(1)} %get-tuple-element.61.refs_1_, bf16[1,3,8,32,128]{4,3,2,1,0:T(8,128)(2,1)S(1)} %bitcast.12, bf16[1,2,8,32,128]{4,3,2,1,0:T(8,128)(2,1)S(1)} %bitcast.17), custom_call_target="tpu_custom_call" | custom-call | tf_op jit(solution)/shard_map/pallas_call | solution.py:27
  (51 shorter events, 17.6 us)
Async XLA Ops:
  1.5 8.8 %collective-permute-start = (bf16[3,8,32,128]{3,2,1,0:T(8,128)(2,1)S(1)}, bf16[3,8,32,128]{3,2,1,0:T(8,128)(2,1)S(1)}, u32[]{:S(2)}, u32[]{:S(2)}) collective-permute-start(bf16[3,8,32,128]{3,2,1,0:T(8,128)(2,1)S(1)} %bitcast.15), channel_id=1, source_target_pairs={{0,1},{1,0},{2,3},{3,2},{4,5},{5,4},{6,7},{7,6},{8,9},{9,8},{10,11... | collective-permute-start | bytes 589832 | tf_op jit(solution)/shard_map/ppermute | solution.py:83
  6.3 7.7 %collective-permute-start.3 = (bf16[3,8,32,128]{3,2,1,0:T(8,128)(2,1)S(1)}, bf16[3,8,32,128]{3,2,1,0:T(8,128)(2,1)S(1)}, u32[]{:S(2)}, u32[]{:S(2)}) collective-permute-start(bf16[3,8,32,128]{3,2,1,0:T(8,128)(2,1)S(1)} %bitcast.14), channel_id=1, source_target_pairs={{0,1},{1,0},{2,3},{3,2},{4,5},{5,4},{6,7},{7,6},{8,9},{9,8},{10,11... | collective-permute-start | bytes 589832 | tf_op jit(solution)/shard_map/ppermute | solution.py:83
  10.4 11.1 %collective-permute-start.2 = (bf16[480,384]{1,0:T(8,128)(2,1)S(1)}, bf16[480,384]{1,0:T(8,128)(2,1)S(1)}, u32[]{:S(2)}, u32[]{:S(2)}) collective-permute-start(bf16[480,384]{1,0:T(8,128)(2,1)S(1)} %shard_map.40.refs_0_.w), channel_id=1, source_target_pairs={{0,4},{2,6},{4,0},{6,2},{8,12},{10,14},{12,8},{14,10},{16,20},{18,... | collective-permute-start | bytes 1105928 | tf_op jit(solution)/shard_map/ppermute | solution.py:83
  12.5 11.7 %collective-permute-start.1 = (bf16[480,384]{1,0:T(8,128)(2,1)S(1)}, bf16[480,384]{1,0:T(8,128)(2,1)S(1)}, u32[]{:S(2)}, u32[]{:S(2)}) collective-permute-start(bf16[480,384]{1,0:T(8,128)(2,1)S(1)} %shard_map.40.refs_0_.w), channel_id=1, source_target_pairs={{0,2},{2,0},{4,6},{6,4},{8,10},{10,8},{12,14},{14,12},{16,18},{18,... | collective-permute-start | bytes 1105928 | tf_op jit(solution)/shard_map/ppermute | solution.py:83
  12.5 11.5 %collective-permute-start.5 = (bf16[3,8,64,128]{3,2,1,0:T(8,128)(2,1)S(1)}, bf16[3,8,64,128]{3,2,1,0:T(8,128)(2,1)S(1)}, u32[]{:S(2)}, u32[]{:S(2)}) collective-permute-start(bf16[3,8,64,128]{3,2,1,0:T(8,128)(2,1)S(1)} %get-tuple-element.41.mine_ref), channel_id=1, source_target_pairs={{0,1},{1,0},{2,3},{3,2},{4,5},{5,4},{6,7},{7,6},{8,9},{9,8},{10,11... | collective-permute-start | bytes 1179656 | tf_op jit(solution)/shard_map/ppermute | solution.py:83
  14.1 17.0 %collective-permute-start.8 = (bf16[480,384]{1,0:T(8,128)(2,1)S(1)}, bf16[480,384]{1,0:T(8,128)(2,1)S(1)}, u32[]{:S(2)}, u32[]{:S(2)}) collective-permute-start(bf16[480,384]{1,0:T(8,128)(2,1)S(1)} %shard_map.42.refs_1_.w), channel_id=1, source_target_pairs={{0,2},{2,0},{4,6},{6,4},{8,10},{10,8},{12,14},{14,12},{16,18},{18,... | collective-permute-start | bytes 1105928 | tf_op jit(solution)/shard_map/ppermute | solution.py:83
  14.4 12.9 %collective-permute-start.9 = (bf16[480,384]{1,0:T(8,128)(2,1)S(1)}, bf16[480,384]{1,0:T(8,128)(2,1)S(1)}, u32[]{:S(2)}, u32[]{:S(2)}) collective-permute-start(bf16[480,384]{1,0:T(8,128)(2,1)S(1)} %shard_map.42.refs_1_.w), channel_id=1, source_target_pairs={{0,4},{2,6},{4,0},{6,2},{8,12},{10,14},{12,8},{14,10},{16,20},{18,... | collective-permute-start | bytes 1105928 | tf_op jit(solution)/shard_map/ppermute | solution.py:83
  21.5 9.3 %collective-permute-start.6 = (bf16[480,384]{1,0:T(8,128)(2,1)S(1)}, bf16[480,384]{1,0:T(8,128)(2,1)S(1)}, u32[]{:S(2)}, u32[]{:S(2)}) collective-permute-start(bf16[480,384]{1,0:T(8,128)(2,1)S(1)} %collective-permute-done.2.x), channel_id=1, source_target_pairs={{0,8},{2,10},{4,28},{6,30},{8,16},{10,18},{12,4},{14,6},{16,24},{1... | collective-permute-start | bytes 1105928 | tf_op jit(solution)/shard_map/ppermute | solution.py:83
  24.0 1.7 %collective-permute-start.4 = (bf16[480,384]{1,0:T(8,128)(2,1)S(1)}, bf16[480,384]{1,0:T(8,128)(2,1)S(1)}, u32[]{:S(2)}, u32[]{:S(2)}) collective-permute-start(bf16[480,384]{1,0:T(8,128)(2,1)S(1)} %collective-permute-done.2.x), channel_id=1, source_target_pairs={{0,2},{2,0},{4,6},{6,4},{8,10},{10,8},{12,14},{14,12},{16,18},{18,... | collective-permute-start | bytes 1105928 | tf_op jit(solution)/shard_map/ppermute | solution.py:83
  27.3 3.9 %collective-permute-start.10 = (bf16[480,384]{1,0:T(8,128)(2,1)S(1)}, bf16[480,384]{1,0:T(8,128)(2,1)S(1)}, u32[]{:S(2)}, u32[]{:S(2)}) collective-permute-start(bf16[480,384]{1,0:T(8,128)(2,1)S(1)} %collective-permute-done.9.x), channel_id=1, source_target_pairs={{0,2},{2,0},{4,6},{6,4},{8,10},{10,8},{12,14},{14,12},{16,18},{18,... | collective-permute-start | bytes 1105928 | tf_op jit(solution)/shard_map/ppermute | solution.py:83
  27.3 12.8 %collective-permute-start.12 = (bf16[480,384]{1,0:T(8,128)(2,1)S(1)}, bf16[480,384]{1,0:T(8,128)(2,1)S(1)}, u32[]{:S(2)}, u32[]{:S(2)}) collective-permute-start(bf16[480,384]{1,0:T(8,128)(2,1)S(1)} %collective-permute-done.9.x), channel_id=1, source_target_pairs={{0,8},{2,10},{4,28},{6,30},{8,16},{10,18},{12,4},{14,6},{16,24},{1... | collective-permute-start | bytes 1105928 | tf_op jit(solution)/shard_map/ppermute | solution.py:83
  33.0 11.2 %collective-permute-start.14 = (bf16[3,16,32,128]{3,2,1,0:T(8,128)(2,1)S(1)}, bf16[3,16,32,128]{3,2,1,0:T(8,128)(2,1)S(1)}, u32[]{:S(2)}, u32[]{:S(2)}) collective-permute-start(bf16[3,16,32,128]{3,2,1,0:T(8,128)(2,1)S(1)} %get-tuple-element.45.w), channel_id=1, source_target_pairs={{0,4},{2,6},{4,0},{6,2},{8,12},{10,14},{12,8},{14,10},{16,20},{18,... | collective-permute-start | bytes 1179656 | tf_op jit(solution)/shard_map/ppermute | solution.py:83
  40.5 4.2 %collective-permute-start.11 = (bf16[3,16,32,128]{3,2,1,0:T(8,128)(2,1)S(1)}, bf16[3,16,32,128]{3,2,1,0:T(8,128)(2,1)S(1)}, u32[]{:S(2)}, u32[]{:S(2)}) collective-permute-start(bf16[3,16,32,128]{3,2,1,0:T(8,128)(2,1)S(1)} %get-tuple-element.45.w), channel_id=1, source_target_pairs={{0,2},{2,0},{4,6},{6,4},{8,10},{10,8},{12,14},{14,12},{16,18},{18,... | collective-permute-start | bytes 1179656 | tf_op jit(solution)/shard_map/ppermute | solution.py:83
  42.4 10.8 %collective-permute-start.19 = (bf16[3,16,32,128]{3,2,1,0:T(8,128)(2,1)S(1)}, bf16[3,16,32,128]{3,2,1,0:T(8,128)(2,1)S(1)}, u32[]{:S(2)}, u32[]{:S(2)}) collective-permute-start(bf16[3,16,32,128]{3,2,1,0:T(8,128)(2,1)S(1)} %get-tuple-element.47.w), channel_id=1, source_target_pairs={{0,4},{2,6},{4,0},{6,2},{8,12},{10,14},{12,8},{14,10},{16,20},{18,... | collective-permute-start | bytes 1179656 | tf_op jit(solution)/shard_map/ppermute | solution.py:83
  44.2 9.0 %collective-permute-start.15 = (bf16[3,16,32,128]{3,2,1,0:T(8,128)(2,1)S(1)}, bf16[3,16,32,128]{3,2,1,0:T(8,128)(2,1)S(1)}, u32[]{:S(2)}, u32[]{:S(2)}) collective-permute-start(bf16[3,16,32,128]{3,2,1,0:T(8,128)(2,1)S(1)} %collective-permute-done.14.x), channel_id=1, source_target_pairs={{0,2},{2,0},{4,6},{6,4},{8,10},{10,8},{12,14},{14,12},{16,18},{18,... | collective-permute-start | bytes 1179656 | tf_op jit(solution)/shard_map/ppermute | solution.py:83
  44.2 13.3 %collective-permute-start.16 = (bf16[3,16,32,128]{3,2,1,0:T(8,128)(2,1)S(1)}, bf16[3,16,32,128]{3,2,1,0:T(8,128)(2,1)S(1)}, u32[]{:S(2)}, u32[]{:S(2)}) collective-permute-start(bf16[3,16,32,128]{3,2,1,0:T(8,128)(2,1)S(1)} %collective-permute-done.14.x), channel_id=1, source_target_pairs={{0,8},{2,10},{4,28},{6,30},{8,16},{10,18},{12,4},{14,6},{16,24},{1... | collective-permute-start | bytes 1179656 | tf_op jit(solution)/shard_map/ppermute | solution.py:83
  44.2 13.3 %collective-permute-start.18 = (bf16[3,16,32,128]{3,2,1,0:T(8,128)(2,1)S(1)}, bf16[3,16,32,128]{3,2,1,0:T(8,128)(2,1)S(1)}, u32[]{:S(2)}, u32[]{:S(2)}) collective-permute-start(bf16[3,16,32,128]{3,2,1,0:T(8,128)(2,1)S(1)} %get-tuple-element.47.w), channel_id=1, source_target_pairs={{0,2},{2,0},{4,6},{6,4},{8,10},{10,8},{12,14},{14,12},{16,18},{18,... | collective-permute-start | bytes 1179656 | tf_op jit(solution)/shard_map/ppermute | solution.py:83
  53.2 5.6 %collective-permute-start.20 = (bf16[3,16,32,128]{3,2,1,0:T(8,128)(2,1)S(1)}, bf16[3,16,32,128]{3,2,1,0:T(8,128)(2,1)S(1)}, u32[]{:S(2)}, u32[]{:S(2)}) collective-permute-start(bf16[3,16,32,128]{3,2,1,0:T(8,128)(2,1)S(1)} %collective-permute-done.19.x), channel_id=1, source_target_pairs={{0,2},{2,0},{4,6},{6,4},{8,10},{10,8},{12,14},{14,12},{16,18},{18,... | collective-permute-start | bytes 1179656 | tf_op jit(solution)/shard_map/ppermute | solution.py:83
  53.2 13.4 %collective-permute-start.21 = (bf16[3,16,32,128]{3,2,1,0:T(8,128)(2,1)S(1)}, bf16[3,16,32,128]{3,2,1,0:T(8,128)(2,1)S(1)}, u32[]{:S(2)}, u32[]{:S(2)}) collective-permute-start(bf16[3,16,32,128]{3,2,1,0:T(8,128)(2,1)S(1)} %collective-permute-done.19.x), channel_id=1, source_target_pairs={{0,8},{2,10},{4,28},{6,30},{8,16},{10,18},{12,4},{14,6},{16,24},{1... | collective-permute-start | bytes 1179656 | tf_op jit(solution)/shard_map/ppermute | solution.py:83
  57.5 2.3 %collective-permute-start.17 = (bf16[3,16,32,128]{3,2,1,0:T(8,128)(2,1)S(1)}, bf16[3,16,32,128]{3,2,1,0:T(8,128)(2,1)S(1)}, u32[]{:S(2)}, u32[]{:S(2)}) collective-permute-start(bf16[3,16,32,128]{3,2,1,0:T(8,128)(2,1)S(1)} %collective-permute-done.16.z), channel_id=1, source_target_pairs={{0,2},{2,0},{4,6},{6,4},{8,10},{10,8},{12,14},{14,12},{16,18},{18,... | collective-permute-start | bytes 1179656 | tf_op jit(solution)/shard_map/ppermute | solution.py:83
  66.6 1.7 %collective-permute-start.22 = (bf16[3,16,32,128]{3,2,1,0:T(8,128)(2,1)S(1)}, bf16[3,16,32,128]{3,2,1,0:T(8,128)(2,1)S(1)}, u32[]{:S(2)}, u32[]{:S(2)}) collective-permute-start(bf16[3,16,32,128]{3,2,1,0:T(8,128)(2,1)S(1)} %collective-permute-done.21.z), channel_id=1, source_target_pairs={{0,2},{2,0},{4,6},{6,4},{8,10},{10,8},{12,14},{14,12},{16,18},{18,... | collective-permute-start | bytes 1179656 | tf_op jit(solution)/shard_map/ppermute | solution.py:83
  66.6 7.7 %collective-permute-start.23 = (bf16[3,8,32,128]{3,2,1,0:T(8,128)(2,1)S(1)}, bf16[3,8,32,128]{3,2,1,0:T(8,128)(2,1)S(1)}, u32[]{:S(2)}, u32[]{:S(2)}) collective-permute-start(bf16[3,8,32,128]{3,2,1,0:T(8,128)(2,1)S(1)} %bitcast.19), channel_id=1, source_target_pairs={{0,1},{1,0},{2,3},{3,2},{4,5},{5,4},{6,7},{7,6},{8,9},{9,8},{10,11... | collective-permute-start | bytes 589832 | tf_op jit(solution)/shard_map/ppermute | solution.py:83
  69.8 7.4 %collective-permute-start.25 = (bf16[2,8,32,128]{3,2,1,0:T(8,128)(2,1)S(1)}, bf16[2,8,32,128]{3,2,1,0:T(8,128)(2,1)S(1)}, u32[]{:S(2)}, u32[]{:S(2)}) collective-permute-start(bf16[2,8,32,128]{3,2,1,0:T(8,128)(2,1)S(1)} %bitcast.21), channel_id=1, source_target_pairs={{0,1},{1,0},{2,3},{3,2},{4,5},{5,4},{6,7},{7,6},{8,9},{9,8},{10,11... | collective-permute-start | bytes 393224 | tf_op jit(solution)/shard_map/ppermute | solution.py:83
  72.1 6.5 %collective-permute-start.24 = (bf16[1,8,32,128]{3,2,1,0:T(8,128)(2,1)S(1)}, bf16[1,8,32,128]{3,2,1,0:T(8,128)(2,1)S(1)}, u32[]{:S(2)}, u32[]{:S(2)}) collective-permute-start(bf16[1,8,32,128]{3,2,1,0:T(8,128)(2,1)S(1)} %bitcast.22), channel_id=1, source_target_pairs={{0,1},{1,0},{2,3},{3,2},{4,5},{5,4},{6,7},{7,6},{8,9},{9,8},{10,11... | collective-permute-start | bytes 196616 | tf_op jit(solution)/shard_map/ppermute | solution.py:83
  (2 other events, 3.4 us)
